TPU v7x, 256 devices: a whole 4x4x8 slice. The times are simulated.
256 devices in a mesh: dp: 8 (over z), tensor: 32 (over x, y, core).
Axes of the slice: x: 4, y: 4, z: 8, core: 2. Of those that a mesh axis runs over, the one named last changes fastest.
Arguments:
- hidden: bfloat16 [16384, 2048], P(('dp', 'tensor')), may hold values from -190 to 190
- norm_gain: float32 [2048], replicated, may hold values from 0.1 to 1.9
- head_weight: bfloat16 [2048, 50304], P(None, 'tensor'), may hold values from -0.3 to 0.3
- value_weight: bfloat16 [2048], replicated, may hold values from -0.125 to 0.125
- token_ids: int32 [16384], P(('dp', 'tensor')), may hold values from 0 to 50303
- slot_mask: int32 [16384], P(('dp', 'tensor')), may hold values from 0 to 1, as said below
- lengths: int32 [8, 8], P('dp'), may hold values from 1 to 512, 2048 in all within a row
- request_order: int32 [64], P('dp'), may hold values from 0 to 63, each once
Outputs:
- token_logprob: float32 [16384], P(('dp', 'tensor'))
- token_entropy: float32 [16384], P(('dp', 'tensor'))
- token_value: float32 [16384], P(('dp', 'tensor'))
- request_score: float32 [64], P('dp')
Inputs may be any that keep to these rules, and one draw needn't show every extreme that they name: `slot_mask`: 0 or 1. Among the 64 slots of one device at most 48 are 1 and at least half of 48, rounded down; in every draw some device has exactly 48.
All inputs are finite; a program needn't handle non-finite values.
Results may differ from a plain program's by a relative error of at most 0.0029.
Values may be sent and summed in bfloat16 or wider, within the bound.
A program may use at most 64 MiB of HBM per device.

v0:
```python
import jax
import jax.numpy as jnp
from jax import lax
from jax.sharding import PartitionSpec as P

EPSILON = 1e-06


def merged_2(value, axis, join):
    pieces = jax.tree.map(lambda part: lax.all_gather(part, axis), value)
    head = jax.tree.map(lambda part: part[0], pieces)
    tail = jax.tree.map(lambda part: part[1:], pieces)
    subtotal, _ = lax.scan(lambda subtotal, share: (join(subtotal, share), None), head, tail)
    return subtotal


def combine_parts(lhs_part, rhs_part):
    row_peak = jnp.maximum(lhs_part[0], rhs_part[0])
    left_factor = jnp.exp(lhs_part[0] - row_peak)
    right_factor = jnp.exp(rhs_part[0] - row_peak)
    row_mass = left_factor * lhs_part[1] + right_factor * rhs_part[1]
    row_spread = left_factor * (
        lhs_part[2] + (lhs_part[0] - row_peak) * lhs_part[1]
    ) + right_factor * (rhs_part[2] + (rhs_part[0] - row_peak) * rhs_part[1])
    return (row_peak, row_mass, row_spread, lhs_part[3] + rhs_part[3])


def on_device(
    hidden, norm_gain, head_weight, value_weight, token_ids, slot_mask, lengths, request_order
):
    own_rows = hidden.shape[0]
    vocab_local = head_weight.shape[1]
    tensor_index = lax.axis_index("tensor")
    widened = hidden.astype(jnp.float32)
    inverse_rms = lax.rsqrt(jnp.mean(widened * widened, axis=1, keepdims=True) + EPSILON)
    normed = (widened * inverse_rms * norm_gain).astype(jnp.bfloat16)
    weight_mask = slot_mask.astype(jnp.float32)
    token_value = weight_mask * jnp.dot(normed, value_weight, preferred_element_type=jnp.float32)
    sent_count = normed.shape[0]
    columns = tensor_index * vocab_local + jnp.arange(vocab_local, dtype=jnp.int32)
    piece_rows = lax.all_gather(normed, "tensor", axis=0, tiled=True)
    piece_ids = lax.all_gather(token_ids, "tensor", axis=0, tiled=True)
    logits = jnp.dot(piece_rows, head_weight, preferred_element_type=jnp.float32)
    row_peak = jnp.max(logits, axis=1)
    shifted = logits - row_peak[:, None]
    weights = jnp.exp(shifted)
    row_mass = jnp.sum(weights, axis=1)
    row_spread = jnp.sum(weights * shifted, axis=1)
    row_target = jnp.sum(jnp.where(columns[None, :] == piece_ids[:, None], logits, 0.0), axis=1)
    updates = (row_peak, row_mass, row_spread, row_target)
    row_peak, row_mass, row_spread, row_target = tuple((update for update in updates))
    own_start = tensor_index * sent_count
    merged = merged_2((row_peak, row_mass, row_spread, row_target), "tensor", combine_parts)
    row_peak, row_mass, row_spread, row_target = [
        lax.dynamic_slice_in_dim(member, own_start, sent_count) for member in merged
    ]
    log_mass = jnp.log(row_mass)
    token_logprob = weight_mask * (row_target - row_peak - log_mass)
    token_entropy = weight_mask * (log_mass - row_spread / row_mass)
    request_count = lengths.shape[1]
    span_lengths = lengths[0]
    span_ends = jnp.cumsum(span_lengths)
    slot_ids = tensor_index * own_rows + jnp.arange(own_rows, dtype=jnp.int32)
    position = jnp.sum((slot_ids[:, None] >= span_ends[None, :]).astype(jnp.int32), axis=1)
    onehot = position[:, None] == jnp.arange(request_count, dtype=jnp.int32)[None, :]
    by_pos = jnp.sum(jnp.where(onehot, token_logprob[:, None], 0.0), axis=0) / span_lengths.astype(
        jnp.float32
    )
    all_requests = request_count * lax.axis_size("dp")
    route_table = request_order[:, None] == jnp.arange(all_requests, dtype=jnp.int32)[None, :]
    by_request = jnp.sum(jnp.where(route_table, by_pos[:, None], 0.0), axis=0)
    totals = lax.psum(by_request, ("dp", "tensor"))
    request_score = lax.dynamic_slice_in_dim(
        totals, lax.axis_index("dp") * request_count, request_count
    )
    return (token_logprob, token_entropy, token_value, request_score)


def solution(mesh):
    return jax.shard_map(
        on_device,
        mesh=mesh,
        in_specs=(
            P(("dp", "tensor"), None),
            P(),
            P(None, "tensor"),
            P(),
            P(("dp", "tensor")),
            P(("dp", "tensor")),
            P("dp", None),
            P("dp"),
        ),
        out_specs=(P(("dp", "tensor")), P(("dp", "tensor")), P(("dp", "tensor")), P("dp")),
        check_vma=False,
    )
```

profile of v0, /device:TPU:1, one launch (start us, length us, event | category | flops | bytes accessed | tf_op | source)
XLA Modules:
  0.0 278.3 jit_solution(18414183828398171453)
XLA Ops:
  7.2 0.0 all-gather.6.cloned.1.call-start
  7.2 1.1 fusion.2
  8.3 1.8 fusion.4
  10.1 0.0 all-gather.6.cloned.1.call-update
  10.2 0.8 reduce-window.8
  11.0 0.7 reshape.86
  11.7 1.3 dynamic-slice
  13.6 0.9 dynamic-update-slice
  14.5 14.7 %all-reduce = s32[2048]{0:T(1024)S(1)} all-reduce(s32[2048]{0:T(1024)S(1)} %dynamic-update-slice), channel_id=1, replica_groups=mesh['dp'=8,'tensor'=32] {'tensor'}, use_global_device_ids=true, to_apply=%add | all-reduce | flops 2048 | bytes 16384
  29.2 0.1 convert_reduce_fusion
  29.3 1.6 fusion.1
  30.9 41.9 %all-gather.6.cloned.1.call-done = bf16[2048,2048]{1,0:T(8,128)(2,1)} async-done(((bf16[64,2048]{1,0:T(8,128)(2,1)}), bf16[2048,2048]{1,0:T(8,128)(2,1)}) %all-gather.6.cloned.1.call-update) | async-done | bytes 8388624 | tf_op jit(solution)/shard_map/all_gather | solution.py:41
  72.9 18.4 %fusion.5 = (f32[2048]{0:T(1024)S(1)}, f32[2048,1572]{0,1:T(8,128)S(1)}) fusion(bf16[2048,2048]{1,0:T(8,128)(2,1)} %all-gather.6.cloned.1.call-done, bf16[2048,1572]{0,1:T(8,128)(2,1)} %param.12), kind=kOutput, calls=%fused_computation.28 | convolution fusion | flops 13190109184 | bytes 27713536 | tf_op jit(solution)/shard_map/dot_general | solution.py:43
  91.3 0.0 copy-start
  91.3 0.0 copy-start.2
  91.3 0.0 copy-start.3
  91.3 4.7 %fusion = (f32[2048]{0:T(1024)S(1)}, f32[2048]{0:T(1024)S(1)}, f32[2048]{0:T(1024)S(1)}) fusion(f32[2048,1572]{0,1:T(8,128)S(1)} %get-tuple-element.88, f32[2048]{0:T(1024)S(1)} %get-tuple-element.87, s32[2048]{0:T(1024)S(1)} %all-reduce, s32[1572]{0:T(1024)S(1)} %iota_add_fusion), kind=kLoop, calls=%fused_computation.8 | loop fusion | flops 22530048 | bytes 12925072 | tf_op jit(solution)/shard_map/reduce_sum | solution.py:48
  96.1 24.5 %all-gather.2 = f32[65536]{0:T(1024)S(1)} all-gather(f32[2048]{0:T(1024)S(1)} %get-tuple-element.58), channel_id=4, replica_groups=mesh['dp'=8,'tensor'=32] {'tensor'}, dimensions={0}, use_global_device_ids=true | all-gather | bytes 270336 | tf_op jit(solution)/shard_map/all_gather | solution.py:10
  120.6 22.6 %all-gather = f32[65536]{0:T(1024)S(1)} all-gather(f32[2048]{0:T(1024)S(1)} %get-tuple-element.87), channel_id=2, replica_groups=mesh['dp'=8,'tensor'=32] {'tensor'}, dimensions={0}, use_global_device_ids=true | all-gather | bytes 270336 | tf_op jit(solution)/shard_map/all_gather | solution.py:10
  143.2 24.1 %all-gather.1 = f32[65536]{0:T(1024)S(1)} all-gather(f32[2048]{0:T(1024)S(1)} %get-tuple-element.59), channel_id=3, replica_groups=mesh['dp'=8,'tensor'=32] {'tensor'}, dimensions={0}, use_global_device_ids=true | all-gather | bytes 270336 | tf_op jit(solution)/shard_map/all_gather | solution.py:10
  167.3 22.8 %all-gather.3 = f32[65536]{0:T(1024)S(1)} all-gather(f32[2048]{0:T(1024)S(1)} %get-tuple-element.60), channel_id=5, replica_groups=mesh['dp'=8,'tensor'=32] {'tensor'}, dimensions={0}, use_global_device_ids=true | all-gather | bytes 270336 | tf_op jit(solution)/shard_map/all_gather | solution.py:10
  190.3 4.3 %while.16 = (s32[]{:T(128)}, f32[2048]{0:T(1024)S(1)}, f32[2048]{0:T(1024)S(1)}, f32[2048]{0:T(1024)S(1)}, f32[2048]{0:T(1024)S(1)}, /*index=5*/f32[31,2048]{1,0...) while((s32[]{:T(128)}, f32[2048]{0:T(1024)S(1)}, ...), condition=%wide.region_6.7_spmd, body=%wide.region_5.6_spmd.sunk | while | flops 32770 | bytes 221301 | solution.py:13
  194.6 0.0 copy-done
  194.6 0.6 subtract_multiply_fusion
  195.2 0.0 copy-start.1
  195.2 0.1 select_reduce_fusion.2
  195.3 0.0 copy-done.2
  195.3 0.0 copy-done.3
  195.3 0.1 select_reduce_fusion.1
  195.4 75.4 %psum.7 = f32[64]{0:T(128)S(1)} all-reduce(f32[64]{0:T(128)S(1)} %select_reduce_fusion.1), channel_id=1, replica_groups=mesh['dp'=8,'tensor'=32] {'dp','tensor'}, use_global_device_ids=true, to_apply=%region_11.12 | all-reduce | flops 64 | bytes 512 | tf_op jit(solution)/shard_map/psum | solution.py:72
  270.9 0.6 dynamic_slice.32
  271.5 0.0 copy-done.1
  (203 shorter events, 2.7 us)
Async XLA Ops:
  7.2 65.7 %all-gather.6.cloned.1.call-start = ((), (), s32[]{:S(2)}) async-start(), calls=%async_computation | async-start | bytes 8650752 | tf_op jit(solution)/shard_map/all_gather | solution.py:41
  91.3 103.3 %copy-start = (s32[64]{0:T(128)S(1)}, s32[64]{0:T(128)}, u32[]{:S(2)}) copy-start(s32[64]{0:T(128)} %param.15) | copy-start | bytes 772
  91.3 104.0 %copy-start.2 = (s32[1,8]{1,0:T(1,128)S(1)}, s32[1,8]{1,0:T(1,128)}, u32[]{:S(2)}) copy-start(s32[1,8]{1,0:T(1,128)} %param.16) | copy-start | bytes 100
  91.3 104.0 %copy-start.3 = (s32[8]{0:T(128)S(1)}, s32[8]{0:T(128)}, u32[]{:S(2)}) copy-start(s32[8]{0:T(128)} %param.17) | copy-start | bytes 100
  195.2 76.3 %copy-start.1 = (f32[64]{0:T(128)}, f32[64]{0:T(128)S(1)}, u32[]{:S(2)}) copy-start(f32[64]{0:T(128)S(1)} %get-tuple-element.86) | copy-start | bytes 772
Sparse Core Ops, SparseCore 0:
  10.6 62.2 all-gather.5
where the time goes:
time: 279 us; the launch traced here: 278 us
  blocking collectives  184 us (66%)
  waiting for transfers between devices  42 us (15%)
  matrix products  20.1 us (7%)
  between operations  14.9 us (5%)
  other arithmetic  10.4 us (4%)
  local copies, waits for them, and re-layouts  5.11 us (2%)
    all_gather x4, blocking collectives, merged_2(): pieces = jax.tree.map(lambda part: lax.all_gather(part, axis), value)  93.9 us
    psum x1, blocking collectives, on_device(): totals = lax.psum(by_request, ('dp', 'tensor'))  75.4 us
    all_gather x1, waiting for transfers between devices, on_device(): piece_rows = lax.all_gather(normed, 'tensor', axis=0, tiled=True)  41.9 us
    dot_general x1, matrix products, on_device(): jnp.dot(piece_rows, head_weight, preferred_element_type=jnp.float32)  18.4 us
    unnamed x1, blocking collectives  14.7 us
  transfers between devices with their start and end apart: 1, of which 1 were waited for; matrix products, arithmetic and copies ran while one was open for 2% of the time, Pallas kernels for 0%

commit v1 on v0

v1 whole, which is shorter than its diff:
```python
import jax
import jax.numpy as jnp
from jax import lax
from jax.sharding import PartitionSpec as P

EPSILON = 1e-06


def on_device(
    hidden, norm_gain, head_weight, value_weight, token_ids, slot_mask, lengths, request_order
):
    own_rows = hidden.shape[0]
    vocab_local = head_weight.shape[1]
    tensor_index = lax.axis_index("tensor")
    widened = hidden.astype(jnp.float32)
    inverse_rms = lax.rsqrt(jnp.mean(widened * widened, axis=1, keepdims=True) + EPSILON)
    normed = (widened * inverse_rms * norm_gain).astype(jnp.bfloat16)
    weight_mask = slot_mask.astype(jnp.float32)
    token_value = weight_mask * jnp.dot(normed, value_weight, preferred_element_type=jnp.float32)

    columns = tensor_index * vocab_local + jnp.arange(vocab_local, dtype=jnp.int32)
    piece_rows = lax.all_gather(normed, "tensor", axis=0, tiled=True)
    piece_meta = lax.all_gather(jnp.stack([token_ids, slot_mask]), "tensor", axis=1, tiled=True)
    piece_ids = piece_meta[0]
    piece_mask = piece_meta[1].astype(jnp.float32)

    logits = jnp.dot(piece_rows, head_weight, preferred_element_type=jnp.float32)
    row_peak = jnp.max(logits, axis=1)
    shifted = logits - row_peak[:, None]
    weights = jnp.exp(shifted)
    row_mass = jnp.sum(weights, axis=1)
    row_spread = jnp.sum(weights * shifted, axis=1)
    row_target = jnp.sum(jnp.where(columns[None, :] == piece_ids[:, None], logits, 0.0), axis=1)

    stats = jnp.stack([row_peak, row_mass, row_spread, row_target])
    parts = lax.all_gather(stats, "tensor", axis=0)
    part_peak, part_mass, part_spread, part_target = parts[:, 0], parts[:, 1], parts[:, 2], parts[:, 3]
    peak = jnp.max(part_peak, axis=0)
    gap = part_peak - peak[None, :]
    factor = jnp.exp(gap)
    mass = jnp.sum(factor * part_mass, axis=0)
    spread = jnp.sum(factor * (part_spread + gap * part_mass), axis=0)
    target = jnp.sum(part_target, axis=0)
    log_mass = jnp.log(mass)
    group_logprob = piece_mask * (target - peak - log_mass)
    group_entropy = log_mass - spread / mass

    own_start = tensor_index * own_rows
    token_logprob = lax.dynamic_slice_in_dim(group_logprob, own_start, own_rows)
    token_entropy = weight_mask * lax.dynamic_slice_in_dim(group_entropy, own_start, own_rows)

    request_count = lengths.shape[1]
    span_lengths = lengths[0]
    span_ends = jnp.cumsum(span_lengths)
    slot_ids = jnp.arange(group_logprob.shape[0], dtype=jnp.int32)
    position = jnp.sum((slot_ids[:, None] >= span_ends[None, :]).astype(jnp.int32), axis=1)
    onehot = position[:, None] == jnp.arange(request_count, dtype=jnp.int32)[None, :]
    by_pos = jnp.sum(jnp.where(onehot, group_logprob[:, None], 0.0), axis=0) / span_lengths.astype(
        jnp.float32
    )
    routed = lax.all_gather(
        jnp.concatenate([by_pos, request_order.astype(jnp.float32)]), "dp", axis=0
    )
    all_totals = routed[:, :request_count].reshape(-1)
    all_owners = routed[:, request_count:].reshape(-1)
    wanted = (lax.axis_index("dp") * request_count + jnp.arange(request_count)).astype(jnp.float32)
    route_table = all_owners[:, None] == wanted[None, :]
    request_score = jnp.sum(jnp.where(route_table, all_totals[:, None], 0.0), axis=0)
    return (token_logprob, token_entropy, token_value, request_score)


def solution(mesh):
    return jax.shard_map(
        on_device,
        mesh=mesh,
        in_specs=(
            P(("dp", "tensor"), None),
            P(),
            P(None, "tensor"),
            P(),
            P(("dp", "tensor")),
            P(("dp", "tensor")),
            P("dp", None),
            P("dp"),
        ),
        out_specs=(P(("dp", "tensor")), P(("dp", "tensor")), P(("dp", "tensor")), P("dp")),
        check_vma=False,
    )
```

time: 279 us -> 174 us (0.62)
  blocking collectives: 184 us -> 39.6 us
  waiting for transfers between devices: 42 us -> 81.3 us
  other arithmetic: 10.4 us -> 14.8 us
  local copies, waits for them, and re-layouts: 5.11 us -> 1.62 us
    psum x1 -> x0, blocking collectives: 75.4 us -> none  [on_device(): totals = lax.psum(by_request, ('dp', 'tensor'))]
    all_gather x4 -> x1, blocking collectives: 93.9 us -> 25.8 us  [on_device(): lax.all_gather(jnp.stack([token_ids, slot_mask]), 'tensor', axis=1, tiled...]
    all_gather x0 -> x1, waiting for transfers between devices: none -> 45.3 us  [on_device(): parts = lax.all_gather(stats, 'tensor', axis=0)]
    all_gather x1, waiting for transfers between devices: 41.9 us -> 35.9 us  [on_device(): piece_rows = lax.all_gather(normed, 'tensor', axis=0, tiled=True)]
    slice x0 -> x2, other arithmetic: none -> 3.65 us  [the longest x1 3.63 us: on_device(): parts[:, 0]]
    reduce_sum x3 -> x4, other arithmetic: 4.94 us -> 5.86 us  [the longest x1 4.73 us: on_device(): row_mass = jnp.sum(weights, axis=1)]
  transfers between devices with their start and end apart: 1 -> 2, of which waited for: 1 -> 2; matrix products, arithmetic and copies ran while one was open for 2% -> 1% of each run, Pallas kernels for 0% -> 0%
where the time goes in v1:
time: 174 us; the launch traced here: 171 us
  waiting for transfers between devices  81.3 us (47%)
  blocking collectives  39.6 us (23%)
  matrix products  19.1 us (11%)
  between operations  14.9 us (9%)
  other arithmetic  14.8 us (9%)
    all_gather x1, waiting for transfers between devices, on_device(): parts = lax.all_gather(stats, 'tensor', axis=0)  45.3 us
    all_gather x1, waiting for transfers between devices, on_device(): piece_rows = lax.all_gather(normed, 'tensor', axis=0, tiled=True)  35.9 us
    all_gather x1, blocking collectives, on_device(): lax.all_gather(jnp.stack([token_ids, slot_mask]), 'tensor', axis=1, tiled...  25.8 us
    dot_general x1, matrix products, on_device(): jnp.dot(piece_rows, head_weight, preferred_element_type=jnp.float32)  18.4 us
    unnamed x1, blocking collectives  13.8 us
    reduce_sum x1, other arithmetic, on_device(): row_mass = jnp.sum(weights, axis=1)  4.73 us
    slice x1, other arithmetic, on_device(): parts[:, 0]  3.63 us
  transfers between devices with their start and end apart: 2, of which 2 were waited for; matrix products, arithmetic and copies ran while one was open for 1% of the time, Pallas kernels for 0%

profile of v1, /device:TPU:1, one launch (start us, length us, event | category | flops | bytes accessed | tf_op | source)
XLA Modules:
  0.0 171.4 jit_solution(14239749646011860981)
XLA Ops:
  7.2 0.0 all-gather.7.cloned.1.call-start
  7.2 1.1 fusion.2
  8.3 1.8 %fusion.4 = bf16[64,2048]{1,0:T(8,128)(2,1)} fusion(bf16[64,2048]{1,0:T(8,128)(2,1)} %param.8, f32[2048]{0:T(1024)} %param.9, f32[64]{0:T(128)S(1)} %add_rsqrt_fusion), kind=kLoop, calls=%fused_computation.10 | loop fusion | flops 524288 | bytes 532736 | tf_op jit(solution)/shard_map/convert_element_type | solution.py:17
  10.1 0.0 all-gather.7.cloned.1.call-update
  10.2 0.0 all-gather.9.cloned.1.call-start
  10.2 0.7 add_bitcast_fusion
  10.9 25.8 %all-gather.2 = s32[32,64,2]{1,2,0:T(2,128)S(1)} all-gather(s32[1,64,2]{1,2,0:T(2,128)S(1)} %add_bitcast_fusion), channel_id=1, replica_groups=mesh['dp'=8,'tensor'=32] {'tensor'}, dimensions={0}, use_global_device_ids=true | all-gather | bytes 16896 | tf_op jit(solution)/shard_map/all_gather | solution.py:23
  36.6 0.1 reshape.81
  36.8 35.9 %all-gather.7.cloned.1.call-done = bf16[2048,2048]{1,0:T(8,128)(2,1)} async-done(((bf16[64,2048]{1,0:T(8,128)(2,1)}), bf16[2048,2048]{1,0:T(8,128)(2,1)}) %all-gather.7.cloned.1.call-update) | async-done | bytes 8388624 | tf_op jit(solution)/shard_map/all_gather | solution.py:22
  72.7 18.4 %fusion.15 = (f32[2048]{0:T(1024)S(1)}, f32[2048,1572]{0,1:T(8,128)S(1)}) fusion(bf16[2048,2048]{1,0:T(8,128)(2,1)} %all-gather.7.cloned.1.call-done, bf16[2048,1572]{0,1:T(8,128)(2,1)} %param.10), kind=kOutput, calls=%fused_computation.43 | convolution fusion | flops 13190109184 | bytes 27713536 | tf_op jit(solution)/shard_map/dot_general | solution.py:27
  91.1 0.0 copy-start.3
  91.1 0.0 copy-start.5
  91.2 4.7 %exponential_reduce_fusion = (f32[2048]{0:T(1024)S(1)}, f32[2048]{0:T(1024)S(1)}, f32[2048]{0:T(1024)S(1)}) fusion(f32[2048,1572]{0,1:T(8,128)S(1)} %get-tuple-element.23, f32[2048]{0:T(1024)S(1)} %get-tuple-element.22, s32[2048]{0:T(1024)S(1)} %bitcast.54, s32[1572]{0:T(1024)S(1)} %iota_add_fusion), kind=kLoop, calls=%fused_computation.1 | loop fusion | flops 22530048 | bytes 12925072 | tf_op jit(solution)/shard_map/reduce_sum | solution.py:31
  95.9 0.6 maximum_bitcast_fusion
  96.5 0.0 all-gather.9.cloned.1.call-update
  96.6 0.2 reduce-window.8
  96.8 0.6 dynamic-slice
  98.1 0.1 convert_reduce_fusion
  98.2 0.7 fusion.1
  98.9 45.3 %all-gather.9.cloned.1.call-done = f32[32,4,2048]{2,1,0:T(4,128)} async-done(((f32[1,4,2048]{2,1,0:T(4,128)}), f32[32,4,2048]{2,1,0:T(4,128)}) %all-gather.9.cloned.1.call-update) | async-done | bytes 1048592 | tf_op jit(solution)/shard_map/all_gather | solution.py:36
  144.2 3.6 %fusion.11 = (f32[32,1,2048]{2,1,0:T(1,128)S(1)}, f32[32,1,2048]{2,1,0:T(1,128)S(1)}, f32[2048]{0:T(1024)S(1)}, f32[2048]{0:T(1024)S(1)}, f32[32,1,2048]{2,1,0:T(1,128)S(1)}) fusion(f32[32,4,2048]{2,1,0:T(4,128)} %all-gather.9.cloned.1.call-done), kind=kLoop, calls=%fused_computation.39 | loop fusion | flops 126976 | bytes 1851392 | tf_op jit(solution)/shard_map/slice | solution.py:37
  147.8 0.3 fusion.7
  148.2 0.1 select_reduce_fusion.1
  148.3 0.6 dynamic_slice.6
  148.9 0.2 maximum_dynamic-update-slice_fusion
  149.1 13.8 %all-reduce = f32[128]{0:T(128)S(1)} all-reduce(f32[128]{0:T(128)S(1)} %maximum_dynamic-update-slice_fusion), channel_id=3, replica_groups=mesh['dp'=8,'tensor'=32] {'dp'}, use_global_device_ids=true, to_apply=%add | all-reduce | flops 128 | bytes 1024
  162.9 0.1 reshape.76
  163.0 0.1 fusion.14
  163.1 0.1 eq.50
  163.1 0.1 broadcast_in_dim.44
  163.2 0.6 fusion.10
  163.8 0.7 select_reduce_fusion.2
  (20 shorter events, 0.1 us)
Async XLA Ops:
  7.2 65.6 %all-gather.7.cloned.1.call-start = ((), (), s32[]{:S(2)}) async-start(), calls=%async_computation | async-start | bytes 8650752 | tf_op jit(solution)/shard_map/all_gather | solution.py:22
  10.2 134.0 %all-gather.9.cloned.1.call-start = ((), (), s32[]{:S(2)}) async-start(), calls=%async_computation.1 | async-start | bytes 1081344 | tf_op jit(solution)/shard_map/all_gather | solution.py:36
  91.1 5.5 %copy-start.3 = (s32[8]{0:T(128)S(1)}, s32[8]{0:T(128)}, u32[]{:S(2)}) copy-start(s32[8]{0:T(128)} %param.15) | copy-start | bytes 100
  91.1 5.5 %copy-start.4 = (s32[1,8]{1,0:T(1,128)S(1)}, s32[1,8]{1,0:T(1,128)}, u32[]{:S(2)}) copy-start(s32[1,8]{1,0:T(1,128)} %param.14) | copy-start | bytes 100
  91.1 5.7 %copy-start.1 = (bf16[2048]{0:T(1024)(128)(2,1)S(1)}, bf16[2048]{0:T(1024)(128)(2,1)}, u32[]{:S(2)}) copy-start(bf16[2048]{0:T(1024)(128)(2,1)} %param.11) | copy-start | bytes 12292
  91.1 5.7 %copy-start.5 = (u32[256]{0:T(256)S(1)}, u32[256]{0:T(256)}, u32[]{:S(2)}) copy-start(u32[256]{0:T(256)} %constant.38) | copy-start | bytes 3076
  91.2 7.0 %copy-start = (bf16[64,2048]{1,0:T(8,128)(2,1)S(1)}, bf16[64,2048]{1,0:T(8,128)(2,1)}, u32[]{:S(2)}) copy-start(bf16[64,2048]{1,0:T(8,128)(2,1)} %fusion.4) | copy-start | bytes 786436
  91.2 7.0 %copy-start.2 = (s32[64]{0:T(128)S(1)}, s32[64]{0:T(128)}, u32[]{:S(2)}) copy-start(s32[64]{0:T(128)} %param.13) | copy-start | bytes 772
Sparse Core Ops, SparseCore 0:
  10.6 62.1 all-gather.6
  96.7 47.4 all-gather.8

commit v2 on v1

v2 whole, which is shorter than its diff:
```python
import jax
import jax.numpy as jnp
from jax import lax
from jax.experimental import pallas as pl
from jax.experimental.pallas import tpu as pltpu
from jax.sharding import PartitionSpec as P

EPSILON = 1e-06
MESH = pl.DeviceIdType.MESH


def exchange_kernel(n_tensor, send_ref, out_ref, held, send_sem, recv_sem):
    me = lax.axis_index("tensor")
    dp = lax.axis_index("dp")
    barrier = pltpu.get_barrier_semaphore()
    for offset in range(1, n_tensor):
        peer = lax.rem(me + offset, n_tensor)
        pl.semaphore_signal(barrier, inc=1, device_id=(dp, peer), device_id_type=MESH)
    pl.semaphore_wait(barrier, n_tensor - 1)
    held[me] = send_ref[me]
    copies = []
    for offset in range(1, n_tensor):
        peer = lax.rem(me + offset, n_tensor)
        copy = pltpu.make_async_remote_copy(
            src_ref=send_ref.at[peer],
            dst_ref=held.at[me],
            send_sem=send_sem.at[offset],
            recv_sem=recv_sem.at[offset],
            device_id=(dp, peer),
            device_id_type=MESH,
        )
        copy.start()
        copies.append(copy)
    for copy in copies:
        copy.wait_send()
    for offset in range(1, n_tensor):
        source = lax.rem(me + n_tensor - offset, n_tensor)
        pltpu.make_async_remote_copy(
            src_ref=send_ref.at[source],
            dst_ref=held.at[source],
            send_sem=send_sem.at[offset],
            recv_sem=recv_sem.at[offset],
            device_id=(dp, source),
            device_id_type=MESH,
        ).wait_recv()
    out_ref[...] = held[...]


def exchange(blocks, n_tensor):
    return pl.pallas_call(
        lambda *refs: exchange_kernel(n_tensor, *refs),
        out_shape=jax.ShapeDtypeStruct(blocks.shape, blocks.dtype),
        in_specs=[pl.BlockSpec(memory_space=pltpu.VMEM)],
        out_specs=pl.BlockSpec(memory_space=pltpu.VMEM),
        scratch_shapes=[
            pltpu.VMEM(blocks.shape, blocks.dtype),
            pltpu.SemaphoreType.DMA((n_tensor,)),
            pltpu.SemaphoreType.DMA((n_tensor,)),
        ],
        compiler_params=pltpu.CompilerParams(collective_id=0, has_side_effects=True),
    )(blocks)


def route_kernel(n_tensor, n_dp, part_ref, ids_ref, out_ref, t_held, d_held, msg,
                 t_send, t_recv, d_send, d_recv):
    me = lax.axis_index("tensor")
    dp = lax.axis_index("dp")
    barrier = pltpu.get_barrier_semaphore()
    for offset in range(1, n_tensor):
        peer = lax.rem(me + offset, n_tensor)
        pl.semaphore_signal(barrier, inc=1, device_id=(dp, peer), device_id_type=MESH)
    for offset in range(1, n_dp):
        peer = lax.rem(dp + offset, n_dp)
        pl.semaphore_signal(barrier, inc=1, device_id=(peer, me), device_id_type=MESH)
    pl.semaphore_wait(barrier, n_tensor - 1 + n_dp - 1)
    t_held[me] = part_ref[...]
    copies = []
    for offset in range(1, n_tensor):
        peer = lax.rem(me + offset, n_tensor)
        copy = pltpu.make_async_remote_copy(
            src_ref=part_ref,
            dst_ref=t_held.at[me],
            send_sem=t_send.at[offset],
            recv_sem=t_recv.at[offset],
            device_id=(dp, peer),
            device_id_type=MESH,
        )
        copy.start()
        copies.append(copy)
    for copy in copies:
        copy.wait_send()
    for offset in range(1, n_tensor):
        source = lax.rem(me + n_tensor - offset, n_tensor)
        pltpu.make_async_remote_copy(
            src_ref=part_ref,
            dst_ref=t_held.at[source],
            send_sem=t_send.at[offset],
            recv_sem=t_recv.at[offset],
            device_id=(dp, source),
            device_id_type=MESH,
        ).wait_recv()
    total = jnp.sum(t_held[...], axis=0)
    row = lax.broadcasted_iota(jnp.int32, total.shape, 0)
    msg[...] = jnp.where(row == 0, total, jnp.where(row == 1, ids_ref[...], 0.0))
    d_held[dp] = msg[...]
    copies = []
    for offset in range(1, n_dp):
        peer = lax.rem(dp + offset, n_dp)
        copy = pltpu.make_async_remote_copy(
            src_ref=msg,
            dst_ref=d_held.at[dp],
            send_sem=d_send.at[offset],
            recv_sem=d_recv.at[offset],
            device_id=(peer, me),
            device_id_type=MESH,
        )
        copy.start()
        copies.append(copy)
    for copy in copies:
        copy.wait_send()
    for offset in range(1, n_dp):
        source = lax.rem(dp + n_dp - offset, n_dp)
        pltpu.make_async_remote_copy(
            src_ref=msg,
            dst_ref=d_held.at[source],
            send_sem=d_send.at[offset],
            recv_sem=d_recv.at[offset],
            device_id=(source, me),
            device_id_type=MESH,
        ).wait_recv()
    out_ref[...] = d_held[...]


def route(part, ids, n_tensor, n_dp):
    tile = part.shape
    return pl.pallas_call(
        lambda *refs: route_kernel(n_tensor, n_dp, *refs),
        out_shape=jax.ShapeDtypeStruct((n_dp,) + tile, jnp.float32),
        in_specs=[pl.BlockSpec(memory_space=pltpu.VMEM)] * 2,
        out_specs=pl.BlockSpec(memory_space=pltpu.VMEM),
        scratch_shapes=[
            pltpu.VMEM((n_tensor,) + tile, jnp.float32),
            pltpu.VMEM((n_dp,) + tile, jnp.float32),
            pltpu.VMEM(tile, jnp.float32),
            pltpu.SemaphoreType.DMA((n_tensor,)),
            pltpu.SemaphoreType.DMA((n_tensor,)),
            pltpu.SemaphoreType.DMA((n_dp,)),
            pltpu.SemaphoreType.DMA((n_dp,)),
        ],
        compiler_params=pltpu.CompilerParams(collective_id=1, has_side_effects=True),
    )(part, ids)


def on_device(
    hidden, norm_gain, head_weight, value_weight, token_ids, slot_mask, lengths, request_order
):
    own_rows = hidden.shape[0]
    vocab_local = head_weight.shape[1]
    n_tensor = lax.axis_size("tensor")
    n_dp = lax.axis_size("dp")
    tensor_index = lax.axis_index("tensor")
    widened = hidden.astype(jnp.float32)
    inverse_rms = lax.rsqrt(jnp.mean(widened * widened, axis=1, keepdims=True) + EPSILON)
    normed = (widened * inverse_rms * norm_gain).astype(jnp.bfloat16)
    weight_mask = slot_mask.astype(jnp.float32)
    token_value = weight_mask * jnp.dot(normed, value_weight, preferred_element_type=jnp.float32)

    columns = tensor_index * vocab_local + jnp.arange(vocab_local, dtype=jnp.int32)
    piece_rows = lax.all_gather(normed, "tensor", axis=0, tiled=True)
    piece_ids = lax.all_gather(token_ids, "tensor", axis=0, tiled=True)

    logits = jnp.dot(piece_rows, head_weight, preferred_element_type=jnp.float32)
    row_peak = jnp.max(logits, axis=1)
    shifted = logits - row_peak[:, None]
    weights = jnp.exp(shifted)
    row_mass = jnp.sum(weights, axis=1)
    row_spread = jnp.sum(weights * shifted, axis=1)
    row_target = jnp.sum(jnp.where(columns[None, :] == piece_ids[:, None], logits, 0.0), axis=1)

    stats = jnp.stack([row_peak, row_mass, row_spread, row_target])
    blocks = stats.reshape(4, n_tensor, own_rows).transpose(1, 0, 2)
    parts = exchange(blocks, n_tensor)
    part_peak, part_mass, part_spread, part_target = parts[:, 0], parts[:, 1], parts[:, 2], parts[:, 3]
    peak = jnp.max(part_peak, axis=0)
    gap = part_peak - peak[None, :]
    factor = jnp.exp(gap)
    mass = jnp.sum(factor * part_mass, axis=0)
    spread = jnp.sum(factor * (part_spread + gap * part_mass), axis=0)
    target = jnp.sum(part_target, axis=0)
    log_mass = jnp.log(mass)
    token_logprob = weight_mask * (target - peak - log_mass)
    token_entropy = weight_mask * (log_mass - spread / mass)

    request_count = lengths.shape[1]
    span_lengths = lengths[0]
    span_ends = jnp.cumsum(span_lengths)
    slot_ids = tensor_index * own_rows + jnp.arange(own_rows, dtype=jnp.int32)
    position = jnp.sum((slot_ids[:, None] >= span_ends[None, :]).astype(jnp.int32), axis=1)
    onehot = position[:, None] == jnp.arange(request_count, dtype=jnp.int32)[None, :]
    by_pos = jnp.sum(jnp.where(onehot, token_logprob[:, None], 0.0), axis=0) / span_lengths.astype(
        jnp.float32
    )
    tile = jnp.zeros((8, 128), jnp.float32)
    part_tile = tile.at[0, :request_count].set(by_pos)
    ids_tile = tile.at[1, :request_count].set(request_order.astype(jnp.float32))
    routed = route(part_tile, ids_tile, n_tensor, n_dp)
    all_totals = routed[:, 0, :request_count].reshape(-1)
    all_owners = routed[:, 1, :request_count].reshape(-1)
    wanted = (lax.axis_index("dp") * request_count + jnp.arange(request_count)).astype(jnp.float32)
    route_table = all_owners[:, None] == wanted[None, :]
    request_score = jnp.sum(jnp.where(route_table, all_totals[:, None], 0.0), axis=0)
    return (token_logprob, token_entropy, token_value, request_score)


def solution(mesh):
    return jax.shard_map(
        on_device,
        mesh=mesh,
        in_specs=(
            P(("dp", "tensor"), None),
            P(),
            P(None, "tensor"),
            P(),
            P(("dp", "tensor")),
            P(("dp", "tensor")),
            P("dp", None),
            P("dp"),
        ),
        out_specs=(P(("dp", "tensor")), P(("dp", "tensor")), P(("dp", "tensor")), P("dp")),
        check_vma=False,
    )
```

time: 174 us -> 139 us (0.80); the launches traced: 171 us -> 139 us
  waiting for transfers between devices: 81.3 us -> 40.7 us
  Pallas kernels: 0 us -> 27 us
  blocking collectives: 39.6 us -> 14.7 us
  local copies, waits for them, and re-layouts: 1.62 us -> 5.34 us
  matrix products: 19.1 us -> 21.2 us
    all_gather x1 -> x0, waiting for transfers between devices: 45.3 us -> none  [on_device(): parts = lax.all_gather(stats, 'tensor', axis=0)]
    pallas_call x0 -> x2, Pallas kernels: none -> 27 us  [the longest x1 16.7 us: route(): pl.pallas_call(lambda *refs: route_kernel(n_tensor, n_dp, *refs), out_sha...]
    all_gather x1 -> x0, blocking collectives: 25.8 us -> none  [on_device(): lax.all_gather(jnp.stack([token_ids, slot_mask]), 'tensor', axis=1, tiled...]
    all_gather x1, waiting for transfers between devices: 35.9 us -> 40.7 us  [on_device(): piece_rows = lax.all_gather(normed, 'tensor', axis=0, tiled=True)]
    reduce_sum x1, other arithmetic: 4.73 us -> 7.38 us  [on_device(): row_mass = jnp.sum(weights, axis=1)]
    slice x2 -> x1, other arithmetic: 3.65 us -> 1.07 us  [on_device(): parts[:, 1]]
    unnamed x16 -> x10, local copies, waits for them, and re-layouts: 0.72 us -> 2.8 us
  transfers between devices with their start and end apart: 2 -> 1, of which waited for: 2 -> 1; matrix products, arithmetic and copies ran while one was open for 1% -> 5% of each run, Pallas kernels for 0% -> 0%
where the time goes in v2:
time: 139 us
  waiting for transfers between devices  40.7 us (29%)
  Pallas kernels  27 us (19%)
  matrix products  21.2 us (15%)
  other arithmetic  15 us (11%)
  between operations  14.8 us (11%)
  blocking collectives  14.7 us (11%)
  local copies, waits for them, and re-layouts  5.34 us (4%)
    all_gather x1, waiting for transfers between devices, on_device(): piece_rows = lax.all_gather(normed, 'tensor', axis=0, tiled=True)  40.7 us
    dot_general x1, matrix products, on_device(): jnp.dot(piece_rows, head_weight, preferred_element_type=jnp.float32)  19.5 us
    pallas_call x1, Pallas kernels, route(): pl.pallas_call(lambda *refs: route_kernel(n_tensor, n_dp, *refs), out_sha...  16.7 us
    unnamed x1, blocking collectives  14.7 us
    pallas_call x1, Pallas kernels, exchange(): pl.pallas_call(lambda *refs: exchange_kernel(n_tensor, *refs), out_shape=...  10.3 us
    reduce_sum x1, other arithmetic, on_device(): row_mass = jnp.sum(weights, axis=1)  7.38 us
    unnamed x10, local copies, waits for them, and re-layouts  2.8 us
  transfers between devices with their start and end apart: 1, of which 1 were waited for; matrix products, arithmetic and copies ran while one was open for 5% of the time, Pallas kernels for 0%

profile of v2, /device:TPU:1, one launch (start us, length us, event | category | flops | bytes accessed | tf_op | source)
XLA Modules:
  0.0 138.8 jit_solution(14190944455807926833)
XLA Ops:
  7.2 0.0 all-gather.2.cloned.1.call-start
  7.2 1.1 fusion.2
  8.3 1.8 %fusion.4 = bf16[64,2048]{1,0:T(8,128)(2,1)} fusion(bf16[64,2048]{1,0:T(8,128)(2,1)} %param.12, f32[2048]{0:T(1024)} %param.13, f32[64]{0:T(128)S(1)} %add_rsqrt_fusion), kind=kLoop, calls=%fused_computation.10 | loop fusion | flops 524288 | bytes 532736 | tf_op jit(solution)/shard_map/convert_element_type | solution.py:164
  10.1 0.0 all-gather.2.cloned.1.call-update
  10.1 0.7 reshape.137
  10.8 1.3 dynamic-slice.15
  12.8 0.8 reduce-window.8
  13.6 0.7 convert_bitcast_fusion
  14.2 0.6 scatter.9.refs_1_
  14.9 0.8 dynamic-update-slice.4
  15.7 14.7 %all-reduce.2 = s32[2048]{0:T(1024)S(1)} all-reduce(s32[2048]{0:T(1024)S(1)} %dynamic-update-slice.4), channel_id=1, replica_groups=mesh['dp'=8,'tensor'=32] {'tensor'}, use_global_device_ids=true, to_apply=%add.2 | all-reduce | flops 2048 | bytes 16384
  30.4 0.1 convert_reduce_fusion
  30.5 1.6 %fusion.1 = f32[64]{0:T(128)} fusion(bf16[64,2048]{1,0:T(8,128)(2,1)} %fusion.4, bf16[2048,1]{0,1:T(2,128)(2,1)S(1)} %reshape.137, s32[64]{0:T(128)} %param.17), kind=kOutput, calls=%fused_computation.5 | convolution fusion | flops 262272 | bytes 266752 | tf_op jit(solution)/shard_map/dot_general | solution.py:166
  32.2 40.7 %all-gather.2.cloned.1.call-done = bf16[2048,2048]{1,0:T(8,128)(2,1)} async-done(((bf16[64,2048]{1,0:T(8,128)(2,1)}), bf16[2048,2048]{1,0:T(8,128)(2,1)}) %all-gather.2.cloned.1.call-update) | async-done | bytes 8388624 | tf_op jit(solution)/shard_map/all_gather | solution.py:169
  72.8 19.5 %fusion.6 = (f32[2048]{0:T(1024)S(1)}, f32[2048,1572]{0,1:T(8,128)}) fusion(bf16[2048,2048]{1,0:T(8,128)(2,1)} %all-gather.2.cloned.1.call-done, bf16[2048,1572]{0,1:T(8,128)(2,1)} %param.14), kind=kOutput, calls=%fused_computation.30 | convolution fusion | flops 13190109184 | bytes 27713536 | tf_op jit(solution)/shard_map/dot_general | solution.py:172
  92.4 0.1 stack.15
  92.5 7.4 %exponential_reduce_fusion = (f32[2048]{0:T(1024)S(1)}, f32[2048]{0:T(1024)S(1)}, f32[2048]{0:T(1024)S(1)}) fusion(f32[2048,1572]{0,1:T(8,128)} %get-tuple-element.42, f32[2048]{0:T(1024)S(1)} %get-tuple-element.41, s32[2048]{0:T(1024)S(1)} %all-reduce.2, s32[1572]{0:T(1024)S(1)} %iota_add_fusion), kind=kLoop, calls=%fused_computation.1 | loop fusion | flops 22530048 | bytes 12925072 | tf_op jit(solution)/shard_map/reduce_sum | solution.py:176
  99.8 0.1 stack.16
  99.9 0.1 stack.17
  100.0 0.1 stack.18
  100.1 0.7 maximum_bitcast_fusion.refs_0_
  100.8 10.3 %shard_map.111 = f32[32,4,64]{2,1,0:T(4,128)} custom-call(f32[32,4,64]{2,1,0:T(4,128)} %maximum_bitcast_fusion.refs_0_), custom_call_target="tpu_custom_call" | custom-call | tf_op jit(solution)/shard_map/pallas_call | solution.py:50
  111.1 1.1 fusion.5
  112.2 0.0 copy-done
  112.2 0.5 subtract_multiply_fusion
  112.8 0.1 select_reduce_fusion.2
  112.9 0.6 scatter.6.refs_0_
  113.5 16.7 %shard_map.112 = f32[8,8,128]{2,1,0:T(8,128)} custom-call(f32[8,128]{1,0:T(8,128)} %scatter.6.refs_0_, f32[8,128]{1,0:T(8,128)} %scatter.9.refs_1_), custom_call_target="tpu_custom_call" | custom-call | tf_op jit(solution)/shard_map/pallas_call | solution.py:136
  130.2 0.9 slice_reduce_fusion.2
  131.1 0.1 eq.47
  131.2 0.1 broadcast_in_dim.40
  131.2 0.7 select_reduce_fusion.1
  (13 shorter events, 0.1 us)
Async XLA Ops:
  7.2 65.7 %all-gather.2.cloned.1.call-start = ((), (), s32[]{:S(2)}) async-start(), calls=%async_computation | async-start | bytes 8650752 | tf_op jit(solution)/shard_map/all_gather | solution.py:169
  92.4 19.9 %copy-start = (s32[64]{0:T(128)S(1)}, s32[64]{0:T(128)}, u32[]{:S(2)}) copy-start(s32[64]{0:T(128)} %param.17) | copy-start | bytes 772
  92.4 20.5 %copy-start.2 = (s32[1,8]{1,0:T(1,128)S(1)}, s32[1,8]{1,0:T(1,128)}, u32[]{:S(2)}) copy-start(s32[1,8]{1,0:T(1,128)} %param.18) | copy-start | bytes 100
  112.8 19.2 %copy-start.1 = (f32[64]{0:T(128)}, f32[64]{0:T(128)S(1)}, u32[]{:S(2)}) copy-start(f32[64]{0:T(128)S(1)} %get-tuple-element.40) | copy-start | bytes 772
Sparse Core Ops, SparseCore 0:
  10.6 62.2 all-gather.1

commit v3 on v2

--- a/solution.py
+++ b/solution.py
@@ -7,6 +7,7 @@
 
 EPSILON = 1e-06
 MESH = pl.DeviceIdType.MESH
+LIVE = 48
 
 
 def exchange_kernel(n_tensor, send_ref, out_ref, held, send_sem, recv_sem):
@@ -166,8 +167,28 @@
     token_value = weight_mask * jnp.dot(normed, value_weight, preferred_element_type=jnp.float32)
 
     columns = tensor_index * vocab_local + jnp.arange(vocab_local, dtype=jnp.int32)
-    piece_rows = lax.all_gather(normed, "tensor", axis=0, tiled=True)
-    piece_ids = lax.all_gather(token_ids, "tensor", axis=0, tiled=True)
+    width = hidden.shape[1]
+    live_sum = jnp.cumsum(slot_mask)
+    slot_index = jnp.arange(own_rows, dtype=jnp.int32)
+    chosen = (slot_mask[None, :] == 1) & (
+        live_sum[None, :] - 1 == jnp.arange(LIVE, dtype=jnp.int32)[:, None]
+    )
+    source = jnp.sum(jnp.where(chosen, slot_index[None, :], 0), axis=1)
+    compact_rows = jnp.take(normed, source, axis=0)
+    compact_ids = jnp.take(token_ids, source)
+    meta = (
+        jnp.zeros((1, width), jnp.bfloat16)
+        .at[0, :LIVE].set((compact_ids // 256).astype(jnp.bfloat16))
+        .at[0, 128:128 + LIVE].set((compact_ids % 256).astype(jnp.bfloat16))
+    )
+    block = jnp.concatenate([compact_rows, meta], axis=0)
+    piece_rows = lax.all_gather(block, "tensor", axis=0, tiled=True)
+    block_rows = LIVE + 1
+    meta_rows = piece_rows.reshape(n_tensor, block_rows, width)[:, LIVE, :].astype(jnp.float32)
+    gathered_ids = (meta_rows[:, :LIVE] * 256.0 + meta_rows[:, 128:128 + LIVE]).astype(jnp.int32)
+    piece_ids = jnp.concatenate(
+        [gathered_ids, jnp.full((n_tensor, 1), -1, jnp.int32)], axis=1
+    ).reshape(-1)
 
     logits = jnp.dot(piece_rows, head_weight, preferred_element_type=jnp.float32)
     row_peak = jnp.max(logits, axis=1)
@@ -178,7 +199,7 @@
     row_target = jnp.sum(jnp.where(columns[None, :] == piece_ids[:, None], logits, 0.0), axis=1)
 
     stats = jnp.stack([row_peak, row_mass, row_spread, row_target])
-    blocks = stats.reshape(4, n_tensor, own_rows).transpose(1, 0, 2)
+    blocks = stats.reshape(4, n_tensor, block_rows)[:, :, :LIVE].transpose(1, 0, 2)
     parts = exchange(blocks, n_tensor)
     part_peak, part_mass, part_spread, part_target = parts[:, 0], parts[:, 1], parts[:, 2], parts[:, 3]
     peak = jnp.max(part_peak, axis=0)
@@ -188,8 +209,9 @@
     spread = jnp.sum(factor * (part_spread + gap * part_mass), axis=0)
     target = jnp.sum(part_target, axis=0)
     log_mass = jnp.log(mass)
-    token_logprob = weight_mask * (target - peak - log_mass)
-    token_entropy = weight_mask * (log_mass - spread / mass)
+    place = jnp.clip(live_sum - 1, 0, LIVE - 1)
+    token_logprob = weight_mask * jnp.take(target - peak - log_mass, place)
+    token_entropy = weight_mask * jnp.take(log_mass - spread / mass, place)
 
     request_count = lengths.shape[1]
     span_lengths = lengths[0]

time: 139 us -> 156 us (1.12)
  waiting for transfers between devices: 40.7 us -> 56 us
  blocking collectives: 14.7 us -> 0 us
  local copies, waits for them, and re-layouts: 5.34 us -> 15.6 us
  other arithmetic: 15 us -> 21.4 us
    all_gather x1, waiting for transfers between devices: 40.7 us -> 56 us  [on_device(): piece_rows = lax.all_gather(block, 'tensor', axis=0, tiled=True)]
    unnamed x1 -> x0, blocking collectives: 14.7 us -> none
    unnamed x10 -> x11, local copies, waits for them, and re-layouts: 2.8 us -> 7.7 us
    another operation x2 -> x8, other arithmetic: 1.49 us -> 4.9 us
    gather x0 -> x4, local copies, waits for them, and re-layouts: none -> 3.03 us  [the longest x1 0.78 us: on_device(): token_logprob = weight_mask * jnp.take(target - peak - log_mass, place)]
  transfers between devices with their start and end apart: 1 -> 1, of which waited for: 1 -> 1; matrix products, arithmetic and copies ran while one was open for 5% -> 3% of each run, Pallas kernels for 0% -> 0%
where the time goes in v3:
time: 156 us
  waiting for transfers between devices  56 us (36%)
  Pallas kernels  26.7 us (17%)
  matrix products  21.9 us (14%)
  other arithmetic  21.4 us (14%)
  local copies, waits for them, and re-layouts  15.6 us (10%)
  between operations  14.2 us (9%)
    all_gather x1, waiting for transfers between devices, on_device(): piece_rows = lax.all_gather(block, 'tensor', axis=0, tiled=True)  56 us
    dot_general x1, matrix products, on_device(): jnp.dot(piece_rows, head_weight, preferred_element_type=jnp.float32)  20.6 us
    pallas_call x1, Pallas kernels, route(): pl.pallas_call(lambda *refs: route_kernel(n_tensor, n_dp, *refs), out_sha...  16.7 us
    pallas_call x1, Pallas kernels, exchange(): pl.pallas_call(lambda *refs: exchange_kernel(n_tensor, *refs), out_shape=...  9.95 us
    reduce_sum x1, other arithmetic, on_device(): row_mass = jnp.sum(weights, axis=1)  7.89 us
    unnamed x11, local copies, waits for them, and re-layouts  7.7 us
    another operation x8, other arithmetic  4.9 us
  transfers between devices with their start and end apart: 1, of which 1 were waited for; matrix products, arithmetic and copies ran while one was open for 3% of the time, Pallas kernels for 0%

profile of v3, /device:TPU:1, one launch (start us, length us, event | category | flops | bytes accessed | tf_op | source)
XLA Modules:
  0.0 155.8 jit_solution(18125534710458942303)
XLA Ops:
  7.2 0.6 compare_reduce_fusion
  7.9 0.6 and_reduce_fusion
  8.5 0.7 broadcast_compare_fusion
  9.2 0.7 copy.21
  10.3 1.1 fusion.2
  11.4 0.6 slice.100
  12.0 0.8 gather_fusion.1
  12.8 1.1 fusion.4
  13.9 0.7 gather_fusion
  14.6 0.7 broadcast_select_fusion.2
  15.2 1.4 broadcast_select_fusion.1
  16.6 0.8 scatter.15
  17.5 0.7 maximum_bitcast_fusion
  18.2 0.8 reduce-window.16
  19.1 0.7 reshape.354
  19.8 0.7 convert_bitcast_fusion
  20.4 0.6 scatter.19.refs_1_
  21.2 1.4 fusion.1
  22.5 56.0 %all-gather.3.cloned.1.call-done = bf16[32,49,2048]{2,1,0:T(8,128)(2,1)} async-done(((bf16[1,49,2048]{2,1,0:T(8,128)(2,1)}), bf16[32,49,2048]{2,1,0:T(8,128)(2,1)}) %all-gather.3.cloned.1.call-update) | async-done | bytes 6422544 | tf_op jit(solution)/shard_map/all_gather | solution.py:185
  78.5 1.4 slice_convert_fusion
  80.1 6.9 %reshape.348 = bf16[1568,2048]{1,0:T(8,128)(2,1)} reshape(bf16[32,49,2048]{2,1,0:T(8,128)(2,1)} %all-gather.3.cloned.1.call-done) | data formatting | bytes 12845056
  87.0 20.6 %fusion.11 = (f32[1568]{0:T(1024)S(1)}, f32[1568,1572]{1,0:T(8,128)}) fusion(bf16[1568,2048]{1,0:T(8,128)(2,1)} %reshape.348, bf16[2048,1572]{0,1:T(8,128)(2,1)} %param.20), kind=kOutput, calls=%fused_computation.73 | convolution fusion | flops 10098677760 | bytes 22727296 | tf_op jit(solution)/shard_map/dot_general | solution.py:193
  107.7 7.9 %exponential_reduce_fusion = (f32[1568]{0:T(1024)S(1)}, f32[1568]{0:T(1024)S(1)}, f32[1568]{0:T(1024)S(1)}) fusion(f32[1568,1572]{1,0:T(8,128)} %get-tuple-element.69, f32[1568]{0:T(1024)S(1)} %get-tuple-element.68, s32[1568]{0:T(1024)S(1)} %eq.67, s32[1572]{0:T(1024)S(1)} %iota_add_fusion), kind=kLoop, calls=%fused_computation.5 | loop fusion | flops 17249568 | bytes 9897232 | tf_op jit(solution)/shard_map/reduce_sum | solution.py:197
  115.9 0.7 fusion.5.refs_0_
  116.6 9.9 %shard_map.111 = f32[32,4,48]{2,1,0:T(4,128)} custom-call(f32[32,4,48]{2,1,0:T(4,128)} %fusion.5.refs_0_), custom_call_target="tpu_custom_call" | custom-call | tf_op jit(solution)/shard_map/pallas_call | solution.py:51
  126.6 1.1 fusion.10
  127.7 0.8 gather_fusion.3
  128.5 0.8 gather_fusion.2
  130.0 0.6 scatter.16.refs_0_
  130.5 16.7 %shard_map.112 = f32[8,8,128]{2,1,0:T(8,128)} custom-call(f32[8,128]{1,0:T(8,128)} %scatter.16.refs_0_, f32[8,128]{1,0:T(8,128)} %scatter.19.refs_1_), custom_call_target="tpu_custom_call" | custom-call | tf_op jit(solution)/shard_map/pallas_call | solution.py:137
  147.3 0.9 slice_reduce_fusion.2
  148.3 0.7 select_reduce_fusion.2
  (42 shorter events, 2.1 us)
Async XLA Ops:
  7.2 4.8 %copy-start = (s32[64]{0:T(128)S(1)}, s32[64]{0:T(128)}, u32[]{:S(2)}) copy-start(s32[64]{0:T(128)} %param.22) | copy-start | bytes 772
  7.2 71.3 %all-gather.3.cloned.1.call-start = ((), (), s32[]{:S(2)}) async-start(), calls=%async_computation | async-start | bytes 7569408 | tf_op jit(solution)/shard_map/all_gather | solution.py:185
  107.6 21.7 %copy-start.1 = (s32[64]{0:T(128)S(1)}, s32[64]{0:T(128)}, u32[]{:S(2)}) copy-start(s32[64]{0:T(128)} %param.23) | copy-start | bytes 772
  107.6 22.4 %copy-start.3 = (s32[1,8]{1,0:T(1,128)S(1)}, s32[1,8]{1,0:T(1,128)}, u32[]{:S(2)}) copy-start(s32[1,8]{1,0:T(1,128)} %param.24) | copy-start | bytes 100
  129.8 19.2 %copy-start.2 = (f32[64]{0:T(128)}, f32[64]{0:T(128)S(1)}, u32[]{:S(2)}) copy-start(f32[64]{0:T(128)S(1)} %get-tuple-element.65) | copy-start | bytes 772
Sparse Core Ops, SparseCore 0:
  18.4 60.1 all-gather.2

commit v4 on v3

--- a/solution.py
+++ b/solution.py
@@ -177,18 +177,15 @@
     compact_rows = jnp.take(normed, source, axis=0)
     compact_ids = jnp.take(token_ids, source)
     meta = (
-        jnp.zeros((1, width), jnp.bfloat16)
-        .at[0, :LIVE].set((compact_ids // 256).astype(jnp.bfloat16))
-        .at[0, 128:128 + LIVE].set((compact_ids % 256).astype(jnp.bfloat16))
-    )
-    block = jnp.concatenate([compact_rows, meta], axis=0)
-    piece_rows = lax.all_gather(block, "tensor", axis=0, tiled=True)
-    block_rows = LIVE + 1
-    meta_rows = piece_rows.reshape(n_tensor, block_rows, width)[:, LIVE, :].astype(jnp.float32)
-    gathered_ids = (meta_rows[:, :LIVE] * 256.0 + meta_rows[:, 128:128 + LIVE]).astype(jnp.int32)
-    piece_ids = jnp.concatenate(
-        [gathered_ids, jnp.full((n_tensor, 1), -1, jnp.int32)], axis=1
-    ).reshape(-1)
+        jnp.zeros((LIVE, 128), jnp.bfloat16)
+        .at[:, 0].set((compact_ids // 256).astype(jnp.bfloat16))
+        .at[:, 1].set((compact_ids % 256).astype(jnp.bfloat16))
+    )
+    block = jnp.concatenate([compact_rows, meta], axis=1)
+    gathered = lax.all_gather(block, "tensor", axis=0, tiled=True)
+    piece_rows = gathered[:, :width]
+    meta_cols = gathered[:, width:width + 2].astype(jnp.float32)
+    piece_ids = (meta_cols[:, 0] * 256.0 + meta_cols[:, 1]).astype(jnp.int32)
 
     logits = jnp.dot(piece_rows, head_weight, preferred_element_type=jnp.float32)
     row_peak = jnp.max(logits, axis=1)
@@ -199,7 +196,7 @@
     row_target = jnp.sum(jnp.where(columns[None, :] == piece_ids[:, None], logits, 0.0), axis=1)
 
     stats = jnp.stack([row_peak, row_mass, row_spread, row_target])
-    blocks = stats.reshape(4, n_tensor, block_rows)[:, :, :LIVE].transpose(1, 0, 2)
+    blocks = stats.reshape(4, n_tensor, LIVE).transpose(1, 0, 2)
     parts = exchange(blocks, n_tensor)
     part_peak, part_mass, part_spread, part_target = parts[:, 0], parts[:, 1], parts[:, 2], parts[:, 3]
     peak = jnp.max(part_peak, axis=0)

time: 156 us -> 140 us (0.90)
  local copies, waits for them, and re-layouts: 15.6 us -> 7.38 us
  matrix products: 21.9 us -> 17.4 us
  other arithmetic: 21.4 us -> 19.1 us
    unnamed x11 -> x9, local copies, waits for them, and re-layouts: 7.7 us -> 0.71 us
    dot_general x1, matrix products: 20.6 us -> 16.1 us  [on_device(): jnp.dot(piece_rows, head_weight, preferred_element_type=jnp.float32)]
    reduce_sum x1, other arithmetic: 7.89 us -> 6.11 us  [on_device(): row_mass = jnp.sum(weights, axis=1)]
    another operation x8 -> x6, other arithmetic: 4.9 us -> 4.19 us
where the time goes in v4:
time: 140 us; the launch traced here: 139 us
  waiting for transfers between devices  54.9 us (39%)
  Pallas kernels  26.4 us (19%)
  other arithmetic  19.1 us (14%)
  matrix products  17.4 us (12%)
  between operations  14.2 us (10%)
  local copies, waits for them, and re-layouts  7.38 us (5%)
    all_gather x1, waiting for transfers between devices, on_device(): gathered = lax.all_gather(block, 'tensor', axis=0, tiled=True)  54.9 us
    pallas_call x1, Pallas kernels, route(): pl.pallas_call(lambda *refs: route_kernel(n_tensor, n_dp, *refs), out_sha...  16.7 us
    dot_general x1, matrix products, on_device(): jnp.dot(piece_rows, head_weight, preferred_element_type=jnp.float32)  16.1 us
    pallas_call x1, Pallas kernels, exchange(): pl.pallas_call(lambda *refs: exchange_kernel(n_tensor, *refs), out_shape=...  9.63 us
    reduce_sum x1, other arithmetic, on_device(): row_mass = jnp.sum(weights, axis=1)  6.11 us
    another operation x6, other arithmetic  4.19 us
  transfers between devices with their start and end apart: 1, of which 1 were waited for; matrix products, arithmetic and copies ran while one was open for 3% of the time, Pallas kernels for 0%

profile of v4, /device:TPU:1, one launch (start us, length us, event | category | flops | bytes accessed | tf_op | source)
XLA Modules:
  0.0 139.4 jit_solution(16617935079007166762)
XLA Ops:
  7.2 0.6 compare_reduce_fusion.1
  7.9 0.6 compare_reduce_fusion
  8.5 1.1 fusion.6
  9.6 0.7 broadcast_compare_fusion
  10.3 0.7 copy.26
  11.2 0.1 select_reduce_fusion.1
  11.6 0.8 gather_fusion.1
  12.5 1.1 fusion.8
  13.6 0.7 gather_fusion
  14.3 1.3 fusion.15
  15.7 0.1 scatter.15
  15.9 0.7 pad_maximum_fusion
  16.6 0.8 reduce-window.16
  17.4 0.7 reshape.331
  18.1 0.7 convert_bitcast_fusion
  18.8 0.6 scatter.19.refs_1_
  19.5 1.4 fusion.3
  20.8 54.9 %all-gather.2.cloned.1.call-done = bf16[1536,2176]{1,0:T(8,128)(2,1)} async-done(((bf16[48,2176]{1,0:T(8,128)(2,1)}), bf16[1536,2176]{1,0:T(8,128)(2,1)}) %all-gather.2.cloned.1.call-update) | async-done | bytes 6684688 | tf_op jit(solution)/shard_map/all_gather | solution.py:185
  75.7 1.0 slice_convert_fusion
  76.8 0.5 fusion.5
  77.3 16.1 %fusion.18 = (f32[1536]{0:T(1024)S(1)}, f32[1536,1572]{0,1:T(8,128)}) fusion(bf16[2048,1572]{0,1:T(8,128)(2,1)} %param.20, bf16[1536,2176]{1,0:T(8,128)(2,1)} %all-gather.2.cloned.1.call-done), kind=kOutput, calls=%fused_computation.74 | convolution fusion | flops 9892581376 | bytes 22411264 | tf_op jit(solution)/shard_map/dot_general | solution.py:190
  93.4 6.1 %exponential_reduce_fusion = (f32[1536]{0:T(1024)S(1)}, f32[1536]{0:T(1024)S(1)}, f32[1536]{0:T(1024)S(1)}) fusion(f32[1536,1572]{0,1:T(8,128)} %get-tuple-element.71, f32[1536]{0:T(1024)S(1)} %get-tuple-element.70, s32[1536]{0:T(1024)S(1)} %fusion.5, s32[1572]{0:T(1024)S(1)} %iota_add_fusion), kind=kLoop, calls=%fused_computation.5 | loop fusion | flops 16897536 | bytes 9695376 | tf_op jit(solution)/shard_map/reduce_sum | solution.py:194
  99.8 0.7 maximum_bitcast_fusion.refs_0_
  100.5 9.6 %shard_map.111 = f32[32,4,48]{2,1,0:T(4,128)} custom-call(f32[32,4,48]{2,1,0:T(4,128)} %maximum_bitcast_fusion.refs_0_), custom_call_target="tpu_custom_call" | custom-call | tf_op jit(solution)/shard_map/pallas_call | solution.py:51
  110.2 1.1 fusion.17
  111.3 0.8 gather_fusion.3
  112.1 0.8 gather_fusion.2
  112.9 0.5 select_multiply_fusion
  113.5 0.6 scatter.16.refs_0_
  114.1 16.7 %shard_map.112 = f32[8,8,128]{2,1,0:T(8,128)} custom-call(f32[8,128]{1,0:T(8,128)} %scatter.16.refs_0_, f32[8,128]{1,0:T(8,128)} %scatter.19.refs_1_), custom_call_target="tpu_custom_call" | custom-call | tf_op jit(solution)/shard_map/pallas_call | solution.py:137
  130.9 0.9 slice_reduce_fusion.2
  131.9 0.7 select_reduce_fusion.2
  (37 shorter events, 1.5 us)
Async XLA Ops:
  7.2 4.4 %copy-start = (s32[64]{0:T(128)S(1)}, s32[64]{0:T(128)}, u32[]{:S(2)}) copy-start(s32[64]{0:T(128)} %param.22) | copy-start | bytes 772
  7.2 68.6 %all-gather.2.cloned.1.call-start = ((), (), s32[]{:S(2)}) async-start(), calls=%async_computation | async-start | bytes 6893568 | tf_op jit(solution)/shard_map/all_gather | solution.py:185
  93.3 19.5 %copy-start.1 = (s32[64]{0:T(128)S(1)}, s32[64]{0:T(128)}, u32[]{:S(2)}) copy-start(s32[64]{0:T(128)} %param.23) | copy-start | bytes 772
  93.3 20.2 %copy-start.3 = (s32[1,8]{1,0:T(1,128)S(1)}, s32[1,8]{1,0:T(1,128)}, u32[]{:S(2)}) copy-start(s32[1,8]{1,0:T(1,128)} %param.24) | copy-start | bytes 100
  113.4 19.2 %copy-start.2 = (f32[64]{0:T(128)}, f32[64]{0:T(128)S(1)}, u32[]{:S(2)}) copy-start(f32[64]{0:T(128)S(1)} %get-tuple-element.67) | copy-start | bytes 772
Sparse Core Ops, SparseCore 0:
  16.7 58.9 all-gather.1

commit v5 on v4

--- a/solution.py
+++ b/solution.py
@@ -152,6 +152,43 @@
     )(part, ids)
 
 
+def stats_kernel(x_ref, w_ref, id_ref, out_ref):
+    logits = jnp.dot(x_ref[...], w_ref[...], preferred_element_type=jnp.float32)
+    peak = jnp.max(logits, axis=1, keepdims=True)
+    shifted = logits - peak
+    weights = jnp.exp(shifted)
+    mass = jnp.sum(weights, axis=1, keepdims=True)
+    spread = jnp.sum(weights * shifted, axis=1, keepdims=True)
+    column = lax.broadcasted_iota(jnp.int32, logits.shape, 1)
+    target = jnp.sum(jnp.where(column == id_ref[...], logits, 0.0), axis=1, keepdims=True)
+    lane = lax.broadcasted_iota(jnp.int32, out_ref.shape, 1)
+    out_ref[...] = jnp.where(
+        lane == 0, peak, jnp.where(lane == 1, mass, jnp.where(lane == 2, spread, target))
+    )
+
+
+def row_stats(rows, weight, local_ids, width, tile):
+    count = rows.shape[0]
+    depth, vocab = weight.shape
+    return pl.pallas_call(
+        stats_kernel,
+        out_shape=jax.ShapeDtypeStruct((count, 128), jnp.float32),
+        grid=(count // tile,),
+        in_specs=[
+            pl.BlockSpec((tile, width), lambda i: (i, 0)),
+            pl.BlockSpec((depth, vocab), lambda i: (0, 0)),
+            pl.BlockSpec((tile, 1), lambda i: (i, 0)),
+        ],
+        out_specs=pl.BlockSpec((tile, 128), lambda i: (i, 0)),
+        compiler_params=pltpu.CompilerParams(vmem_limit_bytes=56 * 1024 * 1024),
+        cost_estimate=pl.CostEstimate(
+            flops=2 * count * depth * vocab,
+            transcendentals=count * vocab,
+            bytes_accessed=2 * count * width + 2 * depth * vocab + 512 * count,
+        ),
+    )(rows, weight, local_ids)
+
+
 def on_device(
     hidden, norm_gain, head_weight, value_weight, token_ids, slot_mask, lengths, request_order
 ):
@@ -166,7 +203,6 @@
     weight_mask = slot_mask.astype(jnp.float32)
     token_value = weight_mask * jnp.dot(normed, value_weight, preferred_element_type=jnp.float32)
 
-    columns = tensor_index * vocab_local + jnp.arange(vocab_local, dtype=jnp.int32)
     width = hidden.shape[1]
     live_sum = jnp.cumsum(slot_mask)
     slot_index = jnp.arange(own_rows, dtype=jnp.int32)
@@ -183,20 +219,12 @@
     )
     block = jnp.concatenate([compact_rows, meta], axis=1)
     gathered = lax.all_gather(block, "tensor", axis=0, tiled=True)
-    piece_rows = gathered[:, :width]
     meta_cols = gathered[:, width:width + 2].astype(jnp.float32)
     piece_ids = (meta_cols[:, 0] * 256.0 + meta_cols[:, 1]).astype(jnp.int32)
-
-    logits = jnp.dot(piece_rows, head_weight, preferred_element_type=jnp.float32)
-    row_peak = jnp.max(logits, axis=1)
-    shifted = logits - row_peak[:, None]
-    weights = jnp.exp(shifted)
-    row_mass = jnp.sum(weights, axis=1)
-    row_spread = jnp.sum(weights * shifted, axis=1)
-    row_target = jnp.sum(jnp.where(columns[None, :] == piece_ids[:, None], logits, 0.0), axis=1)
-
-    stats = jnp.stack([row_peak, row_mass, row_spread, row_target])
-    blocks = stats.reshape(4, n_tensor, LIVE).transpose(1, 0, 2)
+    local_ids = (piece_ids - tensor_index * vocab_local)[:, None]
+    row_count = gathered.shape[0]
+    stats = row_stats(gathered, head_weight, local_ids, width, 256 if row_count % 256 == 0 else row_count)
+    blocks = stats[:, :4].reshape(n_tensor, LIVE, 4).transpose(0, 2, 1)
     parts = exchange(blocks, n_tensor)
     part_peak, part_mass, part_spread, part_target = parts[:, 0], parts[:, 1], parts[:, 2], parts[:, 3]
     peak = jnp.max(part_peak, axis=0)

time: 140 us -> 139 us (level)
  Pallas kernels: 26.4 us -> 45.7 us
  matrix products: 17.4 us -> 0.7 us
  local copies, waits for them, and re-layouts: 7.38 us -> 18.7 us
  waiting for transfers between devices: 54.9 us -> 46.6 us
  other arithmetic: 19.1 us -> 12.4 us
    pallas_call x0 -> x1, Pallas kernels: none -> 19.3 us  [row_stats(): pl.pallas_call(stats_kernel, out_shape=jax.ShapeDtypeStruct((count, 128),...]
    dot_general x1 -> x0, matrix products: 16.1 us -> none  [on_device(): jnp.dot(piece_rows, head_weight, preferred_element_type=jnp.float32)]
    unnamed x9 -> x12, local copies, waits for them, and re-layouts: 0.71 us -> 10.3 us
    all_gather x1, waiting for transfers between devices: 54.9 us -> 46.6 us  [on_device(): gathered = lax.all_gather(block, 'tensor', axis=0, tiled=True)]
    reduce_sum x1 -> x0, other arithmetic: 6.11 us -> none  [on_device(): row_mass = jnp.sum(weights, axis=1)]
    reshape x0 -> x1, local copies, waits for them, and re-layouts: none -> 2.05 us  [on_device(): blocks = stats[:, :4].reshape(n_tensor, LIVE, 4).transpose(0, 2, 1)]
  transfers between devices with their start and end apart: 1 -> 1, of which waited for: 1 -> 1; matrix products, arithmetic and copies ran while one was open for 3% -> 9% of each run, Pallas kernels for 0% -> 0%
where the time goes in v5:
time: 139 us; the launch traced here: 138 us
  waiting for transfers between devices  46.6 us (34%)
  Pallas kernels  45.7 us (33%)
  local copies, waits for them, and re-layouts  18.7 us (13%)
  between operations  14.2 us (10%)
  other arithmetic  12.4 us (9%)
    all_gather x1, waiting for transfers between devices, on_device(): gathered = lax.all_gather(block, 'tensor', axis=0, tiled=True)  46.6 us
    pallas_call x1, Pallas kernels, row_stats(): pl.pallas_call(stats_kernel, out_shape=jax.ShapeDtypeStruct((count, 128),...  19.3 us
    pallas_call x1, Pallas kernels, route(): pl.pallas_call(lambda *refs: route_kernel(n_tensor, n_dp, *refs), out_sha...  16.7 us
    unnamed x12, local copies, waits for them, and re-layouts  10.3 us
    pallas_call x1, Pallas kernels, exchange(): pl.pallas_call(lambda *refs: exchange_kernel(n_tensor, *refs), out_shape=...  9.63 us
    another operation x6, other arithmetic  3.54 us
  transfers between devices with their start and end apart: 1, of which 1 were waited for; matrix products, arithmetic and copies ran while one was open for 9% of the time, Pallas kernels for 0%

profile of v5, /device:TPU:1, one launch (start us, length us, event | category | flops | bytes accessed | tf_op | source)
XLA Modules:
  0.0 138.3 jit_solution(5282340209819471246)
XLA Ops:
  7.2 0.6 compare_reduce_fusion.1
  7.9 0.6 compare_reduce_fusion
  8.5 1.1 fusion.3
  9.6 0.7 broadcast_compare_fusion
  10.3 0.7 copy.40
  11.2 0.1 select_reduce_fusion
  11.6 0.8 gather_fusion.1
  12.5 1.1 fusion.5
  13.6 0.7 gather_fusion
  14.3 1.3 fusion.12
  15.7 0.1 scatter.15
  15.9 0.7 pad_maximum_fusion
  16.6 0.8 reduce-window.16
  17.5 0.7 reshape.321
  18.2 9.6 %copy.46.w_ref = bf16[2048,1572]{1,0:T(8,128)(2,1)} copy(bf16[2048,1572]{0,1:T(8,128)(2,1)} %param.20) | data formatting | bytes 12877824 | tf_op args[2]
  27.7 0.6 scatter.19.refs_1_
  28.5 0.7 fusion
  29.2 46.6 %all-gather.2.cloned.1.call-done.x_ref = bf16[1536,2176]{1,0:T(8,128)(2,1)} async-done(((bf16[48,2176]{1,0:T(8,128)(2,1)}), bf16[1536,2176]{1,0:T(8,128)(2,1)}) %all-gather.2.cloned.1.call-update) | async-done | bytes 6684688 | tf_op jit(solution)/shard_map/all_gather | solution.py:221
  75.8 1.0 slice_convert_fusion
  76.8 1.2 fusion.2.id_ref
  78.0 19.3 %shard_map.111 = f32[1536,128]{1,0:T(8,128)} custom-call(bf16[1536,2176]{1,0:T(8,128)(2,1)} %all-gather.2.cloned.1.call-done.x_ref, bf16[2048,1572]{1,0:T(8,128)(2,1)} %copy.46.w_ref, s32[1536,1]{1,0:T(8,128)} %fusion.2.id_ref), custom_call_target="tpu_custom_call" | custom-call | flops 9890168832 | bytes 13516800 | tf_op jit(solution)/shard_map/pallas_call | solution.py:173
  97.3 2.1 %copy.48 = f32[32,48,4]{1,2,0:T(4,128)} copy(f32[32,48,4]{2,1,0:T(8,128)} %bitcast.25) | data formatting | bytes 49152 | tf_op jit(solution)/shard_map/reshape | solution.py:227
  99.4 9.6 %shard_map.112 = f32[32,4,48]{2,1,0:T(4,128)} custom-call(f32[32,4,48]{2,1,0:T(4,128)} %bitcast.26), custom_call_target="tpu_custom_call" | custom-call | tf_op jit(solution)/shard_map/pallas_call | solution.py:51
  109.0 1.1 fusion.14
  110.2 0.8 gather_fusion.3
  111.0 0.8 gather_fusion.2
  111.7 0.5 select_multiply_fusion
  112.3 0.1 select_reduce_fusion.2
  112.4 0.6 scatter.16.refs_0_
  113.0 16.7 %shard_map.113 = f32[8,8,128]{2,1,0:T(8,128)} custom-call(f32[8,128]{1,0:T(8,128)} %scatter.16.refs_0_, f32[8,128]{1,0:T(8,128)} %scatter.19.refs_1_), custom_call_target="tpu_custom_call" | custom-call | tf_op jit(solution)/shard_map/pallas_call | solution.py:137
  129.7 0.9 slice_reduce_fusion.2
  130.7 0.7 select_reduce_fusion.1
  (34 shorter events, 1.0 us)
Async XLA Ops:
  7.2 4.4 %copy-start = (s32[64]{0:T(128)S(1)}, s32[64]{0:T(128)}, u32[]{:S(2)}) copy-start(s32[64]{0:T(128)} %param.22) | copy-start | bytes 772
  7.2 68.6 %all-gather.2.cloned.1.call-start = ((), (), s32[]{:S(2)}) async-start(), calls=%async_computation | async-start | bytes 6893568 | tf_op jit(solution)/shard_map/all_gather | solution.py:221
  16.6 11.1 %copy-start.3 = (s32[8]{0:T(128)S(1)}, s32[8]{0:T(128)}, u32[]{:S(2)}) copy-start(s32[8]{0:T(128)} %param.25) | copy-start | bytes 100
  16.6 11.8 %copy-start.1 = (s32[64]{0:T(128)S(1)}, s32[64]{0:T(128)}, u32[]{:S(2)}) copy-start(s32[64]{0:T(128)} %param.23) | copy-start | bytes 772
  78.0 34.4 %copy-start.4 = (s32[1,8]{1,0:T(1,128)S(1)}, s32[1,8]{1,0:T(1,128)}, u32[]{:S(2)}) copy-start(s32[1,8]{1,0:T(1,128)} %param.24) | copy-start | bytes 100
  112.3 19.2 %copy-start.2 = (f32[64]{0:T(128)}, f32[64]{0:T(128)S(1)}, u32[]{:S(2)}) copy-start(f32[64]{0:T(128)S(1)} %get-tuple-element.64) | copy-start | bytes 772
Sparse Core Ops, SparseCore 0:
  16.7 58.9 all-gather.1

commit v6 on v5

--- a/solution.py
+++ b/solution.py
@@ -150,6 +150,59 @@
         ],
         compiler_params=pltpu.CompilerParams(collective_id=1, has_side_effects=True),
     )(part, ids)
+
+
+def gather_kernel(n_tensor, block_ref, out_ref, send_sem, recv_sem, local_sem):
+    me = lax.axis_index("tensor")
+    dp = lax.axis_index("dp")
+    barrier = pltpu.get_barrier_semaphore()
+    for offset in range(1, n_tensor):
+        peer = lax.rem(me + offset, n_tensor)
+        pl.semaphore_signal(barrier, inc=1, device_id=(dp, peer), device_id_type=MESH)
+    pl.semaphore_wait(barrier, n_tensor - 1)
+    local = pltpu.make_async_copy(block_ref, out_ref.at[me], local_sem)
+    local.start()
+    copies = []
+    for offset in range(1, n_tensor):
+        peer = lax.rem(me + offset, n_tensor)
+        copy = pltpu.make_async_remote_copy(
+            src_ref=block_ref,
+            dst_ref=out_ref.at[me],
+            send_sem=send_sem.at[offset],
+            recv_sem=recv_sem.at[offset],
+            device_id=(dp, peer),
+            device_id_type=MESH,
+        )
+        copy.start()
+        copies.append(copy)
+    for copy in copies:
+        copy.wait_send()
+    for offset in range(1, n_tensor):
+        source = lax.rem(me + n_tensor - offset, n_tensor)
+        pltpu.make_async_remote_copy(
+            src_ref=block_ref,
+            dst_ref=out_ref.at[source],
+            send_sem=send_sem.at[offset],
+            recv_sem=recv_sem.at[offset],
+            device_id=(dp, source),
+            device_id_type=MESH,
+        ).wait_recv()
+    local.wait()
+
+
+def gather_rows(block, n_tensor):
+    return pl.pallas_call(
+        lambda *refs: gather_kernel(n_tensor, *refs),
+        out_shape=jax.ShapeDtypeStruct((n_tensor,) + block.shape, block.dtype),
+        in_specs=[pl.BlockSpec(memory_space=pl.ANY)],
+        out_specs=pl.BlockSpec(memory_space=pl.ANY),
+        scratch_shapes=[
+            pltpu.SemaphoreType.DMA((n_tensor,)),
+            pltpu.SemaphoreType.DMA((n_tensor,)),
+            pltpu.SemaphoreType.DMA(()),
+        ],
+        compiler_params=pltpu.CompilerParams(collective_id=2, has_side_effects=True),
+    )(block)
 
 
 def stats_kernel(x_ref, w_ref, id_ref, out_ref):
@@ -218,7 +271,7 @@
         .at[:, 1].set((compact_ids % 256).astype(jnp.bfloat16))
     )
     block = jnp.concatenate([compact_rows, meta], axis=1)
-    gathered = lax.all_gather(block, "tensor", axis=0, tiled=True)
+    gathered = gather_rows(block, n_tensor).reshape(n_tensor * LIVE, block.shape[1])
     meta_cols = gathered[:, width:width + 2].astype(jnp.float32)
     piece_ids = (meta_cols[:, 0] * 256.0 + meta_cols[:, 1]).astype(jnp.int32)
     local_ids = (piece_ids - tensor_index * vocab_local)[:, None]

time: 139 us -> 237 us (1.71)
  Pallas kernels: 45.7 us -> 203 us
  waiting for transfers between devices: 46.6 us -> 0 us
  between operations: 14.2 us -> 0.78 us
    pallas_call x0 -> x1, Pallas kernels: none -> 130 us  [gather_rows(): pl.pallas_call(lambda *refs: gather_kernel(n_tensor, *refs), out_shape=ja...]
    all_gather x1 -> x0, waiting for transfers between devices: 46.6 us -> none  [on_device(): gathered = lax.all_gather(block, 'tensor', axis=0, tiled=True)]
    pallas_call x1, Pallas kernels: 9.63 us -> 34.7 us  [exchange(): pl.pallas_call(lambda *refs: exchange_kernel(n_tensor, *refs), out_shape=...]
    unnamed x12 -> x10, local copies, waits for them, and re-layouts: 10.3 us -> 10.3 us
  transfers between devices with their start and end apart: 1 -> 0, of which waited for: 1 -> 0; matrix products, arithmetic and copies ran while one was open for 9% -> 0% of each run, Pallas kernels for 0% -> 0%
where the time goes in v6:
time: 237 us
  Pallas kernels  203 us (86%)
  local copies, waits for them, and re-layouts  18.6 us (8%)
  other arithmetic  13 us (5%)
    pallas_call x1, Pallas kernels, gather_rows(): pl.pallas_call(lambda *refs: gather_kernel(n_tensor, *refs), out_shape=ja...  130 us
    pallas_call x1, Pallas kernels, exchange(): pl.pallas_call(lambda *refs: exchange_kernel(n_tensor, *refs), out_shape=...  34.7 us
    pallas_call x1, Pallas kernels, row_stats(): pl.pallas_call(stats_kernel, out_shape=jax.ShapeDtypeStruct((count, 128),...  19.3 us
    pallas_call x1, Pallas kernels, route(): pl.pallas_call(lambda *refs: route_kernel(n_tensor, n_dp, *refs), out_sha...  19 us
    unnamed x10, local copies, waits for them, and re-layouts  10.3 us

profile of v6, /device:TPU:1, one launch (start us, length us, event | category | flops | bytes accessed | tf_op | source)
XLA Modules:
  0.0 236.5 jit_solution(13027006954637077896)
XLA Ops:
  0.6 0.6 compare_reduce_fusion.1
  1.3 0.6 compare_reduce_fusion
  1.9 0.7 convert_bitcast_fusion
  2.6 0.8 reduce-window.16
  3.5 1.1 fusion.3
  4.6 0.7 broadcast_compare_fusion
  5.3 0.6 scatter.19.refs_1_
  5.9 0.7 reshape.325
  6.6 0.7 copy.40
  7.5 0.1 select_reduce_fusion
  7.9 0.8 gather_fusion.1
  8.8 1.3 fusion.12
  10.2 0.1 scatter.15
  10.3 1.1 fusion.5
  11.4 1.4 fusion
  12.7 0.7 gather_fusion
  13.5 0.7 pad_maximum_fusion.refs_0_
  14.2 129.7 %shard_map.111 = bf16[32,48,2176]{2,1,0:T(8,128)(2,1)} custom-call(bf16[48,2176]{1,0:T(8,128)(2,1)} %pad_maximum_fusion.refs_0_), custom_call_target="tpu_custom_call" | custom-call | tf_op jit(solution)/shard_map/pallas_call | solution.py:194
  144.0 1.0 slice_convert_fusion
  145.0 1.2 fusion.2.id_ref
  146.2 9.6 %copy.46.w_ref = bf16[2048,1572]{1,0:T(8,128)(2,1)} copy(bf16[2048,1572]{0,1:T(8,128)(2,1)} %param.20) | data formatting | bytes 12877824 | tf_op args[2]
  155.8 19.3 %shard_map.112 = f32[1536,128]{1,0:T(8,128)} custom-call(bf16[1536,2176]{1,0:T(8,128)(2,1)} %bitcast.27, bf16[2048,1572]{1,0:T(8,128)(2,1)} %copy.46.w_ref, s32[1536,1]{1,0:T(8,128)} %fusion.2.id_ref), custom_call_target="tpu_custom_call" | custom-call | flops 9890168832 | bytes 13516800 | tf_op jit(solution)/shard_map/pallas_call | solution.py:226
  175.1 2.1 copy.48
  177.2 34.7 %shard_map.113 = f32[32,4,48]{2,1,0:T(4,128)} custom-call(f32[32,4,48]{2,1,0:T(4,128)} %bitcast.29), custom_call_target="tpu_custom_call" | custom-call | tf_op jit(solution)/shard_map/pallas_call | solution.py:51
  211.9 1.1 fusion.14
  213.0 0.8 gather_fusion.3
  213.8 0.8 gather_fusion.2
  214.6 0.5 select_multiply_fusion
  215.3 0.6 scatter.16.refs_0_
  215.9 19.0 %shard_map.114 = f32[8,8,128]{2,1,0:T(8,128)} custom-call(f32[8,128]{1,0:T(8,128)} %scatter.16.refs_0_, f32[8,128]{1,0:T(8,128)} %scatter.19.refs_1_), custom_call_target="tpu_custom_call" | custom-call | tf_op jit(solution)/shard_map/pallas_call | solution.py:137
  234.8 0.9 slice_reduce_fusion.2
  235.8 0.7 select_reduce_fusion.1
  (30 shorter events, 1.1 us)
Async XLA Ops:
  0.6 7.3 %copy-start = (s32[64]{0:T(128)S(1)}, s32[64]{0:T(128)}, u32[]{:S(2)}) copy-start(s32[64]{0:T(128)} %param.22) | copy-start | bytes 772
  155.8 58.8 %copy-start.1 = (s32[64]{0:T(128)S(1)}, s32[64]{0:T(128)}, u32[]{:S(2)}) copy-start(s32[64]{0:T(128)} %param.23) | copy-start | bytes 772
  155.8 59.5 %copy-start.3 = (s32[1,8]{1,0:T(1,128)S(1)}, s32[1,8]{1,0:T(1,128)}, u32[]{:S(2)}) copy-start(s32[1,8]{1,0:T(1,128)} %param.24) | copy-start | bytes 100
  215.1 21.4 %copy-start.2 = (f32[64]{0:T(128)}, f32[64]{0:T(128)S(1)}, u32[]{:S(2)}) copy-start(f32[64]{0:T(128)S(1)} %get-tuple-element.64) | copy-start | bytes 772

commit v7 on v5

--- a/solution.py
+++ b/solution.py
@@ -150,6 +150,142 @@
         ],
         compiler_params=pltpu.CompilerParams(collective_id=1, has_side_effects=True),
     )(part, ids)
+
+
+def finish_kernel(n_tensor, n_dp, send_ref, span_ref, ids_ref, own_ref, routed_ref,
+                  held, t_held, d_held, part_msg, route_msg,
+                  a_send, a_recv, t_send, t_recv, d_send, d_recv):
+    me = lax.axis_index("tensor")
+    dp = lax.axis_index("dp")
+    barrier = pltpu.get_barrier_semaphore()
+    for offset in range(1, n_tensor):
+        peer = lax.rem(me + offset, n_tensor)
+        pl.semaphore_signal(barrier, inc=1, device_id=(dp, peer), device_id_type=MESH)
+    for offset in range(1, n_dp):
+        peer = lax.rem(dp + offset, n_dp)
+        pl.semaphore_signal(barrier, inc=1, device_id=(peer, me), device_id_type=MESH)
+    pl.semaphore_wait(barrier, n_tensor - 1 + n_dp - 1)
+
+    held[me] = send_ref[me]
+    copies = []
+    for offset in range(1, n_tensor):
+        peer = lax.rem(me + offset, n_tensor)
+        copy = pltpu.make_async_remote_copy(
+            src_ref=send_ref.at[peer], dst_ref=held.at[me],
+            send_sem=a_send.at[offset], recv_sem=a_recv.at[offset],
+            device_id=(dp, peer), device_id_type=MESH,
+        )
+        copy.start()
+        copies.append(copy)
+    for copy in copies:
+        copy.wait_send()
+    for offset in range(1, n_tensor):
+        source = lax.rem(me + n_tensor - offset, n_tensor)
+        pltpu.make_async_remote_copy(
+            src_ref=send_ref.at[source], dst_ref=held.at[source],
+            send_sem=a_send.at[offset], recv_sem=a_recv.at[offset],
+            device_id=(dp, source), device_id_type=MESH,
+        ).wait_recv()
+
+    lanes = held.shape[2]
+    peak = lax.fori_loop(
+        0, n_tensor, lambda p, m: jnp.maximum(m, held[p][0:1, :]),
+        jnp.full((1, lanes), -jnp.inf, jnp.float32),
+    )
+
+    def gather_sums(p, sums):
+        mass, spread, target = sums
+        block = held[p]
+        gap = block[0:1, :] - peak
+        factor = jnp.exp(gap)
+        mass = mass + factor * block[1:2, :]
+        spread = spread + factor * (block[2:3, :] + gap * block[1:2, :])
+        return mass, spread, target + block[3:4, :]
+
+    zero = jnp.zeros((1, lanes), jnp.float32)
+    mass, spread, target = lax.fori_loop(0, n_tensor, gather_sums, (zero, zero, zero))
+    log_mass = jnp.log(mass)
+    logprob = target - peak - log_mass
+    entropy = log_mass - spread / mass
+    row = lax.broadcasted_iota(jnp.int32, own_ref.shape, 0)
+    own_ref[...] = jnp.where(row == 0, logprob, jnp.where(row == 1, entropy, 0.0))
+
+    spans = span_ref[...]
+    partial = jnp.sum(spans[:, :lanes] * logprob, axis=1, keepdims=True) / spans[:, 127:128]
+    part_msg[...] = jnp.broadcast_to(partial, part_msg.shape)
+    t_held[me] = part_msg[...]
+    copies = []
+    for offset in range(1, n_tensor):
+        peer = lax.rem(me + offset, n_tensor)
+        copy = pltpu.make_async_remote_copy(
+            src_ref=part_msg, dst_ref=t_held.at[me],
+            send_sem=t_send.at[offset], recv_sem=t_recv.at[offset],
+            device_id=(dp, peer), device_id_type=MESH,
+        )
+        copy.start()
+        copies.append(copy)
+    for copy in copies:
+        copy.wait_send()
+    for offset in range(1, n_tensor):
+        source = lax.rem(me + n_tensor - offset, n_tensor)
+        pltpu.make_async_remote_copy(
+            src_ref=part_msg, dst_ref=t_held.at[source],
+            send_sem=t_send.at[offset], recv_sem=t_recv.at[offset],
+            device_id=(dp, source), device_id_type=MESH,
+        ).wait_recv()
+
+    total = jnp.sum(t_held[...], axis=0)
+    lane = lax.broadcasted_iota(jnp.int32, total.shape, 1)
+    route_msg[...] = jnp.where(lane == 0, total, jnp.where(lane == 1, ids_ref[...], 0.0))
+    d_held[dp] = route_msg[...]
+    copies = []
+    for offset in range(1, n_dp):
+        peer = lax.rem(dp + offset, n_dp)
+        copy = pltpu.make_async_remote_copy(
+            src_ref=route_msg, dst_ref=d_held.at[dp],
+            send_sem=d_send.at[offset], recv_sem=d_recv.at[offset],
+            device_id=(peer, me), device_id_type=MESH,
+        )
+        copy.start()
+        copies.append(copy)
+    for copy in copies:
+        copy.wait_send()
+    for offset in range(1, n_dp):
+        source = lax.rem(dp + n_dp - offset, n_dp)
+        pltpu.make_async_remote_copy(
+            src_ref=route_msg, dst_ref=d_held.at[source],
+            send_sem=d_send.at[offset], recv_sem=d_recv.at[offset],
+            device_id=(source, me), device_id_type=MESH,
+        ).wait_recv()
+    routed_ref[...] = d_held[...]
+
+
+def finish(blocks, spans, ids, n_tensor, n_dp):
+    tile = spans.shape
+    lanes = blocks.shape[2]
+    return pl.pallas_call(
+        lambda *refs: finish_kernel(n_tensor, n_dp, *refs),
+        out_shape=(
+            jax.ShapeDtypeStruct((8, lanes), jnp.float32),
+            jax.ShapeDtypeStruct((n_dp,) + tile, jnp.float32),
+        ),
+        in_specs=[pl.BlockSpec(memory_space=pltpu.VMEM)] * 3,
+        out_specs=(pl.BlockSpec(memory_space=pltpu.VMEM), pl.BlockSpec(memory_space=pltpu.VMEM)),
+        scratch_shapes=[
+            pltpu.VMEM(blocks.shape, jnp.float32),
+            pltpu.VMEM((n_tensor,) + tile, jnp.float32),
+            pltpu.VMEM((n_dp,) + tile, jnp.float32),
+            pltpu.VMEM(tile, jnp.float32),
+            pltpu.VMEM(tile, jnp.float32),
+            pltpu.SemaphoreType.DMA((n_tensor,)),
+            pltpu.SemaphoreType.DMA((n_tensor,)),
+            pltpu.SemaphoreType.DMA((n_tensor,)),
+            pltpu.SemaphoreType.DMA((n_tensor,)),
+            pltpu.SemaphoreType.DMA((n_dp,)),
+            pltpu.SemaphoreType.DMA((n_dp,)),
+        ],
+        compiler_params=pltpu.CompilerParams(collective_id=3, has_side_effects=True),
+    )(blocks, spans, ids)
 
 
 def stats_kernel(x_ref, w_ref, id_ref, out_ref):
@@ -225,34 +361,25 @@
     row_count = gathered.shape[0]
     stats = row_stats(gathered, head_weight, local_ids, width, 256 if row_count % 256 == 0 else row_count)
     blocks = stats[:, :4].reshape(n_tensor, LIVE, 4).transpose(0, 2, 1)
-    parts = exchange(blocks, n_tensor)
-    part_peak, part_mass, part_spread, part_target = parts[:, 0], parts[:, 1], parts[:, 2], parts[:, 3]
-    peak = jnp.max(part_peak, axis=0)
-    gap = part_peak - peak[None, :]
-    factor = jnp.exp(gap)
-    mass = jnp.sum(factor * part_mass, axis=0)
-    spread = jnp.sum(factor * (part_spread + gap * part_mass), axis=0)
-    target = jnp.sum(part_target, axis=0)
-    log_mass = jnp.log(mass)
-    place = jnp.clip(live_sum - 1, 0, LIVE - 1)
-    token_logprob = weight_mask * jnp.take(target - peak - log_mass, place)
-    token_entropy = weight_mask * jnp.take(log_mass - spread / mass, place)
-
     request_count = lengths.shape[1]
     span_lengths = lengths[0]
     span_ends = jnp.cumsum(span_lengths)
-    slot_ids = tensor_index * own_rows + jnp.arange(own_rows, dtype=jnp.int32)
+    slot_ids = tensor_index * own_rows + source
     position = jnp.sum((slot_ids[:, None] >= span_ends[None, :]).astype(jnp.int32), axis=1)
-    onehot = position[:, None] == jnp.arange(request_count, dtype=jnp.int32)[None, :]
-    by_pos = jnp.sum(jnp.where(onehot, token_logprob[:, None], 0.0), axis=0) / span_lengths.astype(
-        jnp.float32
-    )
-    tile = jnp.zeros((8, 128), jnp.float32)
-    part_tile = tile.at[0, :request_count].set(by_pos)
-    ids_tile = tile.at[1, :request_count].set(request_order.astype(jnp.float32))
-    routed = route(part_tile, ids_tile, n_tensor, n_dp)
-    all_totals = routed[:, 0, :request_count].reshape(-1)
-    all_owners = routed[:, 1, :request_count].reshape(-1)
+    live = jnp.arange(LIVE, dtype=jnp.int32) < live_sum[-1]
+    member = (position[None, :] == jnp.arange(8, dtype=jnp.int32)[:, None]) & live[None, :]
+    spans = (
+        jnp.zeros((8, 128), jnp.float32)
+        .at[:, :LIVE].set(member.astype(jnp.float32))
+        .at[:, 127].set(jnp.ones((8,), jnp.float32).at[:request_count].set(span_lengths.astype(jnp.float32)))
+    )
+    ids_tile = jnp.zeros((8, 128), jnp.float32).at[:request_count, 1].set(request_order.astype(jnp.float32))
+    own, routed = finish(blocks, spans, ids_tile, n_tensor, n_dp)
+    place = jnp.clip(live_sum - 1, 0, LIVE - 1)
+    token_logprob = weight_mask * jnp.take(own[0], place)
+    token_entropy = weight_mask * jnp.take(own[1], place)
+    all_totals = routed[:, :request_count, 0].reshape(-1)
+    all_owners = routed[:, :request_count, 1].reshape(-1)
     wanted = (lax.axis_index("dp") * request_count + jnp.arange(request_count)).astype(jnp.float32)
     route_table = all_owners[:, None] == wanted[None, :]
     request_score = jnp.sum(jnp.where(route_table, all_totals[:, None], 0.0), axis=0)

time: 139 us -> 135 us (0.971)
  waiting for transfers between devices: 46.6 us -> 41.9 us
  Pallas kernels: 45.7 us -> 42.2 us
  other arithmetic: 12.4 us -> 15 us
    all_gather x1, waiting for transfers between devices: 46.6 us -> 41.9 us  [on_device(): gathered = lax.all_gather(block, 'tensor', axis=0, tiled=True)]
    pallas_call x2 -> x1, Pallas kernels: 26.3 us -> 22.9 us  [finish(): pl.pallas_call(lambda *refs: finish_kernel(n_tensor, n_dp, *refs), out_sh...]
    another operation x6 -> x9, other arithmetic: 3.54 us -> 6.78 us
    unnamed x12 -> x8, local copies, waits for them, and re-layouts: 10.3 us -> 10.3 us
  transfers between devices with their start and end apart: 1 -> 1, of which waited for: 1 -> 1; matrix products, arithmetic and copies ran while one was open for 9% -> 13% of each run, Pallas kernels for 0% -> 0%
where the time goes in v7:
time: 135 us; the launch traced here: 134 us
  Pallas kernels  42.2 us (31%)
  waiting for transfers between devices  41.9 us (31%)
  local copies, waits for them, and re-layouts  19.8 us (15%)
  other arithmetic  15 us (11%)
  between operations  14.2 us (11%)
    all_gather x1, waiting for transfers between devices, on_device(): gathered = lax.all_gather(block, 'tensor', axis=0, tiled=True)  41.9 us
    pallas_call x1, Pallas kernels, finish(): pl.pallas_call(lambda *refs: finish_kernel(n_tensor, n_dp, *refs), out_sh...  22.9 us
    pallas_call x1, Pallas kernels, row_stats(): pl.pallas_call(stats_kernel, out_shape=jax.ShapeDtypeStruct((count, 128),...  19.3 us
    unnamed x8, local copies, waits for them, and re-layouts  10.3 us
    another operation x9, other arithmetic  6.78 us
  transfers between devices with their start and end apart: 1, of which 1 were waited for; matrix products, arithmetic and copies ran while one was open for 13% of the time, Pallas kernels for 0%

profile of v7, /device:TPU:1, one launch (start us, length us, event | category | flops | bytes accessed | tf_op | source)
XLA Modules:
  0.0 133.8 jit_solution(8023256537438965565)
XLA Ops:
  7.2 0.6 compare_reduce_fusion.2
  7.9 0.6 compare_reduce_fusion.1
  8.5 1.1 fusion.3
  9.6 0.7 broadcast_compare_fusion
  10.3 0.7 copy.40
  11.6 0.8 gather_fusion.1
  12.5 1.1 fusion.5
  13.6 0.7 gather_fusion
  14.3 1.3 fusion.12
  15.9 0.7 pad_maximum_fusion
  17.1 0.8 reduce-window.14
  18.0 0.7 convert_bitcast_fusion
  18.7 1.3 fusion.15
  20.1 0.7 reshape.358
  20.8 0.7 scatter.24.refs_2_
  21.4 0.6 compare_reduce_fusion
  22.1 0.6 iota_compare_fusion.2
  22.8 0.7 convert_select_fusion
  23.5 9.6 %copy.46.w_ref = bf16[2048,1572]{1,0:T(8,128)(2,1)} copy(bf16[2048,1572]{0,1:T(8,128)(2,1)} %param.26) | data formatting | bytes 12877824 | tf_op args[2]
  33.2 0.7 fusion
  33.9 41.9 %all-gather.2.cloned.1.call-done.x_ref = bf16[1536,2176]{1,0:T(8,128)(2,1)} async-done(((bf16[48,2176]{1,0:T(8,128)(2,1)}), bf16[1536,2176]{1,0:T(8,128)(2,1)}) %all-gather.2.cloned.1.call-update) | async-done | bytes 6684688 | tf_op jit(solution)/shard_map/all_gather | solution.py:357
  75.8 1.0 slice_convert_fusion
  76.8 1.2 fusion.2.id_ref
  78.0 19.3 %shard_map.116 = f32[1536,128]{1,0:T(8,128)} custom-call(bf16[1536,2176]{1,0:T(8,128)(2,1)} %all-gather.2.cloned.1.call-done.x_ref, bf16[2048,1572]{1,0:T(8,128)(2,1)} %copy.46.w_ref, s32[1536,1]{1,0:T(8,128)} %fusion.2.id_ref), custom_call_target="tpu_custom_call" | custom-call | flops 9890168832 | bytes 13516800 | tf_op jit(solution)/shard_map/pallas_call | solution.py:309
  97.3 2.1 %copy.48 = f32[32,48,4]{1,2,0:T(4,128)} copy(f32[32,48,4]{2,1,0:T(8,128)} %bitcast.23) | data formatting | bytes 49152 | tf_op jit(solution)/shard_map/reshape | solution.py:363
  99.4 22.9 %shard_map.117 = (f32[8,48]{1,0:T(8,128)}, f32[8,8,128]{2,1,0:T(8,128)}) custom-call(f32[32,4,48]{2,1,0:T(4,128)} %bitcast.24, f32[8,128]{1,0:T(8,128)} %copy-done.1, f32[8,128]{1,0:T(8,128)} %scatter.24.refs_2_), custom_call_target="tpu_custom_call" | custom-call | tf_op jit(solution)/shard_map/pallas_call | solution.py:266
  122.3 0.8 slice_bitcast_fusion
  123.0 0.8 gather_fusion.3
  123.8 0.8 gather_fusion.2
  124.6 1.0 slice_reduce_fusion.1
  125.7 0.5 select_multiply_fusion
  126.3 0.7 select_reduce_fusion.1
  (32 shorter events, 2.0 us)
Async XLA Ops:
  7.2 4.4 %copy-start = (s32[64]{0:T(128)S(1)}, s32[64]{0:T(128)}, u32[]{:S(2)}) copy-start(s32[64]{0:T(128)} %param.28) | copy-start | bytes 772
  7.2 68.6 %all-gather.2.cloned.1.call-start = ((), (), s32[]{:S(2)}) async-start(), calls=%async_computation | async-start | bytes 6893568 | tf_op jit(solution)/shard_map/all_gather | solution.py:357
  16.6 16.6 %copy-start.2 = (s32[64]{0:T(128)S(1)}, s32[64]{0:T(128)}, u32[]{:S(2)}) copy-start(s32[64]{0:T(128)} %param.29) | copy-start | bytes 772
  33.2 64.2 %copy-start.1 = (f32[8,128]{1,0:T(8,128)}, f32[8,128]{1,0:T(8,128)S(1)}, u32[]{:S(2)}) copy-start(f32[8,128]{1,0:T(8,128)S(1)} %scatter.21.refs_1_) | copy-start | bytes 12292
Sparse Core Ops, SparseCore 0:
  16.7 58.9 all-gather.1

commit v8 on v7

--- a/solution.py
+++ b/solution.py
@@ -286,6 +286,42 @@
         ],
         compiler_params=pltpu.CompilerParams(collective_id=3, has_side_effects=True),
     )(blocks, spans, ids)
+
+
+def prep_kernel(hidden_ref, gain_ref, mask_ref, ids_ref, out_ref):
+    width = hidden_ref.shape[1]
+    own_rows = hidden_ref.shape[0]
+    widened = hidden_ref[...].astype(jnp.float32)
+    inverse_rms = lax.rsqrt(jnp.mean(widened * widened, axis=1, keepdims=True) + EPSILON)
+    normed = (widened * inverse_rms * gain_ref[...]).astype(jnp.bfloat16)
+    live = jnp.broadcast_to(mask_ref[...].astype(jnp.float32), (8, own_rows))
+    upper = (
+        lax.broadcasted_iota(jnp.int32, (own_rows, own_rows), 0)
+        <= lax.broadcasted_iota(jnp.int32, (own_rows, own_rows), 1)
+    ).astype(jnp.float32)
+    live_sum = jnp.dot(live, upper, preferred_element_type=jnp.float32)[0:1, :]
+    rank = lax.broadcasted_iota(jnp.int32, (LIVE, own_rows), 0).astype(jnp.float32)
+    chosen = ((live[0:1, :] == 1.0) & (live_sum - 1.0 == rank)).astype(jnp.bfloat16)
+    out_ref[:, :width] = jnp.dot(chosen, normed, preferred_element_type=jnp.float32).astype(jnp.bfloat16)
+    ids = ids_ref[...]
+    high = lax.shift_right_logical(ids, 8).astype(jnp.float32)
+    low = jnp.bitwise_and(ids, 255).astype(jnp.float32)
+    row = lax.broadcasted_iota(jnp.int32, (128, own_rows), 0)
+    meta_in = jnp.where(row == 0, high, jnp.where(row == 1, low, 0.0)).astype(jnp.bfloat16)
+    meta = lax.dot_general(
+        chosen, meta_in, (((1,), (1,)), ((), ())), preferred_element_type=jnp.float32
+    )
+    out_ref[:, width:] = meta.astype(jnp.bfloat16)
+
+
+def prep(hidden, norm_gain, slot_mask, token_ids):
+    own_rows, width = hidden.shape
+    return pl.pallas_call(
+        prep_kernel,
+        out_shape=jax.ShapeDtypeStruct((LIVE, width + 128), jnp.bfloat16),
+        in_specs=[pl.BlockSpec(memory_space=pltpu.VMEM)] * 4,
+        out_specs=pl.BlockSpec(memory_space=pltpu.VMEM),
+    )(hidden, norm_gain.reshape(1, width), slot_mask.reshape(1, own_rows), token_ids.reshape(1, own_rows))
 
 
 def stats_kernel(x_ref, w_ref, id_ref, out_ref):
@@ -346,14 +382,7 @@
         live_sum[None, :] - 1 == jnp.arange(LIVE, dtype=jnp.int32)[:, None]
     )
     source = jnp.sum(jnp.where(chosen, slot_index[None, :], 0), axis=1)
-    compact_rows = jnp.take(normed, source, axis=0)
-    compact_ids = jnp.take(token_ids, source)
-    meta = (
-        jnp.zeros((LIVE, 128), jnp.bfloat16)
-        .at[:, 0].set((compact_ids // 256).astype(jnp.bfloat16))
-        .at[:, 1].set((compact_ids % 256).astype(jnp.bfloat16))
-    )
-    block = jnp.concatenate([compact_rows, meta], axis=1)
+    block = prep(hidden, norm_gain, slot_mask, token_ids)
     gathered = lax.all_gather(block, "tensor", axis=0, tiled=True)
     meta_cols = gathered[:, width:width + 2].astype(jnp.float32)
     piece_ids = (meta_cols[:, 0] * 256.0 + meta_cols[:, 1]).astype(jnp.int32)

time: 135 us -> 128 us (0.948)
  other arithmetic: 15 us -> 7.46 us
  local copies, waits for them, and re-layouts: 19.8 us -> 16.7 us
  waiting for transfers between devices: 41.9 us -> 44.3 us
  Pallas kernels: 42.2 us -> 44.2 us
    another operation x9 -> x7, other arithmetic: 6.78 us -> 2.86 us
    all_gather x1, waiting for transfers between devices: 41.9 us -> 44.3 us  [on_device(): gathered = lax.all_gather(block, 'tensor', axis=0, tiled=True)]
    pallas_call x0 -> x1, Pallas kernels: none -> 2.02 us  [prep(): pl.pallas_call(prep_kernel, out_shape=jax.ShapeDtypeStruct((LIVE, width +...]
    gather x3 -> x0, local copies, waits for them, and re-layouts: 1.57 us -> none  [the longest x2 0.87 us: on_device(): compact_ids = jnp.take(token_ids, source)]
    unnamed x8 -> x16, local copies, waits for them, and re-layouts: 10.3 us -> 9.66 us
  transfers between devices with their start and end apart: 1 -> 1, of which waited for: 1 -> 1; matrix products, arithmetic and copies ran while one was open for 13% -> 12% of each run, Pallas kernels for 0% -> 0%
where the time goes in v8:
time: 128 us
  waiting for transfers between devices  44.3 us (35%)
  Pallas kernels  44.2 us (35%)
  local copies, waits for them, and re-layouts  16.7 us (13%)
  between operations  14.2 us (11%)
  other arithmetic  7.46 us (6%)
    all_gather x1, waiting for transfers between devices, on_device(): gathered = lax.all_gather(block, 'tensor', axis=0, tiled=True)  44.3 us
    pallas_call x1, Pallas kernels, finish(): pl.pallas_call(lambda *refs: finish_kernel(n_tensor, n_dp, *refs), out_sh...  22.9 us
    pallas_call x1, Pallas kernels, row_stats(): pl.pallas_call(stats_kernel, out_shape=jax.ShapeDtypeStruct((count, 128),...  19.3 us
    unnamed x16, local copies, waits for them, and re-layouts  9.66 us
    another operation x7, other arithmetic  2.86 us
  transfers between devices with their start and end apart: 1, of which 1 were waited for; matrix products, arithmetic and copies ran while one was open for 12% of the time, Pallas kernels for 0%

profile of v8, /device:TPU:1, one launch (start us, length us, event | category | flops | bytes accessed | tf_op | source)
XLA Modules:
  0.0 127.7 jit_solution(4764786475052368334)
XLA Ops:
  7.2 2.0 %shard_map.116 = bf16[48,2176]{1,0:T(8,128)(2,1)} custom-call(bf16[64,2048]{1,0:T(8,128)(2,1)} %hidden_ref.1, f32[1,2048]{1,0:T(1,128)} %bitcast.25, s32[1,64]{1,0:T(1,128)} %bitcast.26, s32[1,64]{1,0:T(1,128)} %bitcast.28), custom_call_target="tpu_custom_call" | custom-call | tf_op jit(solution)/shard_map/pallas_call | solution.py:319
  9.3 9.6 %copy.30.w_ref = bf16[2048,1572]{1,0:T(8,128)(2,1)} copy(bf16[2048,1572]{0,1:T(8,128)(2,1)} %param.22) | data formatting | bytes 12877824 | tf_op args[2]
  18.9 0.1 copy.28
  19.0 0.1 reduce-window.13
  19.1 0.2 reduce-window.14
  19.3 0.5 slice.99
  19.8 0.1 copy.33
  19.9 0.6 compare_reduce_fusion
  20.6 0.6 fusion.11
  21.2 0.1 copy.34
  21.3 0.6 compare_reduce_fusion.1
  21.9 0.6 iota_compare_fusion.2
  22.6 0.1 add_reduce_fusion
  22.7 0.1 select_reduce_fusion
  22.8 0.1 convert_reduce_fusion
  22.9 0.7 convert_select_fusion
  23.6 0.7 scatter.14.refs_2_
  24.3 0.1 scatter.11.refs_1_
  24.5 0.2 fusion.3
  24.6 0.8 fusion
  25.4 44.3 %all-gather.2.cloned.1.call-done.x_ref = bf16[1536,2176]{1,0:T(8,128)(2,1)} async-done(((bf16[48,2176]{1,0:T(8,128)(2,1)}), bf16[1536,2176]{1,0:T(8,128)(2,1)}) %all-gather.2.cloned.1.call-update) | async-done | bytes 6684688 | tf_op jit(solution)/shard_map/all_gather | solution.py:386
  69.7 1.0 slice_convert_fusion
  70.7 1.2 fusion.2.id_ref
  71.9 19.3 %shard_map.117 = f32[1536,128]{1,0:T(8,128)} custom-call(bf16[1536,2176]{1,0:T(8,128)(2,1)} %all-gather.2.cloned.1.call-done.x_ref, bf16[2048,1572]{1,0:T(8,128)(2,1)} %copy.30.w_ref, s32[1536,1]{1,0:T(8,128)} %fusion.2.id_ref), custom_call_target="tpu_custom_call" | custom-call | flops 9890168832 | bytes 13516800 | tf_op jit(solution)/shard_map/pallas_call | solution.py:345
  91.2 2.1 %copy.32 = f32[32,48,4]{1,2,0:T(4,128)} copy(f32[32,48,4]{2,1,0:T(8,128)} %bitcast.23) | data formatting | bytes 49152 | tf_op jit(solution)/shard_map/reshape | solution.py:392
  93.3 22.9 %shard_map.118 = (f32[8,48]{1,0:T(8,128)}, f32[8,8,128]{2,1,0:T(8,128)}) custom-call(f32[32,4,48]{2,1,0:T(4,128)} %bitcast.24, f32[8,128]{1,0:T(8,128)} %copy-done.1, f32[8,128]{1,0:T(8,128)} %scatter.14.refs_2_), custom_call_target="tpu_custom_call" | custom-call | tf_op jit(solution)/shard_map/pallas_call | solution.py:266
  116.2 0.8 slice_bitcast_fusion
  116.9 0.8 gather_fusion.1
  117.7 0.8 gather_fusion
  118.5 1.0 slice_reduce_fusion.1
  119.7 0.5 select_multiply_fusion
  120.2 0.7 select_reduce_fusion.1
  (27 shorter events, 0.3 us)
Async XLA Ops:
  7.2 62.5 %all-gather.2.cloned.1.call-start = ((), (), s32[]{:S(2)}) async-start(), calls=%async_computation | async-start | bytes 6893568 | tf_op jit(solution)/shard_map/all_gather | solution.py:386
  9.3 9.7 %copy-start.3 = (s32[64]{0:T(128)S(1)}, s32[64]{0:T(128)}, u32[]{:S(2)}) copy-start(s32[64]{0:T(128)} %param.25) | copy-start | bytes 772
  9.3 9.9 %copy-start.5 = (s32[1,8]{1,0:T(1,128)S(1)}, s32[1,8]{1,0:T(1,128)}, u32[]{:S(2)}) copy-start(s32[1,8]{1,0:T(1,128)} %param.26) | copy-start | bytes 100
  9.3 11.3 %copy-start.6 = (s32[8]{0:T(128)S(1)}, s32[8]{0:T(128)}, u32[]{:S(2)}) copy-start(s32[8]{0:T(128)} %param.27) | copy-start | bytes 100
  9.3 15.0 %copy-start.4 = (bf16[2048]{0:T(1024)(128)(2,1)S(1)}, bf16[2048]{0:T(1024)(128)(2,1)}, u32[]{:S(2)}) copy-start(bf16[2048]{0:T(1024)(128)(2,1)} %param.23) | copy-start | bytes 12292
  9.3 15.1 %copy-start = (bf16[64,2048]{1,0:T(8,128)(2,1)S(1)}, bf16[64,2048]{1,0:T(8,128)(2,1)}, u32[]{:S(2)}) copy-start(bf16[64,2048]{1,0:T(8,128)(2,1)} %hidden_ref.1) | copy-start | bytes 786436
  9.3 15.3 %copy-start.2 = (f32[2048]{0:T(1024)S(1)}, f32[2048]{0:T(1024)}, u32[]{:S(2)}) copy-start(f32[2048]{0:T(1024)} %param.21) | copy-start | bytes 24580
  24.4 66.8 %copy-start.1 = (f32[8,128]{1,0:T(8,128)}, f32[8,128]{1,0:T(8,128)S(1)}, u32[]{:S(2)}) copy-start(f32[8,128]{1,0:T(8,128)S(1)} %scatter.11.refs_1_) | copy-start | bytes 12292
Sparse Core Ops, SparseCore 0:
  10.6 59.0 all-gather.1

commit v9 on v8

--- a/solution.py
+++ b/solution.py
@@ -3,32 +3,44 @@
 from jax import lax
 from jax.experimental import pallas as pl
 from jax.experimental.pallas import tpu as pltpu
-from jax.sharding import PartitionSpec as P
+from jax.sharding import Mesh, PartitionSpec as P
 
 EPSILON = 1e-06
 MESH = pl.DeviceIdType.MESH
 LIVE = 48
 
 
-def exchange_kernel(n_tensor, send_ref, out_ref, held, send_sem, recv_sem):
-    me = lax.axis_index("tensor")
+def tensor_place(t, shape):
+    return (t // (shape[1] * shape[2]), (t // shape[2]) % shape[1], t % shape[2])
+
+
+def tensor_position(shape):
+    return (lax.axis_index("x") * shape[1] + lax.axis_index("y")) * shape[2] + lax.axis_index("core")
+
+
+def finish_kernel(n_tensor, n_dp, shape, send_ref, span_ref, ids_ref, own_ref, routed_ref,
+                  held, t_held, d_held, part_msg, route_msg,
+                  a_send, a_recv, t_send, t_recv, d_send, d_recv):
+    me = tensor_position(shape)
+    mine = (lax.axis_index("x"), lax.axis_index("y"), lax.axis_index("core"))
     dp = lax.axis_index("dp")
     barrier = pltpu.get_barrier_semaphore()
     for offset in range(1, n_tensor):
         peer = lax.rem(me + offset, n_tensor)
-        pl.semaphore_signal(barrier, inc=1, device_id=(dp, peer), device_id_type=MESH)
-    pl.semaphore_wait(barrier, n_tensor - 1)
+        pl.semaphore_signal(barrier, inc=1, device_id=(dp,) + tensor_place(peer, shape), device_id_type=MESH)
+    for offset in range(1, n_dp):
+        peer = lax.rem(dp + offset, n_dp)
+        pl.semaphore_signal(barrier, inc=1, device_id=(peer,) + mine, device_id_type=MESH)
+    pl.semaphore_wait(barrier, n_tensor - 1 + n_dp - 1)
+
     held[me] = send_ref[me]
     copies = []
     for offset in range(1, n_tensor):
         peer = lax.rem(me + offset, n_tensor)
         copy = pltpu.make_async_remote_copy(
-            src_ref=send_ref.at[peer],
-            dst_ref=held.at[me],
-            send_sem=send_sem.at[offset],
-            recv_sem=recv_sem.at[offset],
-            device_id=(dp, peer),
-            device_id_type=MESH,
+            src_ref=send_ref.at[peer], dst_ref=held.at[me],
+            send_sem=a_send.at[offset], recv_sem=a_recv.at[offset],
+            device_id=(dp,) + tensor_place(peer, shape), device_id_type=MESH,
         )
         copy.start()
         copies.append(copy)
@@ -37,154 +49,9 @@
     for offset in range(1, n_tensor):
         source = lax.rem(me + n_tensor - offset, n_tensor)
         pltpu.make_async_remote_copy(
-            src_ref=send_ref.at[source],
-            dst_ref=held.at[source],
-            send_sem=send_sem.at[offset],
-            recv_sem=recv_sem.at[offset],
-            device_id=(dp, source),
-            device_id_type=MESH,
-        ).wait_recv()
-    out_ref[...] = held[...]
-
-
-def exchange(blocks, n_tensor):
-    return pl.pallas_call(
-        lambda *refs: exchange_kernel(n_tensor, *refs),
-        out_shape=jax.ShapeDtypeStruct(blocks.shape, blocks.dtype),
-        in_specs=[pl.BlockSpec(memory_space=pltpu.VMEM)],
-        out_specs=pl.BlockSpec(memory_space=pltpu.VMEM),
-        scratch_shapes=[
-            pltpu.VMEM(blocks.shape, blocks.dtype),
-            pltpu.SemaphoreType.DMA((n_tensor,)),
-            pltpu.SemaphoreType.DMA((n_tensor,)),
-        ],
-        compiler_params=pltpu.CompilerParams(collective_id=0, has_side_effects=True),
-    )(blocks)
-
-
-def route_kernel(n_tensor, n_dp, part_ref, ids_ref, out_ref, t_held, d_held, msg,
-                 t_send, t_recv, d_send, d_recv):
-    me = lax.axis_index("tensor")
-    dp = lax.axis_index("dp")
-    barrier = pltpu.get_barrier_semaphore()
-    for offset in range(1, n_tensor):
-        peer = lax.rem(me + offset, n_tensor)
-        pl.semaphore_signal(barrier, inc=1, device_id=(dp, peer), device_id_type=MESH)
-    for offset in range(1, n_dp):
-        peer = lax.rem(dp + offset, n_dp)
-        pl.semaphore_signal(barrier, inc=1, device_id=(peer, me), device_id_type=MESH)
-    pl.semaphore_wait(barrier, n_tensor - 1 + n_dp - 1)
-    t_held[me] = part_ref[...]
-    copies = []
-    for offset in range(1, n_tensor):
-        peer = lax.rem(me + offset, n_tensor)
-        copy = pltpu.make_async_remote_copy(
-            src_ref=part_ref,
-            dst_ref=t_held.at[me],
-            send_sem=t_send.at[offset],
-            recv_sem=t_recv.at[offset],
-            device_id=(dp, peer),
-            device_id_type=MESH,
-        )
-        copy.start()
-        copies.append(copy)
-    for copy in copies:
-        copy.wait_send()
-    for offset in range(1, n_tensor):
-        source = lax.rem(me + n_tensor - offset, n_tensor)
-        pltpu.make_async_remote_copy(
-            src_ref=part_ref,
-            dst_ref=t_held.at[source],
-            send_sem=t_send.at[offset],
-            recv_sem=t_recv.at[offset],
-            device_id=(dp, source),
-            device_id_type=MESH,
-        ).wait_recv()
-    total = jnp.sum(t_held[...], axis=0)
-    row = lax.broadcasted_iota(jnp.int32, total.shape, 0)
-    msg[...] = jnp.where(row == 0, total, jnp.where(row == 1, ids_ref[...], 0.0))
-    d_held[dp] = msg[...]
-    copies = []
-    for offset in range(1, n_dp):
-        peer = lax.rem(dp + offset, n_dp)
-        copy = pltpu.make_async_remote_copy(
-            src_ref=msg,
-            dst_ref=d_held.at[dp],
-            send_sem=d_send.at[offset],
-            recv_sem=d_recv.at[offset],
-            device_id=(peer, me),
-            device_id_type=MESH,
-        )
-        copy.start()
-        copies.append(copy)
-    for copy in copies:
-        copy.wait_send()
-    for offset in range(1, n_dp):
-        source = lax.rem(dp + n_dp - offset, n_dp)
-        pltpu.make_async_remote_copy(
-            src_ref=msg,
-            dst_ref=d_held.at[source],
-            send_sem=d_send.at[offset],
-            recv_sem=d_recv.at[offset],
-            device_id=(source, me),
-            device_id_type=MESH,
-        ).wait_recv()
-    out_ref[...] = d_held[...]
-
-
-def route(part, ids, n_tensor, n_dp):
-    tile = part.shape
-    return pl.pallas_call(
-        lambda *refs: route_kernel(n_tensor, n_dp, *refs),
-        out_shape=jax.ShapeDtypeStruct((n_dp,) + tile, jnp.float32),
-        in_specs=[pl.BlockSpec(memory_space=pltpu.VMEM)] * 2,
-        out_specs=pl.BlockSpec(memory_space=pltpu.VMEM),
-        scratch_shapes=[
-            pltpu.VMEM((n_tensor,) + tile, jnp.float32),
-            pltpu.VMEM((n_dp,) + tile, jnp.float32),
-            pltpu.VMEM(tile, jnp.float32),
-            pltpu.SemaphoreType.DMA((n_tensor,)),
-            pltpu.SemaphoreType.DMA((n_tensor,)),
-            pltpu.SemaphoreType.DMA((n_dp,)),
-            pltpu.SemaphoreType.DMA((n_dp,)),
-        ],
-        compiler_params=pltpu.CompilerParams(collective_id=1, has_side_effects=True),
-    )(part, ids)
-
-
-def finish_kernel(n_tensor, n_dp, send_ref, span_ref, ids_ref, own_ref, routed_ref,
-                  held, t_held, d_held, part_msg, route_msg,
-                  a_send, a_recv, t_send, t_recv, d_send, d_recv):
-    me = lax.axis_index("tensor")
-    dp = lax.axis_index("dp")
-    barrier = pltpu.get_barrier_semaphore()
-    for offset in range(1, n_tensor):
-        peer = lax.rem(me + offset, n_tensor)
-        pl.semaphore_signal(barrier, inc=1, device_id=(dp, peer), device_id_type=MESH)
-    for offset in range(1, n_dp):
-        peer = lax.rem(dp + offset, n_dp)
-        pl.semaphore_signal(barrier, inc=1, device_id=(peer, me), device_id_type=MESH)
-    pl.semaphore_wait(barrier, n_tensor - 1 + n_dp - 1)
-
-    held[me] = send_ref[me]
-    copies = []
-    for offset in range(1, n_tensor):
-        peer = lax.rem(me + offset, n_tensor)
-        copy = pltpu.make_async_remote_copy(
-            src_ref=send_ref.at[peer], dst_ref=held.at[me],
-            send_sem=a_send.at[offset], recv_sem=a_recv.at[offset],
-            device_id=(dp, peer), device_id_type=MESH,
-        )
-        copy.start()
-        copies.append(copy)
-    for copy in copies:
-        copy.wait_send()
-    for offset in range(1, n_tensor):
-        source = lax.rem(me + n_tensor - offset, n_tensor)
-        pltpu.make_async_remote_copy(
             src_ref=send_ref.at[source], dst_ref=held.at[source],
             send_sem=a_send.at[offset], recv_sem=a_recv.at[offset],
-            device_id=(dp, source), device_id_type=MESH,
+            device_id=(dp,) + tensor_place(source, shape), device_id_type=MESH,
         ).wait_recv()
 
     lanes = held.shape[2]
@@ -220,7 +87,7 @@
         copy = pltpu.make_async_remote_copy(
             src_ref=part_msg, dst_ref=t_held.at[me],
             send_sem=t_send.at[offset], recv_sem=t_recv.at[offset],
-            device_id=(dp, peer), device_id_type=MESH,
+            device_id=(dp,) + tensor_place(peer, shape), device_id_type=MESH,
         )
         copy.start()
         copies.append(copy)
@@ -231,7 +98,7 @@
         pltpu.make_async_remote_copy(
             src_ref=part_msg, dst_ref=t_held.at[source],
             send_sem=t_send.at[offset], recv_sem=t_recv.at[offset],
-            device_id=(dp, source), device_id_type=MESH,
+            device_id=(dp,) + tensor_place(source, shape), device_id_type=MESH,
         ).wait_recv()
 
     total = jnp.sum(t_held[...], axis=0)
@@ -244,7 +111,7 @@
         copy = pltpu.make_async_remote_copy(
             src_ref=route_msg, dst_ref=d_held.at[dp],
             send_sem=d_send.at[offset], recv_sem=d_recv.at[offset],
-            device_id=(peer, me), device_id_type=MESH,
+            device_id=(peer,) + mine, device_id_type=MESH,
         )
         copy.start()
         copies.append(copy)
@@ -255,16 +122,16 @@
         pltpu.make_async_remote_copy(
             src_ref=route_msg, dst_ref=d_held.at[source],
             send_sem=d_send.at[offset], recv_sem=d_recv.at[offset],
-            device_id=(source, me), device_id_type=MESH,
+            device_id=(source,) + mine, device_id_type=MESH,
         ).wait_recv()
     routed_ref[...] = d_held[...]
 
 
-def finish(blocks, spans, ids, n_tensor, n_dp):
+def finish(blocks, spans, ids, n_tensor, n_dp, shape):
     tile = spans.shape
     lanes = blocks.shape[2]
     return pl.pallas_call(
-        lambda *refs: finish_kernel(n_tensor, n_dp, *refs),
+        lambda *refs: finish_kernel(n_tensor, n_dp, shape, *refs),
         out_shape=(
             jax.ShapeDtypeStruct((8, lanes), jnp.float32),
             jax.ShapeDtypeStruct((n_dp,) + tile, jnp.float32),
@@ -366,9 +233,10 @@
 ):
     own_rows = hidden.shape[0]
     vocab_local = head_weight.shape[1]
-    n_tensor = lax.axis_size("tensor")
+    shape = (lax.axis_size("x"), lax.axis_size("y"), lax.axis_size("core"))
+    n_tensor = shape[0] * shape[1] * shape[2]
     n_dp = lax.axis_size("dp")
-    tensor_index = lax.axis_index("tensor")
+    tensor_index = tensor_position(shape)
     widened = hidden.astype(jnp.float32)
     inverse_rms = lax.rsqrt(jnp.mean(widened * widened, axis=1, keepdims=True) + EPSILON)
     normed = (widened * inverse_rms * norm_gain).astype(jnp.bfloat16)
@@ -383,7 +251,10 @@
     )
     source = jnp.sum(jnp.where(chosen, slot_index[None, :], 0), axis=1)
     block = prep(hidden, norm_gain, slot_mask, token_ids)
-    gathered = lax.all_gather(block, "tensor", axis=0, tiled=True)
+    chip_rows = lax.all_gather(block, ("x", "y"), axis=0, tiled=True)
+    gathered = lax.all_gather(
+        chip_rows.reshape(shape[0] * shape[1], LIVE, block.shape[1]), "core", axis=1
+    ).reshape(n_tensor * LIVE, block.shape[1])
     meta_cols = gathered[:, width:width + 2].astype(jnp.float32)
     piece_ids = (meta_cols[:, 0] * 256.0 + meta_cols[:, 1]).astype(jnp.int32)
     local_ids = (piece_ids - tensor_index * vocab_local)[:, None]
@@ -403,7 +274,7 @@
         .at[:, 127].set(jnp.ones((8,), jnp.float32).at[:request_count].set(span_lengths.astype(jnp.float32)))
     )
     ids_tile = jnp.zeros((8, 128), jnp.float32).at[:request_count, 1].set(request_order.astype(jnp.float32))
-    own, routed = finish(blocks, spans, ids_tile, n_tensor, n_dp)
+    own, routed = finish(blocks, spans, ids_tile, n_tensor, n_dp, shape)
     place = jnp.clip(live_sum - 1, 0, LIVE - 1)
     token_logprob = weight_mask * jnp.take(own[0], place)
     token_entropy = weight_mask * jnp.take(own[1], place)
@@ -416,19 +287,26 @@
 
 
 def solution(mesh):
+    n_dp, n_tensor = mesh.devices.shape
+    cores = 2
+    rows = min(4, n_tensor // cores)
+    split = Mesh(
+        mesh.devices.reshape(n_dp, n_tensor // (rows * cores), rows, cores), ("dp", "x", "y", "core")
+    )
+    tensor = ("x", "y", "core")
     return jax.shard_map(
         on_device,
-        mesh=mesh,
+        mesh=split,
         in_specs=(
-            P(("dp", "tensor"), None),
+            P(("dp",) + tensor, None),
             P(),
-            P(None, "tensor"),
+            P(None, tensor),
             P(),
-            P(("dp", "tensor")),
-            P(("dp", "tensor")),
+            P(("dp",) + tensor),
+            P(("dp",) + tensor),
             P("dp", None),
             P("dp"),
         ),
-        out_specs=(P(("dp", "tensor")), P(("dp", "tensor")), P(("dp", "tensor")), P("dp")),
+        out_specs=(P(("dp",) + tensor), P(("dp",) + tensor), P(("dp",) + tensor), P("dp")),
         check_vma=False,
     )

time: 128 us -> 153 us (1.20)
  waiting for transfers between devices: 44.3 us -> 66.6 us
  Pallas kernels: 44.2 us -> 46.3 us
    all_gather x1 -> x2, waiting for transfers between devices: 44.3 us -> 66.6 us  [the longest x1 58.5 us: on_device(): chip_rows = lax.all_gather(block, ('x', 'y'), axis=0, tiled=True)]
    pallas_call x1, Pallas kernels: 22.9 us -> 25 us  [finish(): pl.pallas_call(lambda *refs: finish_kernel(n_tensor, n_dp, shape, *refs),...]
  transfers between devices with their start and end apart: 1 -> 2, of which waited for: 1 -> 2; matrix products, arithmetic and copies ran while one was open for 12% -> 10% of each run, Pallas kernels for 0% -> 0%
where the time goes in v9:
time: 153 us; the launch traced here: 152 us
  waiting for transfers between devices  66.6 us (44%)
  Pallas kernels  46.3 us (30%)
  local copies, waits for them, and re-layouts  16.7 us (11%)
  between operations  14.2 us (9%)
  other arithmetic  7.49 us (5%)
    all_gather x1, waiting for transfers between devices, on_device(): chip_rows = lax.all_gather(block, ('x', 'y'), axis=0, tiled=True)  58.5 us
    pallas_call x1, Pallas kernels, finish(): pl.pallas_call(lambda *refs: finish_kernel(n_tensor, n_dp, shape, *refs),...  25 us
    pallas_call x1, Pallas kernels, row_stats(): pl.pallas_call(stats_kernel, out_shape=jax.ShapeDtypeStruct((count, 128),...  19.3 us
    unnamed x16, local copies, waits for them, and re-layouts  9.66 us
    all_gather x1, waiting for transfers between devices, on_device(): lax.all_gather(chip_rows.reshape(shape[0] * shape[1], LIVE, block.shape[1...  8.11 us
  transfers between devices with their start and end apart: 2, of which 2 were waited for; matrix products, arithmetic and copies ran while one was open for 10% of the time, Pallas kernels for 0%

profile of v9, /device:TPU:1, one launch (start us, length us, event | category | flops | bytes accessed | tf_op | source)
XLA Modules:
  0.0 152.2 jit_solution(10041912933766525542)
XLA Ops:
  7.2 2.0 %shard_map.116 = bf16[48,2176]{1,0:T(8,128)(2,1)} custom-call(bf16[64,2048]{1,0:T(8,128)(2,1)} %hidden_ref.1, f32[1,2048]{1,0:T(1,128)} %bitcast.32, s32[1,64]{1,0:T(1,128)} %bitcast.33, s32[1,64]{1,0:T(1,128)} %bitcast.35), custom_call_target="tpu_custom_call" | custom-call | tf_op jit(solution)/shard_map/pallas_call | solution.py:186
  9.3 58.5 %all-gather.3.cloned.1.call-done = bf16[768,2176]{1,0:T(8,128)(2,1)} async-done(((bf16[48,2176]{1,0:T(8,128)(2,1)}), bf16[768,2176]{1,0:T(8,128)(2,1)}) %all-gather.3.cloned.1.call-update) | async-done | bytes 3342352 | tf_op jit(solution)/shard_map/all_gather | solution.py:254
  67.8 9.6 %copy.34.w_ref = bf16[2048,1572]{1,0:T(8,128)(2,1)} copy(bf16[2048,1572]{0,1:T(8,128)(2,1)} %param.22) | data formatting | bytes 12877824 | tf_op args[2]
  77.4 0.1 copy.31
  77.5 0.1 reduce-window.13
  77.6 0.2 reduce-window.14
  77.8 0.5 slice.99
  78.3 0.1 copy.37
  78.4 0.6 compare_reduce_fusion
  79.1 0.7 fusion.11
  79.8 0.6 compare_reduce_fusion.1
  80.5 0.7 iota_compare_fusion.2
  81.1 0.1 add_reduce_fusion
  81.2 0.1 select_reduce_fusion
  81.4 0.1 convert_reduce_fusion
  81.5 0.7 convert_select_fusion
  82.1 0.7 scatter.14.refs_2_
  82.8 0.1 scatter.11.refs_1_
  83.0 0.2 fusion.3
  83.1 0.8 fusion
  83.9 8.1 %all-gather.5.cloned.1.call-done = bf16[16,2,48,2176]{3,2,1,0:T(8,128)(2,1)} async-done(((bf16[16,1,48,2176]{3,2,1,0:T(8,128)(2,1)}), bf16[16,2,48,2176]{3,2,1,0:T(8,128)(2,1)}) %all-gather.5.cloned.1.call-update) | async-done | bytes 6684688 | tf_op jit(solution)/shard_map/all_gather | solution.py:255
  92.0 1.0 slice_convert_fusion
  93.1 1.2 fusion.2.id_ref
  94.3 19.3 %shard_map.117 = f32[1536,128]{1,0:T(8,128)} custom-call(bf16[1536,2176]{1,0:T(8,128)(2,1)} %bitcast.31, bf16[2048,1572]{1,0:T(8,128)(2,1)} %copy.34.w_ref, s32[1536,1]{1,0:T(8,128)} %fusion.2.id_ref), custom_call_target="tpu_custom_call" | custom-call | flops 9890168832 | bytes 13516800 | tf_op jit(solution)/shard_map/pallas_call | solution.py:212
  113.6 2.1 %copy.36 = f32[32,48,4]{1,2,0:T(4,128)} copy(f32[32,48,4]{2,1,0:T(8,128)} %bitcast.28) | data formatting | bytes 49152 | tf_op jit(solution)/shard_map/reshape | solution.py:263
  115.6 25.0 %shard_map.118 = (f32[8,48]{1,0:T(8,128)}, f32[8,8,128]{2,1,0:T(8,128)}) custom-call(f32[32,4,48]{2,1,0:T(4,128)} %bitcast.29, f32[8,128]{1,0:T(8,128)} %copy-done.1, f32[8,128]{1,0:T(8,128)} %scatter.14.refs_2_), custom_call_target="tpu_custom_call" | custom-call | tf_op jit(solution)/shard_map/pallas_call | solution.py:133
  140.7 0.8 slice_bitcast_fusion
  141.5 0.8 gather_fusion.1
  142.2 0.8 gather_fusion
  143.0 1.0 slice_reduce_fusion.1
  144.2 0.5 select_multiply_fusion
  144.7 0.7 select_reduce_fusion.1
  (30 shorter events, 0.4 us)
Async XLA Ops:
  7.2 60.6 %all-gather.3.cloned.1.call-start = ((), (), s32[]{:S(2)}) async-start(), calls=%async_computation | async-start | bytes 3551232 | tf_op jit(solution)/shard_map/all_gather | solution.py:254
  9.2 82.8 %all-gather.5.cloned.1.call-start = ((), (), s32[]{:S(2)}) async-start(), calls=%async_computation.1 | async-start | bytes 10027008 | tf_op jit(solution)/shard_map/all_gather | solution.py:255
  67.8 9.7 %copy-start.3 = (s32[64]{0:T(128)S(1)}, s32[64]{0:T(128)}, u32[]{:S(2)}) copy-start(s32[64]{0:T(128)} %param.25) | copy-start | bytes 772
  67.8 9.9 %copy-start.5 = (s32[1,8]{1,0:T(1,128)S(1)}, s32[1,8]{1,0:T(1,128)}, u32[]{:S(2)}) copy-start(s32[1,8]{1,0:T(1,128)} %param.26) | copy-start | bytes 100
  67.8 11.3 %copy-start.6 = (s32[8]{0:T(128)S(1)}, s32[8]{0:T(128)}, u32[]{:S(2)}) copy-start(s32[8]{0:T(128)} %param.27) | copy-start | bytes 100
  67.8 15.0 %copy-start.4 = (bf16[2048]{0:T(1024)(128)(2,1)S(1)}, bf16[2048]{0:T(1024)(128)(2,1)}, u32[]{:S(2)}) copy-start(bf16[2048]{0:T(1024)(128)(2,1)} %param.23) | copy-start | bytes 12292
  67.8 15.2 %copy-start = (bf16[64,2048]{1,0:T(8,128)(2,1)S(1)}, bf16[64,2048]{1,0:T(8,128)(2,1)}, u32[]{:S(2)}) copy-start(bf16[64,2048]{1,0:T(8,128)(2,1)} %hidden_ref.1) | copy-start | bytes 786436
  67.8 15.3 %copy-start.2 = (f32[2048]{0:T(1024)S(1)}, f32[2048]{0:T(1024)}, u32[]{:S(2)}) copy-start(f32[2048]{0:T(1024)} %param.21) | copy-start | bytes 24580
  82.9 30.7 %copy-start.1 = (f32[8,128]{1,0:T(8,128)}, f32[8,128]{1,0:T(8,128)S(1)}, u32[]{:S(2)}) copy-start(f32[8,128]{1,0:T(8,128)S(1)} %scatter.11.refs_1_) | copy-start | bytes 12292
Sparse Core Ops, SparseCore 0:
  10.5 57.1 all-gather.2
  69.5 22.4 all-gather.4

commit v10 on v1

v10 whole, which is shorter than its diff:
```python
import jax
import jax.numpy as jnp
from jax import lax
from jax.experimental import pallas as pl
from jax.experimental.pallas import tpu as pltpu
from jax.sharding import PartitionSpec as P

EPSILON = 1e-06
MESH = pl.DeviceIdType.MESH
LIVE = 48


def score_kernel(n_tensor, n_dp, tile, x_ref, w_ref, id_ref, member_ref, len_ref, ids_ref,
                 own_ref, routed_ref, stats_buf, held, t_held, d_held, part_msg, route_msg,
                 a_send, a_recv, t_send, t_recv, d_send, d_recv):
    step = pl.program_id(0)
    last = pl.num_programs(0) - 1
    me = lax.axis_index("tensor")
    dp = lax.axis_index("dp")
    rows = held.shape[1]

    @pl.when(step == 0)
    def _():
        barrier = pltpu.get_barrier_semaphore()
        for offset in range(1, n_tensor):
            peer = lax.rem(me + offset, n_tensor)
            pl.semaphore_signal(barrier, inc=1, device_id=(dp, peer), device_id_type=MESH)
        for offset in range(1, n_dp):
            peer = lax.rem(dp + offset, n_dp)
            pl.semaphore_signal(barrier, inc=1, device_id=(peer, me), device_id_type=MESH)
        pl.semaphore_wait(barrier, n_tensor - 1 + n_dp - 1)

    logits = jnp.dot(x_ref[...], w_ref[...], preferred_element_type=jnp.float32)
    peak = jnp.max(logits, axis=1, keepdims=True)
    shifted = logits - peak
    weights = jnp.exp(shifted)
    mass = jnp.sum(weights, axis=1, keepdims=True)
    spread = jnp.sum(weights * shifted, axis=1, keepdims=True)
    column = lax.broadcasted_iota(jnp.int32, logits.shape, 1)
    target = jnp.sum(jnp.where(column == id_ref[...], logits, 0.0), axis=1, keepdims=True)
    lane = lax.broadcasted_iota(jnp.int32, (tile, 128), 1)
    start = pl.multiple_of(step * tile, 8)
    stats_buf[pl.ds(start, tile)] = jnp.where(
        lane == 0, peak, jnp.where(lane == 1, mass, jnp.where(lane == 2, spread, target))
    )

    for b in range(tile // rows):
        peer = step * (tile // rows) + b
        source_rows = stats_buf.at[pl.ds(pl.multiple_of(peer * rows, 8), rows)]

        @pl.when(peer == me)
        def _():
            held[me] = source_rows[...]

        @pl.when(peer != me)
        def _():
            pltpu.make_async_remote_copy(
                src_ref=source_rows, dst_ref=held.at[me],
                send_sem=a_send.at[peer], recv_sem=a_recv.at[me],
                device_id=(dp, peer), device_id_type=MESH,
            ).start()

    @pl.when(step == last)
    def _():
        for offset in range(1, n_tensor):
            peer = lax.rem(me + offset, n_tensor)
            pltpu.make_async_remote_copy(
                src_ref=stats_buf.at[pl.ds(pl.multiple_of(peer * rows, 8), rows)], dst_ref=held.at[me],
                send_sem=a_send.at[peer], recv_sem=a_recv.at[me],
                device_id=(dp, peer), device_id_type=MESH,
            ).wait_send()
        for offset in range(1, n_tensor):
            source = lax.rem(me + n_tensor - offset, n_tensor)
            pltpu.make_async_remote_copy(
                src_ref=stats_buf.at[pl.ds(pl.multiple_of(me * rows, 8), rows)], dst_ref=held.at[source],
                send_sem=a_send.at[me], recv_sem=a_recv.at[source],
                device_id=(dp, source), device_id_type=MESH,
            ).wait_recv()

        top = lax.fori_loop(
            0, n_tensor, lambda p, m: jnp.maximum(m, held[p][:, 0:1]),
            jnp.full((rows, 1), -jnp.inf, jnp.float32),
        )

        def gather_sums(p, sums):
            total_mass, total_spread, total_target = sums
            block = held[p]
            gap = block[:, 0:1] - top
            factor = jnp.exp(gap)
            total_mass = total_mass + factor * block[:, 1:2]
            total_spread = total_spread + factor * (block[:, 2:3] + gap * block[:, 1:2])
            return total_mass, total_spread, total_target + block[:, 3:4]

        zero = jnp.zeros((rows, 1), jnp.float32)
        total_mass, total_spread, total_target = lax.fori_loop(
            0, n_tensor, gather_sums, (zero, zero, zero)
        )
        log_mass = jnp.log(total_mass)
        logprob = total_target - top - log_mass
        entropy = log_mass - total_spread / total_mass
        own_lane = lax.broadcasted_iota(jnp.int32, own_ref.shape, 1)
        own_ref[...] = jnp.where(own_lane == 0, logprob, jnp.where(own_lane == 1, entropy, 0.0))

        partial = jnp.sum(member_ref[...] * logprob, axis=0, keepdims=True) / len_ref[0:1, :]
        part_msg[...] = jnp.broadcast_to(partial, part_msg.shape)
        t_held[me] = part_msg[...]
        copies = []
        for offset in range(1, n_tensor):
            peer = lax.rem(me + offset, n_tensor)
            copy = pltpu.make_async_remote_copy(
                src_ref=part_msg, dst_ref=t_held.at[me],
                send_sem=t_send.at[offset], recv_sem=t_recv.at[offset],
                device_id=(dp, peer), device_id_type=MESH,
            )
            copy.start()
            copies.append(copy)
        for copy in copies:
            copy.wait_send()
        for offset in range(1, n_tensor):
            source = lax.rem(me + n_tensor - offset, n_tensor)
            pltpu.make_async_remote_copy(
                src_ref=part_msg, dst_ref=t_held.at[source],
                send_sem=t_send.at[offset], recv_sem=t_recv.at[offset],
                device_id=(dp, source), device_id_type=MESH,
            ).wait_recv()

        total = jnp.sum(t_held[...], axis=0)
        row = lax.broadcasted_iota(jnp.int32, total.shape, 0)
        route_msg[...] = jnp.where(row == 0, total, jnp.where(row == 1, ids_ref[...], 0.0))
        d_held[dp] = route_msg[...]
        copies = []
        for offset in range(1, n_dp):
            peer = lax.rem(dp + offset, n_dp)
            copy = pltpu.make_async_remote_copy(
                src_ref=route_msg, dst_ref=d_held.at[dp],
                send_sem=d_send.at[offset], recv_sem=d_recv.at[offset],
                device_id=(peer, me), device_id_type=MESH,
            )
            copy.start()
            copies.append(copy)
        for copy in copies:
            copy.wait_send()
        for offset in range(1, n_dp):
            source = lax.rem(dp + n_dp - offset, n_dp)
            pltpu.make_async_remote_copy(
                src_ref=route_msg, dst_ref=d_held.at[source],
                send_sem=d_send.at[offset], recv_sem=d_recv.at[offset],
                device_id=(source, me), device_id_type=MESH,
            ).wait_recv()
        routed_ref[...] = d_held[...]


def score(rows, weight, local_ids, member, lens, ids, width, tile, n_tensor, n_dp):
    count = rows.shape[0]
    depth, vocab = weight.shape
    full = lambda shape: pl.BlockSpec(shape, lambda i: (0,) * len(shape))
    return pl.pallas_call(
        lambda *refs: score_kernel(n_tensor, n_dp, tile, *refs),
        out_shape=(
            jax.ShapeDtypeStruct((LIVE, 128), jnp.float32),
            jax.ShapeDtypeStruct((n_dp, 8, 128), jnp.float32),
        ),
        grid=(count // tile,),
        in_specs=[
            pl.BlockSpec((tile, width), lambda i: (i, 0)),
            full((depth, vocab)),
            pl.BlockSpec((tile, 1), lambda i: (i, 0)),
            full((LIVE, 128)),
            full((8, 128)),
            full((8, 128)),
        ],
        out_specs=(full((LIVE, 128)), full((n_dp, 8, 128))),
        scratch_shapes=[
            pltpu.VMEM((count, 128), jnp.float32),
            pltpu.VMEM((n_tensor, LIVE, 128), jnp.float32),
            pltpu.VMEM((n_tensor, 8, 128), jnp.float32),
            pltpu.VMEM((n_dp, 8, 128), jnp.float32),
            pltpu.VMEM((8, 128), jnp.float32),
            pltpu.VMEM((8, 128), jnp.float32),
            pltpu.SemaphoreType.DMA((n_tensor,)),
            pltpu.SemaphoreType.DMA((n_tensor,)),
            pltpu.SemaphoreType.DMA((n_tensor,)),
            pltpu.SemaphoreType.DMA((n_tensor,)),
            pltpu.SemaphoreType.DMA((n_dp,)),
            pltpu.SemaphoreType.DMA((n_dp,)),
        ],
        compiler_params=pltpu.CompilerParams(
            collective_id=4, has_side_effects=True, vmem_limit_bytes=56 * 1024 * 1024
        ),
        cost_estimate=pl.CostEstimate(
            flops=2 * count * depth * vocab,
            transcendentals=count * vocab,
            bytes_accessed=2 * count * width + 2 * depth * vocab + 512 * count,
        ),
    )(rows, weight, local_ids, member, lens, ids)


def prep_kernel(hidden_ref, gain_ref, mask_ref, ids_ref, out_ref):
    width = hidden_ref.shape[1]
    own_rows = hidden_ref.shape[0]
    widened = hidden_ref[...].astype(jnp.float32)
    inverse_rms = lax.rsqrt(jnp.mean(widened * widened, axis=1, keepdims=True) + EPSILON)
    normed = (widened * inverse_rms * gain_ref[...]).astype(jnp.bfloat16)
    live = jnp.broadcast_to(mask_ref[...].astype(jnp.float32), (8, own_rows))
    upper = (
        lax.broadcasted_iota(jnp.int32, (own_rows, own_rows), 0)
        <= lax.broadcasted_iota(jnp.int32, (own_rows, own_rows), 1)
    ).astype(jnp.float32)
    live_sum = jnp.dot(live, upper, preferred_element_type=jnp.float32)[0:1, :]
    rank = lax.broadcasted_iota(jnp.int32, (LIVE, own_rows), 0).astype(jnp.float32)
    chosen = ((live[0:1, :] == 1.0) & (live_sum - 1.0 == rank)).astype(jnp.bfloat16)
    out_ref[:, :width] = jnp.dot(chosen, normed, preferred_element_type=jnp.float32).astype(jnp.bfloat16)
    ids = ids_ref[...]
    high = lax.shift_right_logical(ids, 8).astype(jnp.float32)
    low = jnp.bitwise_and(ids, 255).astype(jnp.float32)
    row = lax.broadcasted_iota(jnp.int32, (128, own_rows), 0)
    meta_in = jnp.where(row == 0, high, jnp.where(row == 1, low, 0.0)).astype(jnp.bfloat16)
    meta = lax.dot_general(
        chosen, meta_in, (((1,), (1,)), ((), ())), preferred_element_type=jnp.float32
    )
    out_ref[:, width:] = meta.astype(jnp.bfloat16)


def prep(hidden, norm_gain, slot_mask, token_ids):
    own_rows, width = hidden.shape
    return pl.pallas_call(
        prep_kernel,
        out_shape=jax.ShapeDtypeStruct((LIVE, width + 128), jnp.bfloat16),
        in_specs=[pl.BlockSpec(memory_space=pltpu.VMEM)] * 4,
        out_specs=pl.BlockSpec(memory_space=pltpu.VMEM),
    )(hidden, norm_gain.reshape(1, width), slot_mask.reshape(1, own_rows), token_ids.reshape(1, own_rows))


def on_device(
    hidden, norm_gain, head_weight, value_weight, token_ids, slot_mask, lengths, request_order
):
    own_rows = hidden.shape[0]
    vocab_local = head_weight.shape[1]
    n_tensor = lax.axis_size("tensor")
    n_dp = lax.axis_size("dp")
    tensor_index = lax.axis_index("tensor")
    widened = hidden.astype(jnp.float32)
    inverse_rms = lax.rsqrt(jnp.mean(widened * widened, axis=1, keepdims=True) + EPSILON)
    normed = (widened * inverse_rms * norm_gain).astype(jnp.bfloat16)
    weight_mask = slot_mask.astype(jnp.float32)
    token_value = weight_mask * jnp.dot(normed, value_weight, preferred_element_type=jnp.float32)

    width = hidden.shape[1]
    live_sum = jnp.cumsum(slot_mask)
    slot_index = jnp.arange(own_rows, dtype=jnp.int32)
    chosen = (slot_mask[None, :] == 1) & (
        live_sum[None, :] - 1 == jnp.arange(LIVE, dtype=jnp.int32)[:, None]
    )
    source = jnp.sum(jnp.where(chosen, slot_index[None, :], 0), axis=1)
    block = prep(hidden, norm_gain, slot_mask, token_ids)
    gathered = lax.all_gather(block, "tensor", axis=0, tiled=True)
    meta_cols = gathered[:, width:width + 2].astype(jnp.float32)
    piece_ids = (meta_cols[:, 0] * 256.0 + meta_cols[:, 1]).astype(jnp.int32)
    local_ids = (piece_ids - tensor_index * vocab_local)[:, None]
    request_count = lengths.shape[1]
    span_lengths = lengths[0]
    span_ends = jnp.cumsum(span_lengths)
    slot_ids = tensor_index * own_rows + source
    position = jnp.sum((slot_ids[:, None] >= span_ends[None, :]).astype(jnp.int32), axis=1)
    live = jnp.arange(LIVE, dtype=jnp.int32) < live_sum[-1]
    member = (position[:, None] == jnp.arange(128, dtype=jnp.int32)[None, :]) & live[:, None]
    lens = jnp.ones((8, 128), jnp.float32).at[0, :request_count].set(span_lengths.astype(jnp.float32))
    ids_tile = jnp.zeros((8, 128), jnp.float32).at[1, :request_count].set(request_order.astype(jnp.float32))
    row_count = gathered.shape[0]
    tile = 4 * LIVE if row_count % (4 * LIVE) == 0 else row_count
    own, routed = score(
        gathered, head_weight, local_ids, member.astype(jnp.float32), lens, ids_tile,
        width, tile, n_tensor, n_dp,
    )
    place = jnp.clip(live_sum - 1, 0, LIVE - 1)
    token_logprob = weight_mask * jnp.take(own[:, 0], place)
    token_entropy = weight_mask * jnp.take(own[:, 1], place)
    all_totals = routed[:, 0, :request_count].reshape(-1)
    all_owners = routed[:, 1, :request_count].reshape(-1)
    wanted = (lax.axis_index("dp") * request_count + jnp.arange(request_count)).astype(jnp.float32)
    route_table = all_owners[:, None] == wanted[None, :]
    request_score = jnp.sum(jnp.where(route_table, all_totals[:, None], 0.0), axis=0)
    return (token_logprob, token_entropy, token_value, request_score)


def solution(mesh):
    return jax.shard_map(
        on_device,
        mesh=mesh,
        in_specs=(
            P(("dp", "tensor"), None),
            P(),
            P(None, "tensor"),
            P(),
            P(("dp", "tensor")),
            P(("dp", "tensor")),
            P("dp", None),
            P("dp"),
        ),
        out_specs=(P(("dp", "tensor")), P(("dp", "tensor")), P(("dp", "tensor")), P("dp")),
        check_vma=False,
    )
```

time: 174 us -> 138 us (0.79); the launches traced: 171 us -> 137 us
  Pallas kernels: 0 us -> 55.7 us
  blocking collectives: 39.6 us -> 0 us
  waiting for transfers between devices: 81.3 us -> 44.1 us
  matrix products: 19.1 us -> 0.77 us
  local copies, waits for them, and re-layouts: 1.62 us -> 15.6 us
  other arithmetic: 14.8 us -> 6.91 us
    pallas_call x0 -> x2, Pallas kernels: none -> 55.7 us  [the longest x1 53.7 us: score(): pl.pallas_call(lambda *refs: score_kernel(n_tensor, n_dp, tile, *refs), o...]
    all_gather x2 -> x1, waiting for transfers between devices: 81.3 us -> 44.1 us  [on_device(): gathered = lax.all_gather(block, 'tensor', axis=0, tiled=True)]
    all_gather x1 -> x0, blocking collectives: 25.8 us -> none  [on_device(): lax.all_gather(jnp.stack([token_ids, slot_mask]), 'tensor', axis=1, tiled...]
    dot_general x1 -> x0, matrix products: 18.4 us -> none  [on_device(): jnp.dot(piece_rows, head_weight, preferred_element_type=jnp.float32)]
    unnamed x1 -> x0, blocking collectives: 13.8 us -> none
    unnamed x16 -> x12, local copies, waits for them, and re-layouts: 0.72 us -> 9.6 us
    reduce_sum x3 -> x1, other arithmetic: 5.17 us -> 0.11 us  [on_device(): source = jnp.sum(jnp.where(chosen, slot_index[None, :], 0), axis=1)]
    slice x2 -> x0, other arithmetic: 3.65 us -> none  [the longest x1 3.63 us: on_device(): parts[:, 0]]
  transfers between devices with their start and end apart: 2 -> 1, of which waited for: 2 -> 1; matrix products, arithmetic and copies ran while one was open for 1% -> 12% of each run, Pallas kernels for 0% -> 0%
where the time goes in v10:
time: 138 us; the launch traced here: 137 us
  Pallas kernels  55.7 us (40%)
  waiting for transfers between devices  44.1 us (32%)
  local copies, waits for them, and re-layouts  15.6 us (11%)
  between operations  14.1 us (10%)
  other arithmetic  6.91 us (5%)
    pallas_call x1, Pallas kernels, score(): pl.pallas_call(lambda *refs: score_kernel(n_tensor, n_dp, tile, *refs), o...  53.7 us
    all_gather x1, waiting for transfers between devices, on_device(): gathered = lax.all_gather(block, 'tensor', axis=0, tiled=True)  44.1 us
    unnamed x12, local copies, waits for them, and re-layouts  9.6 us
  transfers between devices with their start and end apart: 1, of which 1 were waited for; matrix products, arithmetic and copies ran while one was open for 12% of the time, Pallas kernels for 0%

profile of v10, /device:TPU:1, one launch (start us, length us, event | category | flops | bytes accessed | tf_op | source)
XLA Modules:
  0.0 137.2 jit_solution(5554611982033421541)
XLA Ops:
  7.2 0.0 all-gather.2.cloned.1.call-start
  7.2 2.0 %shard_map.111 = bf16[48,2176]{1,0:T(8,128)(2,1)} custom-call(bf16[64,2048]{1,0:T(8,128)(2,1)} %hidden_ref.1, f32[1,2048]{1,0:T(1,128)} %bitcast.14, s32[1,64]{1,0:T(1,128)} %bitcast.15, s32[1,64]{1,0:T(1,128)} %bitcast.17), custom_call_target="tpu_custom_call" | custom-call | tf_op jit(solution)/shard_map/pallas_call | solution.py:226
  9.2 0.0 all-gather.2.cloned.1.call-update
  9.3 0.7 copy.18
  10.0 0.7 convert_element_type.41
  10.7 0.1 reduce-window.13
  10.8 0.0 copy-start
  10.8 0.9 reduce-window.14
  11.7 0.5 slice.74
  12.2 9.6 %copy.20.refs_1_ = bf16[2048,1572]{1,0:T(8,128)(2,1)} copy(bf16[2048,1572]{0,1:T(8,128)(2,1)} %param.16) | data formatting | bytes 12877824 | tf_op args[2]
  21.8 0.6 scatter.6.refs_4_
  22.4 0.6 scatter.9.refs_5_
  23.0 0.6 iota_compare_fusion.2
  23.6 0.1 add_reduce_fusion
  23.8 0.0 copy-done.2
  23.8 0.1 select_reduce_fusion
  23.9 0.1 convert_reduce_fusion
  24.0 0.2 fusion.3
  24.2 0.7 fusion.11.refs_3_
  24.9 0.8 fusion
  25.6 44.1 %all-gather.2.cloned.1.call-done.refs_0_ = bf16[1536,2176]{1,0:T(8,128)(2,1)} async-done(((bf16[48,2176]{1,0:T(8,128)(2,1)}), bf16[1536,2176]{1,0:T(8,128)(2,1)}) %all-gather.2.cloned.1.call-update) | async-done | bytes 6684688 | tf_op jit(solution)/shard_map/all_gather | solution.py:256
  69.7 1.0 slice_convert_fusion
  70.8 1.2 fusion.2.refs_2_
  71.9 53.7 %shard_map.112 = (f32[48,128]{1,0:T(8,128)}, f32[8,8,128]{2,1,0:T(8,128)}) custom-call(bf16[1536,2176]{1,0:T(8,128)(2,1)} %all-gather.2.cloned.1.call-done.refs_0_, bf16[2048,1572]{1,0:T(8,128)(2,1)} %copy.20.refs_1_, s32[1536,1]{1,0:T(8,128)} %fusion.2.refs_2_, f32[48,128]{1,0:T(8,128)} %fusion.11.refs_3_, f32[8,128]{1,0:T(8,128)} %scatter.6.refs_4_, ...), custom_call_target="tpu_custom_call" | custom-call | flops 9890168832 | bytes 13516800 | tf_op jit(solution)/shard_map/pallas_call | solution.py:157
  125.6 1.0 slice_reduce_fusion
  126.6 0.8 gather_fusion
  127.4 0.8 gather_fusion.1
  128.1 0.9 slice_reduce_fusion.3
  129.0 0.1 broadcast_in_dim.30
  129.1 0.1 eq.52
  129.2 0.5 select_multiply_fusion
  129.7 0.7 select_reduce_fusion.1
  (16 shorter events, 0.1 us)
Async XLA Ops:
  7.2 62.5 %all-gather.2.cloned.1.call-start = ((), (), s32[]{:S(2)}) async-start(), calls=%async_computation | async-start | bytes 6893568 | tf_op jit(solution)/shard_map/all_gather | solution.py:256
  10.0 11.8 %copy-start.3 = (bf16[2048]{0:T(1024)(128)(2,1)S(1)}, bf16[2048]{0:T(1024)(128)(2,1)}, u32[]{:S(2)}) copy-start(bf16[2048]{0:T(1024)(128)(2,1)} %param.17) | copy-start | bytes 12292
  10.7 11.7 %copy-start.4 = (s32[8]{0:T(128)S(1)}, s32[8]{0:T(128)}, u32[]{:S(2)}) copy-start(s32[8]{0:T(128)} %param.21) | copy-start | bytes 100
  10.8 13.0 %copy-start.2 = (s32[64]{0:T(128)S(1)}, s32[64]{0:T(128)}, u32[]{:S(2)}) copy-start(s32[64]{0:T(128)} %param.19) | copy-start | bytes 772
  10.8 13.2 %copy-start = (bf16[64,2048]{1,0:T(8,128)(2,1)S(1)}, bf16[64,2048]{1,0:T(8,128)(2,1)}, u32[]{:S(2)}) copy-start(bf16[64,2048]{1,0:T(8,128)(2,1)} %hidden_ref.1) | copy-start | bytes 786436
  12.2 12.7 %copy-start.1 = (f32[2048]{0:T(1024)S(1)}, f32[2048]{0:T(1024)}, u32[]{:S(2)}) copy-start(f32[2048]{0:T(1024)} %param.15) | copy-start | bytes 24580
Sparse Core Ops, SparseCore 0:
  10.6 59.0 all-gather.1

commit v11 on v8

--- a/solution.py
+++ b/solution.py
@@ -324,22 +324,25 @@
     )(hidden, norm_gain.reshape(1, width), slot_mask.reshape(1, own_rows), token_ids.reshape(1, own_rows))
 
 
-def stats_kernel(x_ref, w_ref, id_ref, out_ref):
-    logits = jnp.dot(x_ref[...], w_ref[...], preferred_element_type=jnp.float32)
+def stats_kernel(x_ref, w_ref, out_ref):
+    depth, vocab = w_ref.shape
+    logits = jnp.dot(x_ref[:, :depth], w_ref[...], preferred_element_type=jnp.float32)
+    meta = x_ref[:, depth:depth + 128].astype(jnp.float32)
+    token = (meta[:, 0:1] * 256.0 + meta[:, 1:2]).astype(jnp.int32) - lax.axis_index("tensor") * vocab
     peak = jnp.max(logits, axis=1, keepdims=True)
     shifted = logits - peak
     weights = jnp.exp(shifted)
     mass = jnp.sum(weights, axis=1, keepdims=True)
     spread = jnp.sum(weights * shifted, axis=1, keepdims=True)
     column = lax.broadcasted_iota(jnp.int32, logits.shape, 1)
-    target = jnp.sum(jnp.where(column == id_ref[...], logits, 0.0), axis=1, keepdims=True)
+    target = jnp.sum(jnp.where(column == token, logits, 0.0), axis=1, keepdims=True)
     lane = lax.broadcasted_iota(jnp.int32, out_ref.shape, 1)
     out_ref[...] = jnp.where(
         lane == 0, peak, jnp.where(lane == 1, mass, jnp.where(lane == 2, spread, target))
     )
 
 
-def row_stats(rows, weight, local_ids, width, tile):
+def row_stats(rows, weight, tile):
     count = rows.shape[0]
     depth, vocab = weight.shape
     return pl.pallas_call(
@@ -347,18 +350,17 @@
         out_shape=jax.ShapeDtypeStruct((count, 128), jnp.float32),
         grid=(count // tile,),
         in_specs=[
-            pl.BlockSpec((tile, width), lambda i: (i, 0)),
+            pl.BlockSpec((tile, rows.shape[1]), lambda i: (i, 0)),
             pl.BlockSpec((depth, vocab), lambda i: (0, 0)),
-            pl.BlockSpec((tile, 1), lambda i: (i, 0)),
         ],
         out_specs=pl.BlockSpec((tile, 128), lambda i: (i, 0)),
         compiler_params=pltpu.CompilerParams(vmem_limit_bytes=56 * 1024 * 1024),
         cost_estimate=pl.CostEstimate(
             flops=2 * count * depth * vocab,
             transcendentals=count * vocab,
-            bytes_accessed=2 * count * width + 2 * depth * vocab + 512 * count,
+            bytes_accessed=2 * count * rows.shape[1] + 2 * depth * vocab + 512 * count,
         ),
-    )(rows, weight, local_ids)
+    )(rows, weight)
 
 
 def on_device(
@@ -384,11 +386,8 @@
     source = jnp.sum(jnp.where(chosen, slot_index[None, :], 0), axis=1)
     block = prep(hidden, norm_gain, slot_mask, token_ids)
     gathered = lax.all_gather(block, "tensor", axis=0, tiled=True)
-    meta_cols = gathered[:, width:width + 2].astype(jnp.float32)
-    piece_ids = (meta_cols[:, 0] * 256.0 + meta_cols[:, 1]).astype(jnp.int32)
-    local_ids = (piece_ids - tensor_index * vocab_local)[:, None]
     row_count = gathered.shape[0]
-    stats = row_stats(gathered, head_weight, local_ids, width, 256 if row_count % 256 == 0 else row_count)
+    stats = row_stats(gathered, head_weight, 256 if row_count % 256 == 0 else row_count)
     blocks = stats[:, :4].reshape(n_tensor, LIVE, 4).transpose(0, 2, 1)
     request_count = lengths.shape[1]
     span_lengths = lengths[0]

time: 128 us -> 126 us (0.984)
  other arithmetic: 7.46 us -> 5.22 us
  transfers between devices with their start and end apart: 1 -> 1, of which waited for: 1 -> 1; matrix products, arithmetic and copies ran while one was open for 12% -> 13% of each run, Pallas kernels for 0% -> 0%
where the time goes in v11:
time: 126 us; the launch traced here: 125 us
  waiting for transfers between devices  44.3 us (35%)
  Pallas kernels  44.2 us (35%)
  local copies, waits for them, and re-layouts  16.7 us (13%)
  between operations  14.2 us (11%)
  other arithmetic  5.22 us (4%)
    all_gather x1, waiting for transfers between devices, on_device(): gathered = lax.all_gather(block, 'tensor', axis=0, tiled=True)  44.3 us
    pallas_call x1, Pallas kernels, finish(): pl.pallas_call(lambda *refs: finish_kernel(n_tensor, n_dp, *refs), out_sh...  22.9 us
    pallas_call x1, Pallas kernels, row_stats(): pl.pallas_call(stats_kernel, out_shape=jax.ShapeDtypeStruct((count, 128),...  19.3 us
    unnamed x16, local copies, waits for them, and re-layouts  9.66 us
    another operation x7, other arithmetic  2.86 us
  transfers between devices with their start and end apart: 1, of which 1 were waited for; matrix products, arithmetic and copies ran while one was open for 13% of the time, Pallas kernels for 0%

profile of v11, /device:TPU:1, one launch (start us, length us, event | category | flops | bytes accessed | tf_op | source)
XLA Modules:
  0.0 125.5 jit_solution(5706205905664035050)
XLA Ops:
  7.2 2.0 %shard_map.116 = bf16[48,2176]{1,0:T(8,128)(2,1)} custom-call(bf16[64,2048]{1,0:T(8,128)(2,1)} %hidden_ref.1, f32[1,2048]{1,0:T(1,128)} %bitcast.25, s32[1,64]{1,0:T(1,128)} %bitcast.26, s32[1,64]{1,0:T(1,128)} %bitcast.28), custom_call_target="tpu_custom_call" | custom-call | tf_op jit(solution)/shard_map/pallas_call | solution.py:319
  9.3 9.6 %copy.23.w_ref = bf16[2048,1572]{1,0:T(8,128)(2,1)} copy(bf16[2048,1572]{0,1:T(8,128)(2,1)} %param.22) | data formatting | bytes 12877824 | tf_op args[2]
  18.9 0.1 copy.22
  19.0 0.1 reduce-window.13
  19.1 0.2 reduce-window.14
  19.3 0.5 slice.84
  19.8 0.1 copy.26
  19.9 0.6 compare_reduce_fusion
  20.6 0.6 fusion.9
  21.2 0.1 copy.27
  21.3 0.6 compare_reduce_fusion.1
  21.9 0.6 iota_compare_fusion.2
  22.6 0.1 add_reduce_fusion
  22.7 0.1 select_reduce_fusion
  22.8 0.1 convert_reduce_fusion
  22.9 0.7 convert_select_fusion
  23.6 0.7 scatter.14.refs_2_
  24.3 0.1 scatter.11.refs_1_
  24.5 0.2 fusion.1
  24.6 0.8 fusion
  25.4 44.3 %all-gather.2.cloned.1.call-done.x_ref = bf16[1536,2176]{1,0:T(8,128)(2,1)} async-done(((bf16[48,2176]{1,0:T(8,128)(2,1)}), bf16[1536,2176]{1,0:T(8,128)(2,1)}) %all-gather.2.cloned.1.call-update) | async-done | bytes 6684688 | tf_op jit(solution)/shard_map/all_gather | solution.py:388
  69.7 19.3 %shard_map.117 = f32[1536,128]{1,0:T(8,128)} custom-call(bf16[1536,2176]{1,0:T(8,128)(2,1)} %all-gather.2.cloned.1.call-done.x_ref, bf16[2048,1572]{1,0:T(8,128)(2,1)} %copy.23.w_ref), custom_call_target="tpu_custom_call" | custom-call | flops 9890168832 | bytes 13910016 | tf_op jit(solution)/shard_map/pallas_call | solution.py:348
  89.0 2.1 %copy.25 = f32[32,48,4]{1,2,0:T(4,128)} copy(f32[32,48,4]{2,1,0:T(8,128)} %bitcast.23) | data formatting | bytes 49152 | tf_op jit(solution)/shard_map/reshape | solution.py:391
  91.1 22.9 %shard_map.118 = (f32[8,48]{1,0:T(8,128)}, f32[8,8,128]{2,1,0:T(8,128)}) custom-call(f32[32,4,48]{2,1,0:T(4,128)} %bitcast.24, f32[8,128]{1,0:T(8,128)} %copy-done.1, f32[8,128]{1,0:T(8,128)} %scatter.14.refs_2_), custom_call_target="tpu_custom_call" | custom-call | tf_op jit(solution)/shard_map/pallas_call | solution.py:266
  114.0 0.8 slice_bitcast_fusion
  114.7 0.8 gather_fusion.1
  115.5 0.8 gather_fusion
  116.3 1.0 slice_reduce_fusion.1
  117.3 0.1 broadcast_in_dim.46
  117.3 0.1 eq.52
  117.4 0.5 select_multiply_fusion
  118.0 0.7 select_reduce_fusion.1
  (25 shorter events, 0.1 us)
Async XLA Ops:
  7.2 62.5 %all-gather.2.cloned.1.call-start = ((), (), s32[]{:S(2)}) async-start(), calls=%async_computation | async-start | bytes 6893568 | tf_op jit(solution)/shard_map/all_gather | solution.py:388
  9.3 9.7 %copy-start.3 = (s32[64]{0:T(128)S(1)}, s32[64]{0:T(128)}, u32[]{:S(2)}) copy-start(s32[64]{0:T(128)} %param.25) | copy-start | bytes 772
  9.3 9.9 %copy-start.5 = (s32[1,8]{1,0:T(1,128)S(1)}, s32[1,8]{1,0:T(1,128)}, u32[]{:S(2)}) copy-start(s32[1,8]{1,0:T(1,128)} %param.26) | copy-start | bytes 100
  9.3 11.3 %copy-start.6 = (s32[8]{0:T(128)S(1)}, s32[8]{0:T(128)}, u32[]{:S(2)}) copy-start(s32[8]{0:T(128)} %param.27) | copy-start | bytes 100
  9.3 15.0 %copy-start.4 = (bf16[2048]{0:T(1024)(128)(2,1)S(1)}, bf16[2048]{0:T(1024)(128)(2,1)}, u32[]{:S(2)}) copy-start(bf16[2048]{0:T(1024)(128)(2,1)} %param.23) | copy-start | bytes 12292
  9.3 15.1 %copy-start = (bf16[64,2048]{1,0:T(8,128)(2,1)S(1)}, bf16[64,2048]{1,0:T(8,128)(2,1)}, u32[]{:S(2)}) copy-start(bf16[64,2048]{1,0:T(8,128)(2,1)} %hidden_ref.1) | copy-start | bytes 786436
  9.3 15.3 %copy-start.2 = (f32[2048]{0:T(1024)S(1)}, f32[2048]{0:T(1024)}, u32[]{:S(2)}) copy-start(f32[2048]{0:T(1024)} %param.21) | copy-start | bytes 24580
  24.4 64.6 %copy-start.1 = (f32[8,128]{1,0:T(8,128)}, f32[8,128]{1,0:T(8,128)S(1)}, u32[]{:S(2)}) copy-start(f32[8,128]{1,0:T(8,128)S(1)} %scatter.11.refs_1_) | copy-start | bytes 12292
Sparse Core Ops, SparseCore 0:
  10.6 59.0 all-gather.1

commit v12 on v11

--- a/solution.py
+++ b/solution.py
@@ -387,7 +387,7 @@
     block = prep(hidden, norm_gain, slot_mask, token_ids)
     gathered = lax.all_gather(block, "tensor", axis=0, tiled=True)
     row_count = gathered.shape[0]
-    stats = row_stats(gathered, head_weight, 256 if row_count % 256 == 0 else row_count)
+    stats = row_stats(gathered, head_weight, 512 if row_count % 512 == 0 else row_count)
     blocks = stats[:, :4].reshape(n_tensor, LIVE, 4).transpose(0, 2, 1)
     request_count = lengths.shape[1]
     span_lengths = lengths[0]

time: 126 us -> 126 us (level)
  no operation moved by 1% of the time
where the time goes in v12:
time: 126 us; the launch traced here: 125 us
  waiting for transfers between devices  44.3 us (35%)
  Pallas kernels  43.9 us (35%)
  local copies, waits for them, and re-layouts  16.7 us (13%)
  between operations  14.2 us (11%)
  other arithmetic  5.22 us (4%)
    all_gather x1, waiting for transfers between devices, on_device(): gathered = lax.all_gather(block, 'tensor', axis=0, tiled=True)  44.3 us
    pallas_call x1, Pallas kernels, finish(): pl.pallas_call(lambda *refs: finish_kernel(n_tensor, n_dp, *refs), out_sh...  22.9 us
    pallas_call x1, Pallas kernels, row_stats(): pl.pallas_call(stats_kernel, out_shape=jax.ShapeDtypeStruct((count, 128),...  19 us
    unnamed x16, local copies, waits for them, and re-layouts  9.66 us
    another operation x7, other arithmetic  2.86 us
  transfers between devices with their start and end apart: 1, of which 1 were waited for; matrix products, arithmetic and copies ran while one was open for 13% of the time, Pallas kernels for 0%

profile of v12, /device:TPU:1, one launch (start us, length us, event | category | flops | bytes accessed | tf_op | source)
XLA Modules:
  0.0 125.2 jit_solution(7109136816488833589)
XLA Ops:
  7.2 2.0 %shard_map.116 = bf16[48,2176]{1,0:T(8,128)(2,1)} custom-call(bf16[64,2048]{1,0:T(8,128)(2,1)} %hidden_ref.1, f32[1,2048]{1,0:T(1,128)} %bitcast.25, s32[1,64]{1,0:T(1,128)} %bitcast.26, s32[1,64]{1,0:T(1,128)} %bitcast.28), custom_call_target="tpu_custom_call" | custom-call | tf_op jit(solution)/shard_map/pallas_call | solution.py:319
  9.3 9.6 %copy.23.w_ref = bf16[2048,1572]{1,0:T(8,128)(2,1)} copy(bf16[2048,1572]{0,1:T(8,128)(2,1)} %param.22) | data formatting | bytes 12877824 | tf_op args[2]
  18.9 0.1 copy.22
  19.0 0.1 reduce-window.13
  19.1 0.2 reduce-window.14
  19.3 0.5 slice.84
  19.8 0.1 copy.26
  19.9 0.6 compare_reduce_fusion
  20.6 0.6 fusion.9
  21.2 0.1 copy.27
  21.3 0.6 compare_reduce_fusion.1
  21.9 0.6 iota_compare_fusion.2
  22.6 0.1 add_reduce_fusion
  22.7 0.1 select_reduce_fusion
  22.8 0.1 convert_reduce_fusion
  22.9 0.7 convert_select_fusion
  23.6 0.7 scatter.14.refs_2_
  24.3 0.1 scatter.11.refs_1_
  24.5 0.2 fusion.1
  24.6 0.8 fusion
  25.4 44.3 %all-gather.2.cloned.1.call-done.x_ref = bf16[1536,2176]{1,0:T(8,128)(2,1)} async-done(((bf16[48,2176]{1,0:T(8,128)(2,1)}), bf16[1536,2176]{1,0:T(8,128)(2,1)}) %all-gather.2.cloned.1.call-update) | async-done | bytes 6684688 | tf_op jit(solution)/shard_map/all_gather | solution.py:388
  69.7 19.0 %shard_map.117 = f32[1536,128]{1,0:T(8,128)} custom-call(bf16[1536,2176]{1,0:T(8,128)(2,1)} %all-gather.2.cloned.1.call-done.x_ref, bf16[2048,1572]{1,0:T(8,128)(2,1)} %copy.23.w_ref), custom_call_target="tpu_custom_call" | custom-call | flops 9890168832 | bytes 13910016 | tf_op jit(solution)/shard_map/pallas_call | solution.py:348
  88.7 2.1 %copy.25 = f32[32,48,4]{1,2,0:T(4,128)} copy(f32[32,48,4]{2,1,0:T(8,128)} %bitcast.23) | data formatting | bytes 49152 | tf_op jit(solution)/shard_map/reshape | solution.py:391
  90.8 22.9 %shard_map.118 = (f32[8,48]{1,0:T(8,128)}, f32[8,8,128]{2,1,0:T(8,128)}) custom-call(f32[32,4,48]{2,1,0:T(4,128)} %bitcast.24, f32[8,128]{1,0:T(8,128)} %copy-done.1, f32[8,128]{1,0:T(8,128)} %scatter.14.refs_2_), custom_call_target="tpu_custom_call" | custom-call | tf_op jit(solution)/shard_map/pallas_call | solution.py:266
  113.6 0.8 slice_bitcast_fusion
  114.4 0.8 gather_fusion.1
  115.2 0.8 gather_fusion
  116.0 1.0 slice_reduce_fusion.1
  117.0 0.1 broadcast_in_dim.46
  117.0 0.1 eq.52
  117.1 0.5 select_multiply_fusion
  117.6 0.7 select_reduce_fusion.1
  (25 shorter events, 0.1 us)
Async XLA Ops:
  7.2 62.5 %all-gather.2.cloned.1.call-start = ((), (), s32[]{:S(2)}) async-start(), calls=%async_computation | async-start | bytes 6893568 | tf_op jit(solution)/shard_map/all_gather | solution.py:388
  9.3 9.7 %copy-start.3 = (s32[64]{0:T(128)S(1)}, s32[64]{0:T(128)}, u32[]{:S(2)}) copy-start(s32[64]{0:T(128)} %param.25) | copy-start | bytes 772
  9.3 9.9 %copy-start.5 = (s32[1,8]{1,0:T(1,128)S(1)}, s32[1,8]{1,0:T(1,128)}, u32[]{:S(2)}) copy-start(s32[1,8]{1,0:T(1,128)} %param.26) | copy-start | bytes 100
  9.3 11.3 %copy-start.6 = (s32[8]{0:T(128)S(1)}, s32[8]{0:T(128)}, u32[]{:S(2)}) copy-start(s32[8]{0:T(128)} %param.27) | copy-start | bytes 100
  9.3 15.0 %copy-start.4 = (bf16[2048]{0:T(1024)(128)(2,1)S(1)}, bf16[2048]{0:T(1024)(128)(2,1)}, u32[]{:S(2)}) copy-start(bf16[2048]{0:T(1024)(128)(2,1)} %param.23) | copy-start | bytes 12292
  9.3 15.1 %copy-start = (bf16[64,2048]{1,0:T(8,128)(2,1)S(1)}, bf16[64,2048]{1,0:T(8,128)(2,1)}, u32[]{:S(2)}) copy-start(bf16[64,2048]{1,0:T(8,128)(2,1)} %hidden_ref.1) | copy-start | bytes 786436
  9.3 15.3 %copy-start.2 = (f32[2048]{0:T(1024)S(1)}, f32[2048]{0:T(1024)}, u32[]{:S(2)}) copy-start(f32[2048]{0:T(1024)} %param.21) | copy-start | bytes 24580
  24.4 64.3 %copy-start.1 = (f32[8,128]{1,0:T(8,128)}, f32[8,128]{1,0:T(8,128)S(1)}, u32[]{:S(2)}) copy-start(f32[8,128]{1,0:T(8,128)S(1)} %scatter.11.refs_1_) | copy-start | bytes 12292
Sparse Core Ops, SparseCore 0:
  10.6 59.0 all-gather.1

commit v13 on v9

--- a/solution.py
+++ b/solution.py
@@ -3,34 +3,25 @@
 from jax import lax
 from jax.experimental import pallas as pl
 from jax.experimental.pallas import tpu as pltpu
-from jax.sharding import Mesh, PartitionSpec as P
+from jax.sharding import PartitionSpec as P
 
 EPSILON = 1e-06
 MESH = pl.DeviceIdType.MESH
 LIVE = 48
 
 
-def tensor_place(t, shape):
-    return (t // (shape[1] * shape[2]), (t // shape[2]) % shape[1], t % shape[2])
-
-
-def tensor_position(shape):
-    return (lax.axis_index("x") * shape[1] + lax.axis_index("y")) * shape[2] + lax.axis_index("core")
-
-
-def finish_kernel(n_tensor, n_dp, shape, send_ref, span_ref, ids_ref, own_ref, routed_ref,
+def finish_kernel(n_tensor, n_dp, send_ref, span_ref, ids_ref, spread_ref, logprob_ref, entropy_ref, score_ref,
                   held, t_held, d_held, part_msg, route_msg,
                   a_send, a_recv, t_send, t_recv, d_send, d_recv):
-    me = tensor_position(shape)
-    mine = (lax.axis_index("x"), lax.axis_index("y"), lax.axis_index("core"))
+    me = lax.axis_index("tensor")
     dp = lax.axis_index("dp")
     barrier = pltpu.get_barrier_semaphore()
     for offset in range(1, n_tensor):
         peer = lax.rem(me + offset, n_tensor)
-        pl.semaphore_signal(barrier, inc=1, device_id=(dp,) + tensor_place(peer, shape), device_id_type=MESH)
+        pl.semaphore_signal(barrier, inc=1, device_id=(dp, peer), device_id_type=MESH)
     for offset in range(1, n_dp):
         peer = lax.rem(dp + offset, n_dp)
-        pl.semaphore_signal(barrier, inc=1, device_id=(peer,) + mine, device_id_type=MESH)
+        pl.semaphore_signal(barrier, inc=1, device_id=(peer, me), device_id_type=MESH)
     pl.semaphore_wait(barrier, n_tensor - 1 + n_dp - 1)
 
     held[me] = send_ref[me]
@@ -40,7 +31,7 @@
         copy = pltpu.make_async_remote_copy(
             src_ref=send_ref.at[peer], dst_ref=held.at[me],
             send_sem=a_send.at[offset], recv_sem=a_recv.at[offset],
-            device_id=(dp,) + tensor_place(peer, shape), device_id_type=MESH,
+            device_id=(dp, peer), device_id_type=MESH,
         )
         copy.start()
         copies.append(copy)
@@ -51,7 +42,7 @@
         pltpu.make_async_remote_copy(
             src_ref=send_ref.at[source], dst_ref=held.at[source],
             send_sem=a_send.at[offset], recv_sem=a_recv.at[offset],
-            device_id=(dp,) + tensor_place(source, shape), device_id_type=MESH,
+            device_id=(dp, source), device_id_type=MESH,
         ).wait_recv()
 
     lanes = held.shape[2]
@@ -74,8 +65,15 @@
     log_mass = jnp.log(mass)
     logprob = target - peak - log_mass
     entropy = log_mass - spread / mass
-    row = lax.broadcasted_iota(jnp.int32, own_ref.shape, 0)
-    own_ref[...] = jnp.where(row == 0, logprob, jnp.where(row == 1, entropy, 0.0))
+    slots = spread_ref.shape[0]
+    placed = spread_ref[...] > 0.0
+    same = (
+        lax.broadcasted_iota(jnp.int32, (slots, slots), 0)
+        == lax.broadcasted_iota(jnp.int32, (slots, slots), 1)
+    )
+    for value, out in ((logprob, logprob_ref), (entropy, entropy_ref)):
+        column = jnp.sum(jnp.where(placed, value, 0.0), axis=1, keepdims=True)
+        out[...] = jnp.sum(jnp.where(same, column, 0.0), axis=0, keepdims=True)
 
     spans = span_ref[...]
     partial = jnp.sum(spans[:, :lanes] * logprob, axis=1, keepdims=True) / spans[:, 127:128]
@@ -87,7 +85,7 @@
         copy = pltpu.make_async_remote_copy(
             src_ref=part_msg, dst_ref=t_held.at[me],
             send_sem=t_send.at[offset], recv_sem=t_recv.at[offset],
-            device_id=(dp,) + tensor_place(peer, shape), device_id_type=MESH,
+            device_id=(dp, peer), device_id_type=MESH,
         )
         copy.start()
         copies.append(copy)
@@ -98,7 +96,7 @@
         pltpu.make_async_remote_copy(
             src_ref=part_msg, dst_ref=t_held.at[source],
             send_sem=t_send.at[offset], recv_sem=t_recv.at[offset],
-            device_id=(dp,) + tensor_place(source, shape), device_id_type=MESH,
+            device_id=(dp, source), device_id_type=MESH,
         ).wait_recv()
 
     total = jnp.sum(t_held[...], axis=0)
@@ -111,7 +109,7 @@
         copy = pltpu.make_async_remote_copy(
             src_ref=route_msg, dst_ref=d_held.at[dp],
             send_sem=d_send.at[offset], recv_sem=d_recv.at[offset],
-            device_id=(peer,) + mine, device_id_type=MESH,
+            device_id=(peer, me), device_id_type=MESH,
         )
         copy.start()
         copies.append(copy)
@@ -122,22 +120,30 @@
         pltpu.make_async_remote_copy(
             src_ref=route_msg, dst_ref=d_held.at[source],
             send_sem=d_send.at[offset], recv_sem=d_recv.at[offset],
-            device_id=(source,) + mine, device_id_type=MESH,
+            device_id=(source, me), device_id_type=MESH,
         ).wait_recv()
-    routed_ref[...] = d_held[...]
-
-
-def finish(blocks, spans, ids, n_tensor, n_dp, shape):
+    count = score_ref.shape[1]
+    wanted = (dp * count + lax.broadcasted_iota(jnp.int32, (1, count), 1)).astype(jnp.float32)
+    score = jnp.zeros((1, count), jnp.float32)
+    for group in range(n_dp):
+        block = d_held[group]
+        hit = block[:count, 1:2] == wanted
+        score = score + jnp.sum(jnp.where(hit, block[:count, 0:1], 0.0), axis=0, keepdims=True)
+    score_ref[...] = score
+
+
+def finish(blocks, spans, ids, spread, n_tensor, n_dp, count):
     tile = spans.shape
     lanes = blocks.shape[2]
     return pl.pallas_call(
-        lambda *refs: finish_kernel(n_tensor, n_dp, shape, *refs),
+        lambda *refs: finish_kernel(n_tensor, n_dp, *refs),
         out_shape=(
-            jax.ShapeDtypeStruct((8, lanes), jnp.float32),
-            jax.ShapeDtypeStruct((n_dp,) + tile, jnp.float32),
+            jax.ShapeDtypeStruct((1, spread.shape[0]), jnp.float32),
+            jax.ShapeDtypeStruct((1, spread.shape[0]), jnp.float32),
+            jax.ShapeDtypeStruct((1, count), jnp.float32),
         ),
-        in_specs=[pl.BlockSpec(memory_space=pltpu.VMEM)] * 3,
-        out_specs=(pl.BlockSpec(memory_space=pltpu.VMEM), pl.BlockSpec(memory_space=pltpu.VMEM)),
+        in_specs=[pl.BlockSpec(memory_space=pltpu.VMEM)] * 4,
+        out_specs=(pl.BlockSpec(memory_space=pltpu.VMEM),) * 3,
         scratch_shapes=[
             pltpu.VMEM(blocks.shape, jnp.float32),
             pltpu.VMEM((n_tensor,) + tile, jnp.float32),
@@ -152,7 +158,7 @@
             pltpu.SemaphoreType.DMA((n_dp,)),
         ],
         compiler_params=pltpu.CompilerParams(collective_id=3, has_side_effects=True),
-    )(blocks, spans, ids)
+    )(blocks, spans, ids, spread)
 
 
 def prep_kernel(hidden_ref, gain_ref, mask_ref, ids_ref, out_ref):
@@ -191,22 +197,25 @@
     )(hidden, norm_gain.reshape(1, width), slot_mask.reshape(1, own_rows), token_ids.reshape(1, own_rows))
 
 
-def stats_kernel(x_ref, w_ref, id_ref, out_ref):
-    logits = jnp.dot(x_ref[...], w_ref[...], preferred_element_type=jnp.float32)
+def stats_kernel(x_ref, w_ref, out_ref):
+    depth, vocab = w_ref.shape
+    logits = jnp.dot(x_ref[:, :depth], w_ref[...], preferred_element_type=jnp.float32)
+    meta = x_ref[:, depth:depth + 128].astype(jnp.float32)
+    token = (meta[:, 0:1] * 256.0 + meta[:, 1:2]).astype(jnp.int32) - lax.axis_index("tensor") * vocab
     peak = jnp.max(logits, axis=1, keepdims=True)
     shifted = logits - peak
     weights = jnp.exp(shifted)
     mass = jnp.sum(weights, axis=1, keepdims=True)
     spread = jnp.sum(weights * shifted, axis=1, keepdims=True)
     column = lax.broadcasted_iota(jnp.int32, logits.shape, 1)
-    target = jnp.sum(jnp.where(column == id_ref[...], logits, 0.0), axis=1, keepdims=True)
+    target = jnp.sum(jnp.where(column == token, logits, 0.0), axis=1, keepdims=True)
     lane = lax.broadcasted_iota(jnp.int32, out_ref.shape, 1)
     out_ref[...] = jnp.where(
         lane == 0, peak, jnp.where(lane == 1, mass, jnp.where(lane == 2, spread, target))
     )
 
 
-def row_stats(rows, weight, local_ids, width, tile):
+def row_stats(rows, weight, tile):
     count = rows.shape[0]
     depth, vocab = weight.shape
     return pl.pallas_call(
@@ -214,18 +223,17 @@
         out_shape=jax.ShapeDtypeStruct((count, 128), jnp.float32),
         grid=(count // tile,),
         in_specs=[
-            pl.BlockSpec((tile, width), lambda i: (i, 0)),
+            pl.BlockSpec((tile, rows.shape[1]), lambda i: (i, 0)),
             pl.BlockSpec((depth, vocab), lambda i: (0, 0)),
-            pl.BlockSpec((tile, 1), lambda i: (i, 0)),
         ],
         out_specs=pl.BlockSpec((tile, 128), lambda i: (i, 0)),
         compiler_params=pltpu.CompilerParams(vmem_limit_bytes=56 * 1024 * 1024),
         cost_estimate=pl.CostEstimate(
             flops=2 * count * depth * vocab,
             transcendentals=count * vocab,
-            bytes_accessed=2 * count * width + 2 * depth * vocab + 512 * count,
+            bytes_accessed=2 * count * rows.shape[1] + 2 * depth * vocab + 512 * count,
         ),
-    )(rows, weight, local_ids)
+    )(rows, weight)
 
 
 def on_device(
@@ -233,10 +241,9 @@
 ):
     own_rows = hidden.shape[0]
     vocab_local = head_weight.shape[1]
-    shape = (lax.axis_size("x"), lax.axis_size("y"), lax.axis_size("core"))
-    n_tensor = shape[0] * shape[1] * shape[2]
+    n_tensor = lax.axis_size("tensor")
     n_dp = lax.axis_size("dp")
-    tensor_index = tensor_position(shape)
+    tensor_index = lax.axis_index("tensor")
     widened = hidden.astype(jnp.float32)
     inverse_rms = lax.rsqrt(jnp.mean(widened * widened, axis=1, keepdims=True) + EPSILON)
     normed = (widened * inverse_rms * norm_gain).astype(jnp.bfloat16)
@@ -251,15 +258,9 @@
     )
     source = jnp.sum(jnp.where(chosen, slot_index[None, :], 0), axis=1)
     block = prep(hidden, norm_gain, slot_mask, token_ids)
-    chip_rows = lax.all_gather(block, ("x", "y"), axis=0, tiled=True)
-    gathered = lax.all_gather(
-        chip_rows.reshape(shape[0] * shape[1], LIVE, block.shape[1]), "core", axis=1
-    ).reshape(n_tensor * LIVE, block.shape[1])
-    meta_cols = gathered[:, width:width + 2].astype(jnp.float32)
-    piece_ids = (meta_cols[:, 0] * 256.0 + meta_cols[:, 1]).astype(jnp.int32)
-    local_ids = (piece_ids - tensor_index * vocab_local)[:, None]
+    gathered = lax.all_gather(block, "tensor", axis=0, tiled=True)
     row_count = gathered.shape[0]
-    stats = row_stats(gathered, head_weight, local_ids, width, 256 if row_count % 256 == 0 else row_count)
+    stats = row_stats(gathered, head_weight, 256 if row_count % 256 == 0 else row_count)
     blocks = stats[:, :4].reshape(n_tensor, LIVE, 4).transpose(0, 2, 1)
     request_count = lengths.shape[1]
     span_lengths = lengths[0]
@@ -274,39 +275,31 @@
         .at[:, 127].set(jnp.ones((8,), jnp.float32).at[:request_count].set(span_lengths.astype(jnp.float32)))
     )
     ids_tile = jnp.zeros((8, 128), jnp.float32).at[:request_count, 1].set(request_order.astype(jnp.float32))
-    own, routed = finish(blocks, spans, ids_tile, n_tensor, n_dp, shape)
-    place = jnp.clip(live_sum - 1, 0, LIVE - 1)
-    token_logprob = weight_mask * jnp.take(own[0], place)
-    token_entropy = weight_mask * jnp.take(own[1], place)
-    all_totals = routed[:, :request_count, 0].reshape(-1)
-    all_owners = routed[:, :request_count, 1].reshape(-1)
-    wanted = (lax.axis_index("dp") * request_count + jnp.arange(request_count)).astype(jnp.float32)
-    route_table = all_owners[:, None] == wanted[None, :]
-    request_score = jnp.sum(jnp.where(route_table, all_totals[:, None], 0.0), axis=0)
+    place = live_sum - 1
+    spread = ((place[:, None] == jnp.arange(LIVE, dtype=jnp.int32)[None, :]) & (slot_mask[:, None] == 1))
+    logprob_row, entropy_row, score_row = finish(
+        blocks, spans, ids_tile, spread.astype(jnp.float32), n_tensor, n_dp, request_count
+    )
+    token_logprob = logprob_row.reshape(own_rows)
+    token_entropy = entropy_row.reshape(own_rows)
+    request_score = score_row.reshape(request_count)
     return (token_logprob, token_entropy, token_value, request_score)
 
 
 def solution(mesh):
-    n_dp, n_tensor = mesh.devices.shape
-    cores = 2
-    rows = min(4, n_tensor // cores)
-    split = Mesh(
-        mesh.devices.reshape(n_dp, n_tensor // (rows * cores), rows, cores), ("dp", "x", "y", "core")
-    )
-    tensor = ("x", "y", "core")
     return jax.shard_map(
         on_device,
-        mesh=split,
+        mesh=mesh,
         in_specs=(
-            P(("dp",) + tensor, None),
+            P(("dp", "tensor"), None),
             P(),
-            P(None, tensor),
+            P(None, "tensor"),
             P(),
-            P(("dp",) + tensor),
-            P(("dp",) + tensor),
+            P(("dp", "tensor")),
+            P(("dp", "tensor")),
             P("dp", None),
             P("dp"),
         ),
-        out_specs=(P(("dp",) + tensor), P(("dp",) + tensor), P(("dp",) + tensor), P("dp")),
+        out_specs=(P(("dp", "tensor")), P(("dp", "tensor")), P(("dp", "tensor")), P("dp")),
         check_vma=False,
     )

time: 153 us -> 125 us (0.82)
  waiting for transfers between devices: 66.6 us -> 43.7 us
  other arithmetic: 7.49 us -> 4.68 us
  Pallas kernels: 46.3 us -> 44.2 us
    all_gather x2 -> x1, waiting for transfers between devices: 66.6 us -> 43.6 us  [on_device(): gathered = lax.all_gather(block, 'tensor', axis=0, tiled=True)]
    unnamed x16 -> x19, local copies, waits for them, and re-layouts: 9.66 us -> 13 us
    pallas_call x1, Pallas kernels: 25 us -> 22.9 us  [finish(): pl.pallas_call(lambda *refs: finish_kernel(n_tensor, n_dp, *refs), out_sh...]
    gather x2 -> x0, local copies, waits for them, and re-layouts: 1.55 us -> none  [the longest x1 0.78 us: on_device(): token_logprob = weight_mask * jnp.take(own[0], place)]
  transfers between devices with their start and end apart: 2 -> 1, of which waited for: 2 -> 1; matrix products, arithmetic and copies ran while one was open for 10% -> 13% of each run, Pallas kernels for 0% -> 0%
where the time goes in v13:
time: 125 us; the launch traced here: 124 us
  Pallas kernels  44.2 us (35%)
  waiting for transfers between devices  43.7 us (35%)
  local copies, waits for them, and re-layouts  16.6 us (13%)
  between operations  14.2 us (11%)
  other arithmetic  4.68 us (4%)
    all_gather x1, waiting for transfers between devices, on_device(): gathered = lax.all_gather(block, 'tensor', axis=0, tiled=True)  43.6 us
    pallas_call x1, Pallas kernels, finish(): pl.pallas_call(lambda *refs: finish_kernel(n_tensor, n_dp, *refs), out_sh...  22.9 us
    pallas_call x1, Pallas kernels, row_stats(): pl.pallas_call(stats_kernel, out_shape=jax.ShapeDtypeStruct((count, 128),...  19.3 us
    unnamed x19, local copies, waits for them, and re-layouts  13 us
    another operation x7, other arithmetic  2.86 us
  transfers between devices with their start and end apart: 1, of which 1 were waited for; matrix products, arithmetic and copies ran while one was open for 13% of the time, Pallas kernels for 0%

profile of v13, /device:TPU:1, one launch (start us, length us, event | category | flops | bytes accessed | tf_op | source)
XLA Modules:
  0.0 124.1 jit_solution(4994079687149320303)
XLA Ops:
  7.2 0.0 all-gather.2.cloned.1.call-start
  7.2 2.0 %shard_map.116 = bf16[48,2176]{1,0:T(8,128)(2,1)} custom-call(bf16[64,2048]{1,0:T(8,128)(2,1)} %hidden_ref.1, f32[1,2048]{1,0:T(1,128)} %bitcast.24, s32[1,64]{1,0:T(1,128)} %bitcast.25, s32[1,64]{1,0:T(1,128)} %bitcast.27), custom_call_target="tpu_custom_call" | custom-call | tf_op jit(solution)/shard_map/pallas_call | solution.py:192
  9.2 0.0 all-gather.2.cloned.1.call-update
  9.3 0.0 copy-start.4
  9.3 0.0 copy-start.6
  9.3 9.6 %copy.22.w_ref = bf16[2048,1572]{1,0:T(8,128)(2,1)} copy(bf16[2048,1572]{0,1:T(8,128)(2,1)} %param.20) | data formatting | bytes 12877824 | tf_op args[2]
  18.9 0.1 copy.25
  19.0 0.1 reduce-window.13
  19.1 0.2 reduce-window.14
  19.3 0.5 slice.64
  19.8 0.1 copy.26
  19.9 0.6 compare_reduce_fusion
  20.6 0.6 fusion.11
  21.2 0.1 copy.27
  21.3 0.6 compare_reduce_fusion.1
  21.9 0.6 iota_compare_fusion.3
  22.6 0.1 add_reduce_fusion
  22.7 0.1 select_reduce_fusion
  22.8 0.1 convert_reduce_fusion
  22.9 0.7 convert_select_fusion
  23.6 0.7 scatter.14.refs_2_
  24.3 0.1 scatter.11.refs_1_
  24.4 0.2 fusion.1
  24.6 0.7 fusion.8.refs_3_
  25.3 0.8 fusion
  26.0 43.6 %all-gather.2.cloned.1.call-done.x_ref = bf16[1536,2176]{1,0:T(8,128)(2,1)} async-done(((bf16[48,2176]{1,0:T(8,128)(2,1)}), bf16[1536,2176]{1,0:T(8,128)(2,1)}) %all-gather.2.cloned.1.call-update) | async-done | bytes 6684688 | tf_op jit(solution)/shard_map/all_gather | solution.py:261
  69.7 19.3 %shard_map.117 = f32[1536,128]{1,0:T(8,128)} custom-call(bf16[1536,2176]{1,0:T(8,128)(2,1)} %all-gather.2.cloned.1.call-done.x_ref, bf16[2048,1572]{1,0:T(8,128)(2,1)} %copy.22.w_ref), custom_call_target="tpu_custom_call" | custom-call | flops 9890168832 | bytes 13910016 | tf_op jit(solution)/shard_map/pallas_call | solution.py:221
  89.0 2.1 %copy.24 = f32[32,48,4]{1,2,0:T(4,128)} copy(f32[32,48,4]{2,1,0:T(8,128)} %bitcast.22) | data formatting | bytes 49152 | tf_op jit(solution)/shard_map/reshape | solution.py:264
  91.1 22.9 %shard_map.118 = (f32[1,64]{1,0:T(1,128)}, f32[1,64]{1,0:T(1,128)}, f32[1,8]{1,0:T(1,128)}) custom-call(f32[32,4,48]{2,1,0:T(4,128)} %bitcast.23, f32[8,128]{1,0:T(8,128)} %copy-done.1, f32[8,128]{1,0:T(8,128)} %scatter.14.refs_2_, f32[64,48]{1,0:T(8,128)} %fusion.8.refs_3_), custom_call_target="tpu_custom_call" | custom-call | tf_op jit(solution)/shard_map/pallas_call | solution.py:138
  113.9 1.1 copy.34
  115.1 1.1 copy.35
  116.2 1.1 copy.36
  (18 shorter events, 0.1 us)
Async XLA Ops:
  7.2 62.5 %all-gather.2.cloned.1.call-start = ((), (), s32[]{:S(2)}) async-start(), calls=%async_computation | async-start | bytes 6893568 | tf_op jit(solution)/shard_map/all_gather | solution.py:261
  9.3 9.7 %copy-start.4 = (s32[64]{0:T(128)S(1)}, s32[64]{0:T(128)}, u32[]{:S(2)}) copy-start(s32[64]{0:T(128)} %param.23) | copy-start | bytes 772
  9.3 9.9 %copy-start.5 = (s32[1,8]{1,0:T(1,128)S(1)}, s32[1,8]{1,0:T(1,128)}, u32[]{:S(2)}) copy-start(s32[1,8]{1,0:T(1,128)} %param.24) | copy-start | bytes 100
  9.3 11.3 %copy-start.6 = (s32[8]{0:T(128)S(1)}, s32[8]{0:T(128)}, u32[]{:S(2)}) copy-start(s32[8]{0:T(128)} %param.25) | copy-start | bytes 100
  9.3 15.0 %copy-start.3 = (bf16[2048]{0:T(1024)(128)(2,1)S(1)}, bf16[2048]{0:T(1024)(128)(2,1)}, u32[]{:S(2)}) copy-start(bf16[2048]{0:T(1024)(128)(2,1)} %param.21) | copy-start | bytes 12292
  9.3 15.1 %copy-start = (bf16[64,2048]{1,0:T(8,128)(2,1)S(1)}, bf16[64,2048]{1,0:T(8,128)(2,1)}, u32[]{:S(2)}) copy-start(bf16[64,2048]{1,0:T(8,128)(2,1)} %hidden_ref.1) | copy-start | bytes 786436
  9.3 16.0 %copy-start.2 = (f32[2048]{0:T(1024)S(1)}, f32[2048]{0:T(1024)}, u32[]{:S(2)}) copy-start(f32[2048]{0:T(1024)} %param.19) | copy-start | bytes 24580
  24.4 64.6 %copy-start.1 = (f32[8,128]{1,0:T(8,128)}, f32[8,128]{1,0:T(8,128)S(1)}, u32[]{:S(2)}) copy-start(f32[8,128]{1,0:T(8,128)S(1)} %scatter.11.refs_1_) | copy-start | bytes 12292
Sparse Core Ops, SparseCore 0:
  10.6 59.0 all-gather.1

commit v14 on v13

--- a/solution.py
+++ b/solution.py
@@ -10,7 +10,7 @@
 LIVE = 48
 
 
-def finish_kernel(n_tensor, n_dp, send_ref, span_ref, ids_ref, spread_ref, logprob_ref, entropy_ref, score_ref,
+def finish_kernel(n_tensor, n_dp, count, send_ref, span_ref, ids_ref, spread_ref, result_ref,
                   held, t_held, d_held, part_msg, route_msg,
                   a_send, a_recv, t_send, t_recv, d_send, d_recv):
     me = lax.axis_index("tensor")
@@ -71,9 +71,10 @@
         lax.broadcasted_iota(jnp.int32, (slots, slots), 0)
         == lax.broadcasted_iota(jnp.int32, (slots, slots), 1)
     )
-    for value, out in ((logprob, logprob_ref), (entropy, entropy_ref)):
+    result_ref[...] = jnp.zeros(result_ref.shape, jnp.float32)
+    for index, value in enumerate((logprob, entropy)):
         column = jnp.sum(jnp.where(placed, value, 0.0), axis=1, keepdims=True)
-        out[...] = jnp.sum(jnp.where(same, column, 0.0), axis=0, keepdims=True)
+        result_ref[index:index + 1, :slots] = jnp.sum(jnp.where(same, column, 0.0), axis=0, keepdims=True)
 
     spans = span_ref[...]
     partial = jnp.sum(spans[:, :lanes] * logprob, axis=1, keepdims=True) / spans[:, 127:128]
@@ -122,28 +123,23 @@
             send_sem=d_send.at[offset], recv_sem=d_recv.at[offset],
             device_id=(source, me), device_id_type=MESH,
         ).wait_recv()
-    count = score_ref.shape[1]
     wanted = (dp * count + lax.broadcasted_iota(jnp.int32, (1, count), 1)).astype(jnp.float32)
     score = jnp.zeros((1, count), jnp.float32)
     for group in range(n_dp):
         block = d_held[group]
         hit = block[:count, 1:2] == wanted
         score = score + jnp.sum(jnp.where(hit, block[:count, 0:1], 0.0), axis=0, keepdims=True)
-    score_ref[...] = score
+    result_ref[2:3, :count] = score
 
 
 def finish(blocks, spans, ids, spread, n_tensor, n_dp, count):
     tile = spans.shape
     lanes = blocks.shape[2]
     return pl.pallas_call(
-        lambda *refs: finish_kernel(n_tensor, n_dp, *refs),
-        out_shape=(
-            jax.ShapeDtypeStruct((1, spread.shape[0]), jnp.float32),
-            jax.ShapeDtypeStruct((1, spread.shape[0]), jnp.float32),
-            jax.ShapeDtypeStruct((1, count), jnp.float32),
-        ),
+        lambda *refs: finish_kernel(n_tensor, n_dp, count, *refs),
+        out_shape=jax.ShapeDtypeStruct((8, 128), jnp.float32),
         in_specs=[pl.BlockSpec(memory_space=pltpu.VMEM)] * 4,
-        out_specs=(pl.BlockSpec(memory_space=pltpu.VMEM),) * 3,
+        out_specs=pl.BlockSpec(memory_space=pltpu.VMEM),
         scratch_shapes=[
             pltpu.VMEM(blocks.shape, jnp.float32),
             pltpu.VMEM((n_tensor,) + tile, jnp.float32),
@@ -277,12 +273,10 @@
     ids_tile = jnp.zeros((8, 128), jnp.float32).at[:request_count, 1].set(request_order.astype(jnp.float32))
     place = live_sum - 1
     spread = ((place[:, None] == jnp.arange(LIVE, dtype=jnp.int32)[None, :]) & (slot_mask[:, None] == 1))
-    logprob_row, entropy_row, score_row = finish(
-        blocks, spans, ids_tile, spread.astype(jnp.float32), n_tensor, n_dp, request_count
-    )
-    token_logprob = logprob_row.reshape(own_rows)
-    token_entropy = entropy_row.reshape(own_rows)
-    request_score = score_row.reshape(request_count)
+    result = finish(blocks, spans, ids_tile, spread.astype(jnp.float32), n_tensor, n_dp, request_count)
+    token_logprob = result[0, :own_rows]
+    token_entropy = result[1, :own_rows]
+    request_score = result[2, :request_count]
     return (token_logprob, token_entropy, token_value, request_score)
 
 

time: 125 us -> 124 us (level)
    unnamed x19 -> x16, local copies, waits for them, and re-layouts: 13 us -> 9.66 us
    squeeze x0 -> x2, local copies, waits for them, and re-layouts: none -> 2.45 us  [the longest x1 1.27 us: on_device(): token_entropy = result[1, :own_rows]]
where the time goes in v14:
time: 124 us; the launch traced here: 123 us
  Pallas kernels  44.3 us (36%)
  waiting for transfers between devices  43.7 us (35%)
  local copies, waits for them, and re-layouts  15.7 us (13%)
  between operations  14.2 us (11%)
  other arithmetic  4.68 us (4%)
    all_gather x1, waiting for transfers between devices, on_device(): gathered = lax.all_gather(block, 'tensor', axis=0, tiled=True)  43.6 us
    pallas_call x1, Pallas kernels, finish(): pl.pallas_call(lambda *refs: finish_kernel(n_tensor, n_dp, count, *refs),...  22.9 us
    pallas_call x1, Pallas kernels, row_stats(): pl.pallas_call(stats_kernel, out_shape=jax.ShapeDtypeStruct((count, 128),...  19.3 us
    unnamed x16, local copies, waits for them, and re-layouts  9.66 us
    another operation x7, other arithmetic  2.86 us
  transfers between devices with their start and end apart: 1, of which 1 were waited for; matrix products, arithmetic and copies ran while one was open for 13% of the time, Pallas kernels for 0%

profile of v14, /device:TPU:1, one launch (start us, length us, event | category | flops | bytes accessed | tf_op | source)
XLA Modules:
  0.0 123.3 jit_solution(15325690046583563617)
XLA Ops:
  7.2 0.0 all-gather.2.cloned.1.call-start
  7.2 2.0 %shard_map.116 = bf16[48,2176]{1,0:T(8,128)(2,1)} custom-call(bf16[64,2048]{1,0:T(8,128)(2,1)} %hidden_ref.1, f32[1,2048]{1,0:T(1,128)} %bitcast.27, s32[1,64]{1,0:T(1,128)} %bitcast.28, s32[1,64]{1,0:T(1,128)} %bitcast.30), custom_call_target="tpu_custom_call" | custom-call | tf_op jit(solution)/shard_map/pallas_call | solution.py:188
  9.2 0.0 all-gather.2.cloned.1.call-update
  9.3 0.0 copy-start.4
  9.3 0.0 copy-start.6
  9.3 0.0 copy-start.3
  9.3 9.6 %copy.22.w_ref = bf16[2048,1572]{1,0:T(8,128)(2,1)} copy(bf16[2048,1572]{0,1:T(8,128)(2,1)} %param.20) | data formatting | bytes 12877824 | tf_op args[2]
  18.9 0.1 copy.25
  19.0 0.1 reduce-window.13
  19.1 0.2 reduce-window.14
  19.3 0.5 slice.76
  19.8 0.1 copy.26
  19.9 0.6 compare_reduce_fusion
  20.6 0.6 fusion.11
  21.2 0.1 copy.27
  21.3 0.6 compare_reduce_fusion.1
  21.9 0.6 iota_compare_fusion.3
  22.6 0.1 add_reduce_fusion
  22.7 0.1 select_reduce_fusion
  22.8 0.1 convert_reduce_fusion
  22.9 0.7 convert_select_fusion
  23.6 0.7 scatter.14.refs_2_
  24.3 0.1 scatter.11.refs_1_
  24.4 0.2 fusion.1
  24.6 0.7 fusion.8.refs_3_
  25.3 0.8 fusion
  26.0 43.6 %all-gather.2.cloned.1.call-done.x_ref = bf16[1536,2176]{1,0:T(8,128)(2,1)} async-done(((bf16[48,2176]{1,0:T(8,128)(2,1)}), bf16[1536,2176]{1,0:T(8,128)(2,1)}) %all-gather.2.cloned.1.call-update) | async-done | bytes 6684688 | tf_op jit(solution)/shard_map/all_gather | solution.py:257
  69.7 19.3 %shard_map.117 = f32[1536,128]{1,0:T(8,128)} custom-call(bf16[1536,2176]{1,0:T(8,128)(2,1)} %all-gather.2.cloned.1.call-done.x_ref, bf16[2048,1572]{1,0:T(8,128)(2,1)} %copy.22.w_ref), custom_call_target="tpu_custom_call" | custom-call | flops 9890168832 | bytes 13910016 | tf_op jit(solution)/shard_map/pallas_call | solution.py:217
  89.0 2.1 %copy.24 = f32[32,48,4]{1,2,0:T(4,128)} copy(f32[32,48,4]{2,1,0:T(8,128)} %bitcast.25) | data formatting | bytes 49152 | tf_op jit(solution)/shard_map/reshape | solution.py:260
  91.1 22.9 %shard_map.118 = f32[8,128]{1,0:T(8,128)} custom-call(f32[32,4,48]{2,1,0:T(4,128)} %bitcast.26, f32[8,128]{1,0:T(8,128)} %copy-done.1, f32[8,128]{1,0:T(8,128)} %scatter.14.refs_2_, f32[64,48]{1,0:T(8,128)} %fusion.8.refs_3_), custom_call_target="tpu_custom_call" | custom-call | tf_op jit(solution)/shard_map/pallas_call | solution.py:138
  114.0 1.3 %slice_bitcast_fusion.1 = (f32[64]{0:T(128)}, f32[64]{0:T(128)}) fusion(f32[8,128]{1,0:T(8,128)} %shard_map.118), kind=kLoop, calls=%fused_computation.26 | loop fusion | bytes 1024 | tf_op jit(solution)/shard_map/squeeze | solution.py:278
  115.3 1.2 slice_bitcast_fusion
  (17 shorter events, 0.1 us)
Async XLA Ops:
  7.2 62.5 %all-gather.2.cloned.1.call-start = ((), (), s32[]{:S(2)}) async-start(), calls=%async_computation | async-start | bytes 6893568 | tf_op jit(solution)/shard_map/all_gather | solution.py:257
  9.3 9.7 %copy-start.4 = (s32[64]{0:T(128)S(1)}, s32[64]{0:T(128)}, u32[]{:S(2)}) copy-start(s32[64]{0:T(128)} %param.23) | copy-start | bytes 772
  9.3 9.9 %copy-start.5 = (s32[1,8]{1,0:T(1,128)S(1)}, s32[1,8]{1,0:T(1,128)}, u32[]{:S(2)}) copy-start(s32[1,8]{1,0:T(1,128)} %param.24) | copy-start | bytes 100
  9.3 11.3 %copy-start.6 = (s32[8]{0:T(128)S(1)}, s32[8]{0:T(128)}, u32[]{:S(2)}) copy-start(s32[8]{0:T(128)} %param.25) | copy-start | bytes 100
  9.3 15.0 %copy-start.3 = (bf16[2048]{0:T(1024)(128)(2,1)S(1)}, bf16[2048]{0:T(1024)(128)(2,1)}, u32[]{:S(2)}) copy-start(bf16[2048]{0:T(1024)(128)(2,1)} %param.21) | copy-start | bytes 12292
  9.3 15.1 %copy-start = (bf16[64,2048]{1,0:T(8,128)(2,1)S(1)}, bf16[64,2048]{1,0:T(8,128)(2,1)}, u32[]{:S(2)}) copy-start(bf16[64,2048]{1,0:T(8,128)(2,1)} %hidden_ref.1) | copy-start | bytes 786436
  9.3 16.0 %copy-start.2 = (f32[2048]{0:T(1024)S(1)}, f32[2048]{0:T(1024)}, u32[]{:S(2)}) copy-start(f32[2048]{0:T(1024)} %param.19) | copy-start | bytes 24580
  24.4 64.6 %copy-start.1 = (f32[8,128]{1,0:T(8,128)}, f32[8,128]{1,0:T(8,128)S(1)}, u32[]{:S(2)}) copy-start(f32[8,128]{1,0:T(8,128)S(1)} %scatter.11.refs_1_) | copy-start | bytes 12292
Sparse Core Ops, SparseCore 0:
  10.6 59.0 all-gather.1

commit v15 on v14

--- a/solution.py
+++ b/solution.py
@@ -193,43 +193,48 @@
     )(hidden, norm_gain.reshape(1, width), slot_mask.reshape(1, own_rows), token_ids.reshape(1, own_rows))
 
 
-def stats_kernel(x_ref, w_ref, out_ref):
-    depth, vocab = w_ref.shape
-    logits = jnp.dot(x_ref[:, :depth], w_ref[...], preferred_element_type=jnp.float32)
-    meta = x_ref[:, depth:depth + 128].astype(jnp.float32)
-    token = (meta[:, 0:1] * 256.0 + meta[:, 1:2]).astype(jnp.int32) - lax.axis_index("tensor") * vocab
-    peak = jnp.max(logits, axis=1, keepdims=True)
+def stats_kernel(x_ref, wt_ref, out_ref):
+    vocab, depth = wt_ref.shape
+    contract_last = (((1,), (1,)), ((), ()))
+    logits = lax.dot_general(wt_ref[...], x_ref[:, :depth], contract_last, preferred_element_type=jnp.float32)
+    pick = (
+        lax.broadcasted_iota(jnp.int32, (8, 128), 0) == lax.broadcasted_iota(jnp.int32, (8, 128), 1)
+    ).astype(jnp.bfloat16)
+    meta = lax.dot_general(pick, x_ref[:, depth:depth + 128], contract_last, preferred_element_type=jnp.float32)
+    token = (meta[0:1, :] * 256.0 + meta[1:2, :]).astype(jnp.int32) - lax.axis_index("tensor") * vocab
+    peak = jnp.max(logits, axis=0, keepdims=True)
     shifted = logits - peak
     weights = jnp.exp(shifted)
-    mass = jnp.sum(weights, axis=1, keepdims=True)
-    spread = jnp.sum(weights * shifted, axis=1, keepdims=True)
-    column = lax.broadcasted_iota(jnp.int32, logits.shape, 1)
-    target = jnp.sum(jnp.where(column == token, logits, 0.0), axis=1, keepdims=True)
-    lane = lax.broadcasted_iota(jnp.int32, out_ref.shape, 1)
+    mass = jnp.sum(weights, axis=0, keepdims=True)
+    spread = jnp.sum(weights * shifted, axis=0, keepdims=True)
+    entry = lax.broadcasted_iota(jnp.int32, logits.shape, 0)
+    target = jnp.sum(jnp.where(entry == token, logits, 0.0), axis=0, keepdims=True)
+    row = lax.broadcasted_iota(jnp.int32, out_ref.shape, 0)
     out_ref[...] = jnp.where(
-        lane == 0, peak, jnp.where(lane == 1, mass, jnp.where(lane == 2, spread, target))
-    )
-
-
-def row_stats(rows, weight, tile):
+        row == 0, peak,
+        jnp.where(row == 1, mass, jnp.where(row == 2, spread, jnp.where(row == 3, target, 0.0))),
+    )
+
+
+def row_stats(rows, weight_t, tile):
     count = rows.shape[0]
-    depth, vocab = weight.shape
+    vocab, depth = weight_t.shape
     return pl.pallas_call(
         stats_kernel,
-        out_shape=jax.ShapeDtypeStruct((count, 128), jnp.float32),
+        out_shape=jax.ShapeDtypeStruct((8, count), jnp.float32),
         grid=(count // tile,),
         in_specs=[
             pl.BlockSpec((tile, rows.shape[1]), lambda i: (i, 0)),
-            pl.BlockSpec((depth, vocab), lambda i: (0, 0)),
+            pl.BlockSpec((vocab, depth), lambda i: (0, 0)),
         ],
-        out_specs=pl.BlockSpec((tile, 128), lambda i: (i, 0)),
+        out_specs=pl.BlockSpec((8, tile), lambda i: (0, i)),
         compiler_params=pltpu.CompilerParams(vmem_limit_bytes=56 * 1024 * 1024),
         cost_estimate=pl.CostEstimate(
             flops=2 * count * depth * vocab,
             transcendentals=count * vocab,
-            bytes_accessed=2 * count * rows.shape[1] + 2 * depth * vocab + 512 * count,
+            bytes_accessed=2 * count * rows.shape[1] + 2 * depth * vocab + 32 * count,
         ),
-    )(rows, weight)
+    )(rows, weight_t)
 
 
 def on_device(
@@ -256,8 +261,8 @@
     block = prep(hidden, norm_gain, slot_mask, token_ids)
     gathered = lax.all_gather(block, "tensor", axis=0, tiled=True)
     row_count = gathered.shape[0]
-    stats = row_stats(gathered, head_weight, 256 if row_count % 256 == 0 else row_count)
-    blocks = stats[:, :4].reshape(n_tensor, LIVE, 4).transpose(0, 2, 1)
+    stats = row_stats(gathered, head_weight.T, 256 if row_count % 256 == 0 else row_count)
+    blocks = stats[:4].reshape(4, n_tensor, LIVE).transpose(1, 0, 2)
     request_count = lengths.shape[1]
     span_lengths = lengths[0]
     span_ends = jnp.cumsum(span_lengths)

time: 124 us -> 123 us (level)
  local copies, waits for them, and re-layouts: 15.7 us -> 6.88 us
  waiting for transfers between devices: 43.7 us -> 47.5 us
  other arithmetic: 4.68 us -> 8.27 us
    unnamed x16 -> x3, local copies, waits for them, and re-layouts: 9.66 us -> 0.7 us
    all_gather x1, waiting for transfers between devices: 43.6 us -> 47.5 us  [on_device(): gathered = lax.all_gather(block, 'tensor', axis=0, tiled=True)]
    another operation x7, other arithmetic: 2.86 us -> 4.82 us
    reshape x1 -> x2, local copies, waits for them, and re-layouts: 2.06 us -> 0.75 us  [on_device(): blocks = stats[:4].reshape(4, n_tensor, LIVE).transpose(1, 0, 2)]
  transfers between devices with their start and end apart: 1 -> 1, of which waited for: 1 -> 1; matrix products, arithmetic and copies ran while one was open for 13% -> 11% of each run, Pallas kernels for 0% -> 0%
where the time goes in v15:
time: 123 us
  waiting for transfers between devices  47.5 us (39%)
  Pallas kernels  44 us (36%)
  between operations  14.1 us (11%)
  other arithmetic  8.27 us (7%)
  local copies, waits for them, and re-layouts  6.88 us (6%)
  matrix products  1.73 us (1%)
    all_gather x1, waiting for transfers between devices, on_device(): gathered = lax.all_gather(block, 'tensor', axis=0, tiled=True)  47.5 us
    pallas_call x1, Pallas kernels, finish(): pl.pallas_call(lambda *refs: finish_kernel(n_tensor, n_dp, count, *refs),...  22.9 us
    pallas_call x1, Pallas kernels, row_stats(): pl.pallas_call(stats_kernel, out_shape=jax.ShapeDtypeStruct((8, count), j...  19 us
    another operation x7, other arithmetic  4.82 us
  transfers between devices with their start and end apart: 1, of which 1 were waited for; matrix products, arithmetic and copies ran while one was open for 11% of the time, Pallas kernels for 0%

profile of v15, /device:TPU:1, one launch (start us, length us, event | category | flops | bytes accessed | tf_op | source)
XLA Modules:
  0.0 122.5 jit_solution(12287160135352828260)
XLA Ops:
  7.2 0.0 all-gather.2.cloned.1.call-start
  7.2 2.0 %shard_map.116 = bf16[48,2176]{1,0:T(8,128)(2,1)} custom-call(bf16[64,2048]{1,0:T(8,128)(2,1)} %hidden_ref.1, f32[1,2048]{1,0:T(1,128)} %bitcast.27, s32[1,64]{1,0:T(1,128)} %bitcast.28, s32[1,64]{1,0:T(1,128)} %bitcast.30), custom_call_target="tpu_custom_call" | custom-call | tf_op jit(solution)/shard_map/pallas_call | solution.py:188
  9.2 0.7 copy.20
  10.0 0.1 reduce-window.13
  10.1 0.8 reduce-window.14
  10.9 0.5 slice.76
  11.4 0.7 convert_bitcast_fusion
  12.1 0.1 copy.21
  12.2 0.6 compare_reduce_fusion
  12.8 1.3 %fusion.11 = f32[8,1]{0,1:T(1,128)S(1)} fusion(pred[]{:T(512)} %compare_reduce_fusion, s32[8]{0:T(128)} %param.25), kind=kLoop, calls=%fused_computation.24 | loop fusion | flops 16 | bytes 65 | tf_op jit(solution)/shard_map/reshape.134
  14.1 0.1 copy.22
  14.2 0.6 compare_reduce_fusion.1
  14.8 0.6 iota_compare_fusion.3
  15.5 0.1 add_reduce_fusion
  15.6 0.7 broadcast_compare_fusion
  16.3 0.1 select_reduce_fusion
  16.4 0.1 convert_reduce_fusion
  16.5 0.7 convert_select_fusion
  17.2 0.7 scatter.14.refs_2_
  17.8 0.7 reshape.196
  18.5 0.1 scatter.11.refs_1_
  18.6 1.1 fusion.1
  19.7 0.7 fusion.8.refs_3_
  20.4 1.7 %fusion = f32[64]{0:T(128)} fusion(bf16[2048,1]{0,1:T(2,128)(2,1)S(1)} %reshape.196, bf16[64,2048]{1,0:T(8,128)(2,1)} %hidden_ref.1, f32[2048]{0:T(1024)} %param.19, f32[64]{0:T(128)S(1)} %add_rsqrt_fusion, s32[64]{0:T(128)} %param.23), kind=kOutput, calls=%fused_computation.1 | convolution fusion | flops 786560 | bytes 275200 | tf_op jit(solution)/shard_map/dot_general | solution.py:252
  22.2 47.5 %all-gather.2.cloned.1.call-done.x_ref = bf16[1536,2176]{1,0:T(8,128)(2,1)} async-done(((bf16[48,2176]{1,0:T(8,128)(2,1)}), bf16[1536,2176]{1,0:T(8,128)(2,1)}) %all-gather.2.cloned.1.call-update) | async-done | bytes 6684688 | tf_op jit(solution)/shard_map/all_gather | solution.py:262
  69.7 19.0 %shard_map.117 = f32[8,1536]{1,0:T(8,128)} custom-call(bf16[1536,2176]{1,0:T(8,128)(2,1)} %all-gather.2.cloned.1.call-done.x_ref, bf16[1572,2048]{1,0:T(8,128)(2,1)} %bitcast.31), custom_call_target="tpu_custom_call" | custom-call | flops 9890168832 | bytes 13172736 | tf_op jit(solution)/shard_map/pallas_call | solution.py:222
  88.7 0.8 slice.75
  89.5 0.1 reshape.190
  89.6 0.7 copy.24
  90.3 22.9 %shard_map.118 = f32[8,128]{1,0:T(8,128)} custom-call(f32[32,4,48]{2,1,0:T(4,128)} %bitcast.26, f32[8,128]{1,0:T(8,128)} %copy-done, f32[8,128]{1,0:T(8,128)} %scatter.14.refs_2_, f32[64,48]{1,0:T(8,128)} %fusion.8.refs_3_), custom_call_target="tpu_custom_call" | custom-call | tf_op jit(solution)/shard_map/pallas_call | solution.py:138
  113.2 1.3 %slice_bitcast_fusion.1 = (f32[64]{0:T(128)}, f32[64]{0:T(128)}) fusion(f32[8,128]{1,0:T(8,128)} %shard_map.118), kind=kLoop, calls=%fused_computation.27 | loop fusion | bytes 1024 | tf_op jit(solution)/shard_map/squeeze | solution.py:283
  114.5 1.2 slice_bitcast_fusion
  (6 shorter events, 0.0 us)
Async XLA Ops:
  7.2 62.5 %all-gather.2.cloned.1.call-start = ((), (), s32[]{:S(2)}) async-start(), calls=%async_computation | async-start | bytes 6893568 | tf_op jit(solution)/shard_map/all_gather | solution.py:262
  18.6 70.1 %copy-start = (f32[8,128]{1,0:T(8,128)}, f32[8,128]{1,0:T(8,128)S(1)}, u32[]{:S(2)}) copy-start(f32[8,128]{1,0:T(8,128)S(1)} %scatter.11.refs_1_) | copy-start | bytes 12292
Sparse Core Ops, SparseCore 0:
  10.6 59.0 all-gather.1

commit v16 on v15

--- a/solution.py
+++ b/solution.py
@@ -261,7 +261,7 @@
     block = prep(hidden, norm_gain, slot_mask, token_ids)
     gathered = lax.all_gather(block, "tensor", axis=0, tiled=True)
     row_count = gathered.shape[0]
-    stats = row_stats(gathered, head_weight.T, 256 if row_count % 256 == 0 else row_count)
+    stats = row_stats(gathered, head_weight.T, 512 if row_count % 512 == 0 else row_count)
     blocks = stats[:4].reshape(4, n_tensor, LIVE).transpose(1, 0, 2)
     request_count = lengths.shape[1]
     span_lengths = lengths[0]

time: 123 us -> 123 us (level)
  transfers between devices with their start and end apart: 1 -> 1, of which waited for: 1 -> 1; matrix products, arithmetic and copies ran while one was open for 11% -> 10% of each run, Pallas kernels for 0% -> 0%
where the time goes in v16:
time: 123 us
  waiting for transfers between devices  47.5 us (39%)
  Pallas kernels  44.2 us (36%)
  between operations  14.1 us (11%)
  other arithmetic  8.27 us (7%)
  local copies, waits for them, and re-layouts  6.88 us (6%)
  matrix products  1.73 us (1%)
    all_gather x1, waiting for transfers between devices, on_device(): gathered = lax.all_gather(block, 'tensor', axis=0, tiled=True)  47.5 us
    pallas_call x1, Pallas kernels, finish(): pl.pallas_call(lambda *refs: finish_kernel(n_tensor, n_dp, count, *refs),...  22.9 us
    pallas_call x1, Pallas kernels, row_stats(): pl.pallas_call(stats_kernel, out_shape=jax.ShapeDtypeStruct((8, count), j...  19.2 us
    another operation x7, other arithmetic  4.82 us
  transfers between devices with their start and end apart: 1, of which 1 were waited for; matrix products, arithmetic and copies ran while one was open for 10% of the time, Pallas kernels for 0%

profile of v16, /device:TPU:1, one launch (start us, length us, event | category | flops | bytes accessed | tf_op | source)
XLA Modules:
  0.0 122.7 jit_solution(8213464957516534259)
XLA Ops:
  7.2 0.0 all-gather.2.cloned.1.call-start
  7.2 2.0 %shard_map.116 = bf16[48,2176]{1,0:T(8,128)(2,1)} custom-call(bf16[64,2048]{1,0:T(8,128)(2,1)} %hidden_ref.1, f32[1,2048]{1,0:T(1,128)} %bitcast.27, s32[1,64]{1,0:T(1,128)} %bitcast.28, s32[1,64]{1,0:T(1,128)} %bitcast.30), custom_call_target="tpu_custom_call" | custom-call | tf_op jit(solution)/shard_map/pallas_call | solution.py:188
  9.2 0.7 copy.20
  10.0 0.1 reduce-window.13
  10.1 0.8 reduce-window.14
  10.9 0.5 slice.76
  11.4 0.7 convert_bitcast_fusion
  12.1 0.1 copy.21
  12.2 0.6 compare_reduce_fusion
  12.8 1.3 %fusion.11 = f32[8,1]{0,1:T(1,128)S(1)} fusion(pred[]{:T(512)} %compare_reduce_fusion, s32[8]{0:T(128)} %param.25), kind=kLoop, calls=%fused_computation.24 | loop fusion | flops 16 | bytes 65 | tf_op jit(solution)/shard_map/reshape.134
  14.1 0.1 copy.22
  14.2 0.6 compare_reduce_fusion.1
  14.8 0.6 iota_compare_fusion.3
  15.5 0.1 add_reduce_fusion
  15.6 0.7 broadcast_compare_fusion
  16.3 0.1 select_reduce_fusion
  16.4 0.1 convert_reduce_fusion
  16.5 0.7 convert_select_fusion
  17.2 0.7 scatter.14.refs_2_
  17.8 0.7 reshape.196
  18.5 0.1 scatter.11.refs_1_
  18.6 1.1 fusion.1
  19.7 0.7 fusion.8.refs_3_
  20.4 1.7 %fusion = f32[64]{0:T(128)} fusion(bf16[2048,1]{0,1:T(2,128)(2,1)S(1)} %reshape.196, bf16[64,2048]{1,0:T(8,128)(2,1)} %hidden_ref.1, f32[2048]{0:T(1024)} %param.19, f32[64]{0:T(128)S(1)} %add_rsqrt_fusion, s32[64]{0:T(128)} %param.23), kind=kOutput, calls=%fused_computation.1 | convolution fusion | flops 786560 | bytes 275200 | tf_op jit(solution)/shard_map/dot_general | solution.py:252
  22.2 47.5 %all-gather.2.cloned.1.call-done.x_ref = bf16[1536,2176]{1,0:T(8,128)(2,1)} async-done(((bf16[48,2176]{1,0:T(8,128)(2,1)}), bf16[1536,2176]{1,0:T(8,128)(2,1)}) %all-gather.2.cloned.1.call-update) | async-done | bytes 6684688 | tf_op jit(solution)/shard_map/all_gather | solution.py:262
  69.7 19.2 %shard_map.117 = f32[8,1536]{1,0:T(8,128)} custom-call(bf16[1536,2176]{1,0:T(8,128)(2,1)} %all-gather.2.cloned.1.call-done.x_ref, bf16[1572,2048]{1,0:T(8,128)(2,1)} %bitcast.31), custom_call_target="tpu_custom_call" | custom-call | flops 9890168832 | bytes 13172736 | tf_op jit(solution)/shard_map/pallas_call | solution.py:222
  88.9 0.8 slice.75
  89.7 0.1 reshape.190
  89.8 0.7 copy.24
  90.5 22.9 %shard_map.118 = f32[8,128]{1,0:T(8,128)} custom-call(f32[32,4,48]{2,1,0:T(4,128)} %bitcast.26, f32[8,128]{1,0:T(8,128)} %copy-done, f32[8,128]{1,0:T(8,128)} %scatter.14.refs_2_, f32[64,48]{1,0:T(8,128)} %fusion.8.refs_3_), custom_call_target="tpu_custom_call" | custom-call | tf_op jit(solution)/shard_map/pallas_call | solution.py:138
  113.4 1.3 %slice_bitcast_fusion.1 = (f32[64]{0:T(128)}, f32[64]{0:T(128)}) fusion(f32[8,128]{1,0:T(8,128)} %shard_map.118), kind=kLoop, calls=%fused_computation.27 | loop fusion | bytes 1024 | tf_op jit(solution)/shard_map/squeeze | solution.py:283
  114.7 1.2 slice_bitcast_fusion
  (6 shorter events, 0.0 us)
Async XLA Ops:
  7.2 62.5 %all-gather.2.cloned.1.call-start = ((), (), s32[]{:S(2)}) async-start(), calls=%async_computation | async-start | bytes 6893568 | tf_op jit(solution)/shard_map/all_gather | solution.py:262
  18.6 70.3 %copy-start = (f32[8,128]{1,0:T(8,128)}, f32[8,128]{1,0:T(8,128)S(1)}, u32[]{:S(2)}) copy-start(f32[8,128]{1,0:T(8,128)S(1)} %scatter.11.refs_1_) | copy-start | bytes 12292
Sparse Core Ops, SparseCore 0:
  10.6 59.0 all-gather.1

commit v17 on v15

--- a/solution.py
+++ b/solution.py
@@ -205,8 +205,12 @@
     peak = jnp.max(logits, axis=0, keepdims=True)
     shifted = logits - peak
     weights = jnp.exp(shifted)
-    mass = jnp.sum(weights, axis=0, keepdims=True)
-    spread = jnp.sum(weights * shifted, axis=0, keepdims=True)
+    ones = jnp.ones((8, vocab), jnp.float32)
+    column_sum = lambda value: jnp.dot(
+        ones, value, preferred_element_type=jnp.float32, precision=lax.Precision.HIGHEST
+    )[0:1, :]
+    mass = column_sum(weights)
+    spread = column_sum(weights * shifted)
     entry = lax.broadcasted_iota(jnp.int32, logits.shape, 0)
     target = jnp.sum(jnp.where(entry == token, logits, 0.0), axis=0, keepdims=True)
     row = lax.broadcasted_iota(jnp.int32, out_ref.shape, 0)

time: 123 us -> 146 us (1.19)
  Pallas kernels: 44 us -> 66.6 us
    pallas_call x1, Pallas kernels: 19 us -> 41.7 us  [row_stats(): pl.pallas_call(stats_kernel, out_shape=jax.ShapeDtypeStruct((8, count), j...]
  transfers between devices with their start and end apart: 1 -> 1, of which waited for: 1 -> 1; matrix products, arithmetic and copies ran while one was open for 11% -> 9% of each run, Pallas kernels for 0% -> 0%
where the time goes in v17:
time: 146 us; the launch traced here: 145 us
  Pallas kernels  66.6 us (46%)
  waiting for transfers between devices  47.5 us (33%)
  between operations  14.1 us (10%)
  other arithmetic  8.27 us (6%)
  local copies, waits for them, and re-layouts  6.88 us (5%)
  matrix products  1.73 us (1%)
    all_gather x1, waiting for transfers between devices, on_device(): gathered = lax.all_gather(block, 'tensor', axis=0, tiled=True)  47.5 us
    pallas_call x1, Pallas kernels, row_stats(): pl.pallas_call(stats_kernel, out_shape=jax.ShapeDtypeStruct((8, count), j...  41.7 us
    pallas_call x1, Pallas kernels, finish(): pl.pallas_call(lambda *refs: finish_kernel(n_tensor, n_dp, count, *refs),...  22.9 us
    another operation x7, other arithmetic  4.82 us
  transfers between devices with their start and end apart: 1, of which 1 were waited for; matrix products, arithmetic and copies ran while one was open for 9% of the time, Pallas kernels for 0%

profile of v17, /device:TPU:1, one launch (start us, length us, event | category | flops | bytes accessed | tf_op | source)
XLA Modules:
  0.0 145.2 jit_solution(12078981960655778053)
XLA Ops:
  7.2 0.0 all-gather.2.cloned.1.call-start
  7.2 2.0 %shard_map.116 = bf16[48,2176]{1,0:T(8,128)(2,1)} custom-call(bf16[64,2048]{1,0:T(8,128)(2,1)} %hidden_ref.1, f32[1,2048]{1,0:T(1,128)} %bitcast.27, s32[1,64]{1,0:T(1,128)} %bitcast.28, s32[1,64]{1,0:T(1,128)} %bitcast.30), custom_call_target="tpu_custom_call" | custom-call | tf_op jit(solution)/shard_map/pallas_call | solution.py:188
  9.2 0.7 copy.20
  10.0 0.1 reduce-window.13
  10.1 0.8 reduce-window.14
  10.9 0.5 slice.76
  11.4 0.7 convert_bitcast_fusion
  12.1 0.1 copy.21
  12.2 0.6 compare_reduce_fusion
  12.8 1.3 fusion.11
  14.1 0.1 copy.22
  14.2 0.6 compare_reduce_fusion.1
  14.8 0.6 iota_compare_fusion.3
  15.5 0.1 add_reduce_fusion
  15.6 0.7 broadcast_compare_fusion
  16.3 0.1 select_reduce_fusion
  16.4 0.1 convert_reduce_fusion
  16.5 0.7 convert_select_fusion
  17.2 0.7 scatter.14.refs_2_
  17.8 0.7 reshape.196
  18.5 0.1 scatter.11.refs_1_
  18.6 1.1 fusion.1
  19.7 0.7 fusion.8.refs_3_
  20.4 1.7 %fusion = f32[64]{0:T(128)} fusion(bf16[2048,1]{0,1:T(2,128)(2,1)S(1)} %reshape.196, bf16[64,2048]{1,0:T(8,128)(2,1)} %hidden_ref.1, f32[2048]{0:T(1024)} %param.19, f32[64]{0:T(128)S(1)} %add_rsqrt_fusion, s32[64]{0:T(128)} %param.23), kind=kOutput, calls=%fused_computation.1 | convolution fusion | flops 786560 | bytes 275200 | tf_op jit(solution)/shard_map/dot_general | solution.py:256
  22.2 47.5 %all-gather.2.cloned.1.call-done.x_ref = bf16[1536,2176]{1,0:T(8,128)(2,1)} async-done(((bf16[48,2176]{1,0:T(8,128)(2,1)}), bf16[1536,2176]{1,0:T(8,128)(2,1)}) %all-gather.2.cloned.1.call-update) | async-done | bytes 6684688 | tf_op jit(solution)/shard_map/all_gather | solution.py:266
  69.7 41.7 %shard_map.117 = f32[8,1536]{1,0:T(8,128)} custom-call(bf16[1536,2176]{1,0:T(8,128)(2,1)} %all-gather.2.cloned.1.call-done.x_ref, bf16[1572,2048]{1,0:T(8,128)(2,1)} %bitcast.31), custom_call_target="tpu_custom_call" | custom-call | flops 9890168832 | bytes 13172736 | tf_op jit(solution)/shard_map/pallas_call | solution.py:226
  111.4 0.8 slice.75
  112.2 0.1 reshape.190
  112.3 0.7 copy.24
  112.9 22.9 %shard_map.118 = f32[8,128]{1,0:T(8,128)} custom-call(f32[32,4,48]{2,1,0:T(4,128)} %bitcast.26, f32[8,128]{1,0:T(8,128)} %copy-done, f32[8,128]{1,0:T(8,128)} %scatter.14.refs_2_, f32[64,48]{1,0:T(8,128)} %fusion.8.refs_3_), custom_call_target="tpu_custom_call" | custom-call | tf_op jit(solution)/shard_map/pallas_call | solution.py:138
  135.9 1.3 slice_bitcast_fusion.1
  137.2 1.2 slice_bitcast_fusion
  (6 shorter events, 0.0 us)
Async XLA Ops:
  7.2 62.5 %all-gather.2.cloned.1.call-start = ((), (), s32[]{:S(2)}) async-start(), calls=%async_computation | async-start | bytes 6893568 | tf_op jit(solution)/shard_map/all_gather | solution.py:266
  18.6 92.8 %copy-start = (f32[8,128]{1,0:T(8,128)}, f32[8,128]{1,0:T(8,128)S(1)}, u32[]{:S(2)}) copy-start(f32[8,128]{1,0:T(8,128)S(1)} %scatter.11.refs_1_) | copy-start | bytes 12292
Sparse Core Ops, SparseCore 0:
  10.6 59.0 all-gather.1

commit v18 on v15

--- a/solution.py
+++ b/solution.py
@@ -65,16 +65,6 @@
     log_mass = jnp.log(mass)
     logprob = target - peak - log_mass
     entropy = log_mass - spread / mass
-    slots = spread_ref.shape[0]
-    placed = spread_ref[...] > 0.0
-    same = (
-        lax.broadcasted_iota(jnp.int32, (slots, slots), 0)
-        == lax.broadcasted_iota(jnp.int32, (slots, slots), 1)
-    )
-    result_ref[...] = jnp.zeros(result_ref.shape, jnp.float32)
-    for index, value in enumerate((logprob, entropy)):
-        column = jnp.sum(jnp.where(placed, value, 0.0), axis=1, keepdims=True)
-        result_ref[index:index + 1, :slots] = jnp.sum(jnp.where(same, column, 0.0), axis=0, keepdims=True)
 
     spans = span_ref[...]
     partial = jnp.sum(spans[:, :lanes] * logprob, axis=1, keepdims=True) / spans[:, 127:128]
@@ -90,6 +80,16 @@
         )
         copy.start()
         copies.append(copy)
+    slots = spread_ref.shape[0]
+    placed = spread_ref[...] > 0.0
+    same = (
+        lax.broadcasted_iota(jnp.int32, (slots, slots), 0)
+        == lax.broadcasted_iota(jnp.int32, (slots, slots), 1)
+    )
+    result_ref[...] = jnp.zeros(result_ref.shape, jnp.float32)
+    for index, value in enumerate((logprob, entropy)):
+        column = jnp.sum(jnp.where(placed, value, 0.0), axis=1, keepdims=True)
+        result_ref[index:index + 1, :slots] = jnp.sum(jnp.where(same, column, 0.0), axis=0, keepdims=True)
     for copy in copies:
         copy.wait_send()
     for offset in range(1, n_tensor):

time: 123 us -> 123 us (level)
  no operation moved by 1% of the time
where the time goes in v18:
time: 123 us
  waiting for transfers between devices  47.5 us (39%)
  Pallas kernels  44 us (36%)
  between operations  14.1 us (11%)
  other arithmetic  8.27 us (7%)
  local copies, waits for them, and re-layouts  6.88 us (6%)
  matrix products  1.73 us (1%)
    all_gather x1, waiting for transfers between devices, on_device(): gathered = lax.all_gather(block, 'tensor', axis=0, tiled=True)  47.5 us
    pallas_call x1, Pallas kernels, finish(): pl.pallas_call(lambda *refs: finish_kernel(n_tensor, n_dp, count, *refs),...  22.9 us
    pallas_call x1, Pallas kernels, row_stats(): pl.pallas_call(stats_kernel, out_shape=jax.ShapeDtypeStruct((8, count), j...  19 us
    another operation x7, other arithmetic  4.82 us
  transfers between devices with their start and end apart: 1, of which 1 were waited for; matrix products, arithmetic and copies ran while one was open for 11% of the time, Pallas kernels for 0%

profile of v18, /device:TPU:1, one launch (start us, length us, event | category | flops | bytes accessed | tf_op | source)
XLA Modules:
  0.0 122.5 jit_solution(2375112677307473927)
XLA Ops:
  7.2 0.0 all-gather.2.cloned.1.call-start
  7.2 2.0 %shard_map.116 = bf16[48,2176]{1,0:T(8,128)(2,1)} custom-call(bf16[64,2048]{1,0:T(8,128)(2,1)} %hidden_ref.1, f32[1,2048]{1,0:T(1,128)} %bitcast.27, s32[1,64]{1,0:T(1,128)} %bitcast.28, s32[1,64]{1,0:T(1,128)} %bitcast.30), custom_call_target="tpu_custom_call" | custom-call | tf_op jit(solution)/shard_map/pallas_call | solution.py:188
  9.2 0.7 copy.20
  10.0 0.1 reduce-window.13
  10.1 0.8 reduce-window.14
  10.9 0.5 slice.76
  11.4 0.7 convert_bitcast_fusion
  12.1 0.1 copy.21
  12.2 0.6 compare_reduce_fusion
  12.8 1.3 %fusion.11 = f32[8,1]{0,1:T(1,128)S(1)} fusion(pred[]{:T(512)} %compare_reduce_fusion, s32[8]{0:T(128)} %param.25), kind=kLoop, calls=%fused_computation.24 | loop fusion | flops 16 | bytes 65 | tf_op jit(solution)/shard_map/reshape.134
  14.1 0.1 copy.22
  14.2 0.6 compare_reduce_fusion.1
  14.8 0.6 iota_compare_fusion.3
  15.5 0.1 add_reduce_fusion
  15.6 0.7 broadcast_compare_fusion
  16.3 0.1 select_reduce_fusion
  16.4 0.1 convert_reduce_fusion
  16.5 0.7 convert_select_fusion
  17.2 0.7 scatter.14.refs_2_
  17.8 0.7 reshape.196
  18.5 0.1 scatter.11.refs_1_
  18.6 1.1 fusion.1
  19.7 0.7 fusion.8.refs_3_
  20.4 1.7 %fusion = f32[64]{0:T(128)} fusion(bf16[2048,1]{0,1:T(2,128)(2,1)S(1)} %reshape.196, bf16[64,2048]{1,0:T(8,128)(2,1)} %hidden_ref.1, f32[2048]{0:T(1024)} %param.19, f32[64]{0:T(128)S(1)} %add_rsqrt_fusion, s32[64]{0:T(128)} %param.23), kind=kOutput, calls=%fused_computation.1 | convolution fusion | flops 786560 | bytes 275200 | tf_op jit(solution)/shard_map/dot_general | solution.py:252
  22.2 47.5 %all-gather.2.cloned.1.call-done.x_ref = bf16[1536,2176]{1,0:T(8,128)(2,1)} async-done(((bf16[48,2176]{1,0:T(8,128)(2,1)}), bf16[1536,2176]{1,0:T(8,128)(2,1)}) %all-gather.2.cloned.1.call-update) | async-done | bytes 6684688 | tf_op jit(solution)/shard_map/all_gather | solution.py:262
  69.7 19.0 %shard_map.117 = f32[8,1536]{1,0:T(8,128)} custom-call(bf16[1536,2176]{1,0:T(8,128)(2,1)} %all-gather.2.cloned.1.call-done.x_ref, bf16[1572,2048]{1,0:T(8,128)(2,1)} %bitcast.31), custom_call_target="tpu_custom_call" | custom-call | flops 9890168832 | bytes 13172736 | tf_op jit(solution)/shard_map/pallas_call | solution.py:222
  88.7 0.8 slice.75
  89.5 0.1 reshape.190
  89.6 0.7 copy.24
  90.3 22.9 %shard_map.118 = f32[8,128]{1,0:T(8,128)} custom-call(f32[32,4,48]{2,1,0:T(4,128)} %bitcast.26, f32[8,128]{1,0:T(8,128)} %copy-done, f32[8,128]{1,0:T(8,128)} %scatter.14.refs_2_, f32[64,48]{1,0:T(8,128)} %fusion.8.refs_3_), custom_call_target="tpu_custom_call" | custom-call | tf_op jit(solution)/shard_map/pallas_call | solution.py:138
  113.2 1.3 %slice_bitcast_fusion.1 = (f32[64]{0:T(128)}, f32[64]{0:T(128)}) fusion(f32[8,128]{1,0:T(8,128)} %shard_map.118), kind=kLoop, calls=%fused_computation.27 | loop fusion | bytes 1024 | tf_op jit(solution)/shard_map/squeeze | solution.py:283
  114.5 1.2 slice_bitcast_fusion
  (6 shorter events, 0.0 us)
Async XLA Ops:
  7.2 62.5 %all-gather.2.cloned.1.call-start = ((), (), s32[]{:S(2)}) async-start(), calls=%async_computation | async-start | bytes 6893568 | tf_op jit(solution)/shard_map/all_gather | solution.py:262
  18.6 70.1 %copy-start = (f32[8,128]{1,0:T(8,128)}, f32[8,128]{1,0:T(8,128)S(1)}, u32[]{:S(2)}) copy-start(f32[8,128]{1,0:T(8,128)S(1)} %scatter.11.refs_1_) | copy-start | bytes 12292
Sparse Core Ops, SparseCore 0:
  10.6 59.0 all-gather.1

commit v19 on v15

--- a/solution.py
+++ b/solution.py
@@ -193,22 +193,51 @@
     )(hidden, norm_gain.reshape(1, width), slot_mask.reshape(1, own_rows), token_ids.reshape(1, own_rows))
 
 
-def stats_kernel(x_ref, wt_ref, out_ref):
+def stats_kernel(x_ref, wt_ref, out_ref, logits_ref):
     vocab, depth = wt_ref.shape
+    tile = x_ref.shape[0]
     contract_last = (((1,), (1,)), ((), ()))
-    logits = lax.dot_general(wt_ref[...], x_ref[:, :depth], contract_last, preferred_element_type=jnp.float32)
+    logits_ref[...] = lax.dot_general(
+        wt_ref[...], x_ref[:, :depth], contract_last, preferred_element_type=jnp.float32
+    )
     pick = (
         lax.broadcasted_iota(jnp.int32, (8, 128), 0) == lax.broadcasted_iota(jnp.int32, (8, 128), 1)
     ).astype(jnp.bfloat16)
     meta = lax.dot_general(pick, x_ref[:, depth:depth + 128], contract_last, preferred_element_type=jnp.float32)
     token = (meta[0:1, :] * 256.0 + meta[1:2, :]).astype(jnp.int32) - lax.axis_index("tensor") * vocab
-    peak = jnp.max(logits, axis=0, keepdims=True)
-    shifted = logits - peak
-    weights = jnp.exp(shifted)
-    mass = jnp.sum(weights, axis=0, keepdims=True)
-    spread = jnp.sum(weights * shifted, axis=0, keepdims=True)
-    entry = lax.broadcasted_iota(jnp.int32, logits.shape, 0)
-    target = jnp.sum(jnp.where(entry == token, logits, 0.0), axis=0, keepdims=True)
+    chunks = vocab // 8
+    rest = vocab - chunks * 8
+
+    def top(c, m):
+        return jnp.maximum(m, logits_ref[pl.ds(pl.multiple_of(c * 8, 8), 8), :])
+
+    peak = jnp.max(lax.fori_loop(0, chunks, top, jnp.full((8, tile), -jnp.inf, jnp.float32)), axis=0, keepdims=True)
+    if rest:
+        peak = jnp.maximum(peak, jnp.max(logits_ref[chunks * 8:vocab, :], axis=0, keepdims=True))
+
+    def accumulate(block, first, sums):
+        mass, spread, target = sums
+        shifted = block - peak
+        weights = jnp.exp(shifted)
+        entry = first + lax.broadcasted_iota(jnp.int32, block.shape, 0)
+        return (
+            mass + jnp.sum(weights, axis=0, keepdims=True) if block.shape[0] != 8 else mass + weights,
+            spread + jnp.sum(weights * shifted, axis=0, keepdims=True) if block.shape[0] != 8 else spread + weights * shifted,
+            target + jnp.sum(jnp.where(entry == token, block, 0.0), axis=0, keepdims=True)
+            if block.shape[0] != 8 else target + jnp.where(entry == token, block, 0.0),
+        )
+
+    def body(c, sums):
+        start = pl.multiple_of(c * 8, 8)
+        return accumulate(logits_ref[pl.ds(start, 8), :], start, sums)
+
+    zero = jnp.zeros((8, tile), jnp.float32)
+    sums = lax.fori_loop(0, chunks, body, (zero, zero, zero))
+    mass, spread, target = (jnp.sum(value, axis=0, keepdims=True) for value in sums)
+    if rest:
+        one = jnp.zeros((1, tile), jnp.float32)
+        extra = accumulate(logits_ref[chunks * 8:vocab, :], chunks * 8, (one, one, one))
+        mass, spread, target = mass + extra[0], spread + extra[1], target + extra[2]
     row = lax.broadcasted_iota(jnp.int32, out_ref.shape, 0)
     out_ref[...] = jnp.where(
         row == 0, peak,
@@ -228,6 +257,7 @@
             pl.BlockSpec((vocab, depth), lambda i: (0, 0)),
         ],
         out_specs=pl.BlockSpec((8, tile), lambda i: (0, i)),
+        scratch_shapes=[pltpu.VMEM((vocab, tile), jnp.float32)],
         compiler_params=pltpu.CompilerParams(vmem_limit_bytes=56 * 1024 * 1024),
         cost_estimate=pl.CostEstimate(
             flops=2 * count * depth * vocab,

time: 123 us -> 142 us (1.15)
  Pallas kernels: 44 us -> 63.2 us
    pallas_call x1, Pallas kernels: 19 us -> 38.3 us  [row_stats(): pl.pallas_call(stats_kernel, out_shape=jax.ShapeDtypeStruct((8, count), j...]
  transfers between devices with their start and end apart: 1 -> 1, of which waited for: 1 -> 1; matrix products, arithmetic and copies ran while one was open for 11% -> 9% of each run, Pallas kernels for 0% -> 0%
where the time goes in v19:
time: 142 us
  Pallas kernels  63.2 us (45%)
  waiting for transfers between devices  47.5 us (33%)
  between operations  14.1 us (10%)
  other arithmetic  8.27 us (6%)
  local copies, waits for them, and re-layouts  6.88 us (5%)
  matrix products  1.73 us (1%)
    all_gather x1, waiting for transfers between devices, on_device(): gathered = lax.all_gather(block, 'tensor', axis=0, tiled=True)  47.5 us
    pallas_call x1, Pallas kernels, row_stats(): pl.pallas_call(stats_kernel, out_shape=jax.ShapeDtypeStruct((8, count), j...  38.3 us
    pallas_call x1, Pallas kernels, finish(): pl.pallas_call(lambda *refs: finish_kernel(n_tensor, n_dp, count, *refs),...  22.9 us
    another operation x7, other arithmetic  4.82 us
  transfers between devices with their start and end apart: 1, of which 1 were waited for; matrix products, arithmetic and copies ran while one was open for 9% of the time, Pallas kernels for 0%

profile of v19, /device:TPU:1, one launch (start us, length us, event | category | flops | bytes accessed | tf_op | source)
XLA Modules:
  0.0 141.8 jit_solution(3219121028984384765)
XLA Ops:
  7.2 0.0 all-gather.2.cloned.1.call-start
  7.2 2.0 %shard_map.116 = bf16[48,2176]{1,0:T(8,128)(2,1)} custom-call(bf16[64,2048]{1,0:T(8,128)(2,1)} %hidden_ref.1, f32[1,2048]{1,0:T(1,128)} %bitcast.27, s32[1,64]{1,0:T(1,128)} %bitcast.28, s32[1,64]{1,0:T(1,128)} %bitcast.30), custom_call_target="tpu_custom_call" | custom-call | tf_op jit(solution)/shard_map/pallas_call | solution.py:188
  9.2 0.7 copy.20
  10.0 0.1 reduce-window.13
  10.1 0.8 reduce-window.14
  10.9 0.5 slice.76
  11.4 0.7 convert_bitcast_fusion
  12.1 0.1 copy.21
  12.2 0.6 compare_reduce_fusion
  12.8 1.3 fusion.11
  14.1 0.1 copy.22
  14.2 0.6 compare_reduce_fusion.1
  14.8 0.6 iota_compare_fusion.3
  15.5 0.1 add_reduce_fusion
  15.6 0.7 broadcast_compare_fusion
  16.3 0.1 select_reduce_fusion
  16.4 0.1 convert_reduce_fusion
  16.5 0.7 convert_select_fusion
  17.2 0.7 scatter.14.refs_2_
  17.8 0.7 reshape.196
  18.5 0.1 scatter.11.refs_1_
  18.6 1.1 fusion.1
  19.7 0.7 fusion.8.refs_3_
  20.4 1.7 %fusion = f32[64]{0:T(128)} fusion(bf16[2048,1]{0,1:T(2,128)(2,1)S(1)} %reshape.196, bf16[64,2048]{1,0:T(8,128)(2,1)} %hidden_ref.1, f32[2048]{0:T(1024)} %param.19, f32[64]{0:T(128)S(1)} %add_rsqrt_fusion, s32[64]{0:T(128)} %param.23), kind=kOutput, calls=%fused_computation.1 | convolution fusion | flops 786560 | bytes 275200 | tf_op jit(solution)/shard_map/dot_general | solution.py:282
  22.2 47.5 %all-gather.2.cloned.1.call-done.x_ref = bf16[1536,2176]{1,0:T(8,128)(2,1)} async-done(((bf16[48,2176]{1,0:T(8,128)(2,1)}), bf16[1536,2176]{1,0:T(8,128)(2,1)}) %all-gather.2.cloned.1.call-update) | async-done | bytes 6684688 | tf_op jit(solution)/shard_map/all_gather | solution.py:292
  69.7 38.3 %shard_map.117 = f32[8,1536]{1,0:T(8,128)} custom-call(bf16[1536,2176]{1,0:T(8,128)(2,1)} %all-gather.2.cloned.1.call-done.x_ref, bf16[1572,2048]{1,0:T(8,128)(2,1)} %bitcast.31), custom_call_target="tpu_custom_call" | custom-call | flops 9890168832 | bytes 13172736 | tf_op jit(solution)/shard_map/pallas_call | solution.py:251
  107.9 0.8 slice.75
  108.7 0.1 reshape.190
  108.8 0.7 copy.24
  109.5 22.9 %shard_map.118 = f32[8,128]{1,0:T(8,128)} custom-call(f32[32,4,48]{2,1,0:T(4,128)} %bitcast.26, f32[8,128]{1,0:T(8,128)} %copy-done, f32[8,128]{1,0:T(8,128)} %scatter.14.refs_2_, f32[64,48]{1,0:T(8,128)} %fusion.8.refs_3_), custom_call_target="tpu_custom_call" | custom-call | tf_op jit(solution)/shard_map/pallas_call | solution.py:138
  132.5 1.3 slice_bitcast_fusion.1
  133.7 1.2 slice_bitcast_fusion
  (6 shorter events, 0.0 us)
Async XLA Ops:
  7.2 62.5 %all-gather.2.cloned.1.call-start = ((), (), s32[]{:S(2)}) async-start(), calls=%async_computation | async-start | bytes 6893568 | tf_op jit(solution)/shard_map/all_gather | solution.py:292
  18.6 89.3 %copy-start = (f32[8,128]{1,0:T(8,128)}, f32[8,128]{1,0:T(8,128)S(1)}, u32[]{:S(2)}) copy-start(f32[8,128]{1,0:T(8,128)S(1)} %scatter.11.refs_1_) | copy-start | bytes 12292
Sparse Core Ops, SparseCore 0:
  10.6 59.0 all-gather.1

commit v20 on v19

--- a/solution.py
+++ b/solution.py
@@ -211,7 +211,9 @@
     def top(c, m):
         return jnp.maximum(m, logits_ref[pl.ds(pl.multiple_of(c * 8, 8), 8), :])
 
-    peak = jnp.max(lax.fori_loop(0, chunks, top, jnp.full((8, tile), -jnp.inf, jnp.float32)), axis=0, keepdims=True)
+    peak = jnp.max(
+        lax.fori_loop(0, chunks, top, jnp.full((8, tile), -jnp.inf, jnp.float32), unroll=7), axis=0, keepdims=True
+    )
     if rest:
         peak = jnp.maximum(peak, jnp.max(logits_ref[chunks * 8:vocab, :], axis=0, keepdims=True))
 
@@ -232,7 +234,7 @@
         return accumulate(logits_ref[pl.ds(start, 8), :], start, sums)
 
     zero = jnp.zeros((8, tile), jnp.float32)
-    sums = lax.fori_loop(0, chunks, body, (zero, zero, zero))
+    sums = lax.fori_loop(0, chunks, body, (zero, zero, zero), unroll=7)
     mass, spread, target = (jnp.sum(value, axis=0, keepdims=True) for value in sums)
     if rest:
         one = jnp.zeros((1, tile), jnp.float32)

time: 142 us -> 126 us (0.89)
  Pallas kernels: 63.2 us -> 46.6 us
    pallas_call x1, Pallas kernels: 38.3 us -> 21.6 us  [row_stats(): pl.pallas_call(stats_kernel, out_shape=jax.ShapeDtypeStruct((8, count), j...]
  transfers between devices with their start and end apart: 1 -> 1, of which waited for: 1 -> 1; matrix products, arithmetic and copies ran while one was open for 9% -> 10% of each run, Pallas kernels for 0% -> 0%
where the time goes in v20:
time: 126 us; the launch traced here: 125 us
  waiting for transfers between devices  47.5 us (38%)
  Pallas kernels  46.6 us (37%)
  between operations  14.1 us (11%)
  other arithmetic  8.27 us (7%)
  local copies, waits for them, and re-layouts  6.88 us (5%)
  matrix products  1.73 us (1%)
    all_gather x1, waiting for transfers between devices, on_device(): gathered = lax.all_gather(block, 'tensor', axis=0, tiled=True)  47.5 us
    pallas_call x1, Pallas kernels, finish(): pl.pallas_call(lambda *refs: finish_kernel(n_tensor, n_dp, count, *refs),...  22.9 us
    pallas_call x1, Pallas kernels, row_stats(): pl.pallas_call(stats_kernel, out_shape=jax.ShapeDtypeStruct((8, count), j...  21.6 us
    another operation x7, other arithmetic  4.82 us
  transfers between devices with their start and end apart: 1, of which 1 were waited for; matrix products, arithmetic and copies ran while one was open for 10% of the time, Pallas kernels for 0%

profile of v20, /device:TPU:1, one launch (start us, length us, event | category | flops | bytes accessed | tf_op | source)
XLA Modules:
  0.0 125.1 jit_solution(14691392745033882048)
XLA Ops:
  7.2 0.0 all-gather.2.cloned.1.call-start
  7.2 2.0 %shard_map.116 = bf16[48,2176]{1,0:T(8,128)(2,1)} custom-call(bf16[64,2048]{1,0:T(8,128)(2,1)} %hidden_ref.1, f32[1,2048]{1,0:T(1,128)} %bitcast.27, s32[1,64]{1,0:T(1,128)} %bitcast.28, s32[1,64]{1,0:T(1,128)} %bitcast.30), custom_call_target="tpu_custom_call" | custom-call | tf_op jit(solution)/shard_map/pallas_call | solution.py:188
  9.2 0.7 copy.20
  10.0 0.1 reduce-window.13
  10.1 0.8 reduce-window.14
  10.9 0.5 slice.76
  11.4 0.7 convert_bitcast_fusion
  12.1 0.1 copy.21
  12.2 0.6 compare_reduce_fusion
  12.8 1.3 %fusion.11 = f32[8,1]{0,1:T(1,128)S(1)} fusion(pred[]{:T(512)} %compare_reduce_fusion, s32[8]{0:T(128)} %param.25), kind=kLoop, calls=%fused_computation.24 | loop fusion | flops 16 | bytes 65 | tf_op jit(solution)/shard_map/reshape.134
  14.1 0.1 copy.22
  14.2 0.6 compare_reduce_fusion.1
  14.8 0.6 iota_compare_fusion.3
  15.5 0.1 add_reduce_fusion
  15.6 0.7 broadcast_compare_fusion
  16.3 0.1 select_reduce_fusion
  16.4 0.1 convert_reduce_fusion
  16.5 0.7 convert_select_fusion
  17.2 0.7 scatter.14.refs_2_
  17.8 0.7 reshape.196
  18.5 0.1 scatter.11.refs_1_
  18.6 1.1 fusion.1
  19.7 0.7 fusion.8.refs_3_
  20.4 1.7 %fusion = f32[64]{0:T(128)} fusion(bf16[2048,1]{0,1:T(2,128)(2,1)S(1)} %reshape.196, bf16[64,2048]{1,0:T(8,128)(2,1)} %hidden_ref.1, f32[2048]{0:T(1024)} %param.19, f32[64]{0:T(128)S(1)} %add_rsqrt_fusion, s32[64]{0:T(128)} %param.23), kind=kOutput, calls=%fused_computation.1 | convolution fusion | flops 786560 | bytes 275200 | tf_op jit(solution)/shard_map/dot_general | solution.py:284
  22.2 47.5 %all-gather.2.cloned.1.call-done.x_ref = bf16[1536,2176]{1,0:T(8,128)(2,1)} async-done(((bf16[48,2176]{1,0:T(8,128)(2,1)}), bf16[1536,2176]{1,0:T(8,128)(2,1)}) %all-gather.2.cloned.1.call-update) | async-done | bytes 6684688 | tf_op jit(solution)/shard_map/all_gather | solution.py:294
  69.7 21.6 %shard_map.117 = f32[8,1536]{1,0:T(8,128)} custom-call(bf16[1536,2176]{1,0:T(8,128)(2,1)} %all-gather.2.cloned.1.call-done.x_ref, bf16[1572,2048]{1,0:T(8,128)(2,1)} %bitcast.31), custom_call_target="tpu_custom_call" | custom-call | flops 9890168832 | bytes 13172736 | tf_op jit(solution)/shard_map/pallas_call | solution.py:253
  91.3 0.8 slice.75
  92.1 0.1 reshape.190
  92.2 0.7 copy.24
  92.9 22.9 %shard_map.118 = f32[8,128]{1,0:T(8,128)} custom-call(f32[32,4,48]{2,1,0:T(4,128)} %bitcast.26, f32[8,128]{1,0:T(8,128)} %copy-done, f32[8,128]{1,0:T(8,128)} %scatter.14.refs_2_, f32[64,48]{1,0:T(8,128)} %fusion.8.refs_3_), custom_call_target="tpu_custom_call" | custom-call | tf_op jit(solution)/shard_map/pallas_call | solution.py:138
  115.8 1.3 %slice_bitcast_fusion.1 = (f32[64]{0:T(128)}, f32[64]{0:T(128)}) fusion(f32[8,128]{1,0:T(8,128)} %shard_map.118), kind=kLoop, calls=%fused_computation.27 | loop fusion | bytes 1024 | tf_op jit(solution)/shard_map/squeeze | solution.py:315
  117.1 1.2 slice_bitcast_fusion
  (6 shorter events, 0.0 us)
Async XLA Ops:
  7.2 62.5 %all-gather.2.cloned.1.call-start = ((), (), s32[]{:S(2)}) async-start(), calls=%async_computation | async-start | bytes 6893568 | tf_op jit(solution)/shard_map/all_gather | solution.py:294
  18.6 72.7 %copy-start = (f32[8,128]{1,0:T(8,128)}, f32[8,128]{1,0:T(8,128)S(1)}, u32[]{:S(2)}) copy-start(f32[8,128]{1,0:T(8,128)S(1)} %scatter.11.refs_1_) | copy-start | bytes 12292
Sparse Core Ops, SparseCore 0:
  10.6 59.0 all-gather.1

commit v21 on v20

--- a/solution.py
+++ b/solution.py
@@ -212,7 +212,7 @@
         return jnp.maximum(m, logits_ref[pl.ds(pl.multiple_of(c * 8, 8), 8), :])
 
     peak = jnp.max(
-        lax.fori_loop(0, chunks, top, jnp.full((8, tile), -jnp.inf, jnp.float32), unroll=7), axis=0, keepdims=True
+        lax.fori_loop(0, chunks, top, jnp.full((8, tile), -jnp.inf, jnp.float32), unroll=28), axis=0, keepdims=True
     )
     if rest:
         peak = jnp.maximum(peak, jnp.max(logits_ref[chunks * 8:vocab, :], axis=0, keepdims=True))
@@ -234,7 +234,7 @@
         return accumulate(logits_ref[pl.ds(start, 8), :], start, sums)
 
     zero = jnp.zeros((8, tile), jnp.float32)
-    sums = lax.fori_loop(0, chunks, body, (zero, zero, zero), unroll=7)
+    sums = lax.fori_loop(0, chunks, body, (zero, zero, zero), unroll=28)
     mass, spread, target = (jnp.sum(value, axis=0, keepdims=True) for value in sums)
     if rest:
         one = jnp.zeros((1, tile), jnp.float32)

time: 126 us -> 124 us (0.984)
  Pallas kernels: 46.6 us -> 45.2 us
    pallas_call x1, Pallas kernels: 21.6 us -> 20.2 us  [row_stats(): pl.pallas_call(stats_kernel, out_shape=jax.ShapeDtypeStruct((8, count), j...]
where the time goes in v21:
time: 124 us
  waiting for transfers between devices  47.5 us (38%)
  Pallas kernels  45.2 us (36%)
  between operations  14.1 us (11%)
  other arithmetic  8.27 us (7%)
  local copies, waits for them, and re-layouts  6.88 us (6%)
  matrix products  1.73 us (1%)
    all_gather x1, waiting for transfers between devices, on_device(): gathered = lax.all_gather(block, 'tensor', axis=0, tiled=True)  47.5 us
    pallas_call x1, Pallas kernels, finish(): pl.pallas_call(lambda *refs: finish_kernel(n_tensor, n_dp, count, *refs),...  22.9 us
    pallas_call x1, Pallas kernels, row_stats(): pl.pallas_call(stats_kernel, out_shape=jax.ShapeDtypeStruct((8, count), j...  20.2 us
    another operation x7, other arithmetic  4.82 us
  transfers between devices with their start and end apart: 1, of which 1 were waited for; matrix products, arithmetic and copies ran while one was open for 10% of the time, Pallas kernels for 0%

profile of v21, /device:TPU:1, one launch (start us, length us, event | category | flops | bytes accessed | tf_op | source)
XLA Modules:
  0.0 123.8 jit_solution(11203030938957293543)
XLA Ops:
  7.2 0.0 all-gather.2.cloned.1.call-start
  7.2 2.0 %shard_map.116 = bf16[48,2176]{1,0:T(8,128)(2,1)} custom-call(bf16[64,2048]{1,0:T(8,128)(2,1)} %hidden_ref.1, f32[1,2048]{1,0:T(1,128)} %bitcast.27, s32[1,64]{1,0:T(1,128)} %bitcast.28, s32[1,64]{1,0:T(1,128)} %bitcast.30), custom_call_target="tpu_custom_call" | custom-call | tf_op jit(solution)/shard_map/pallas_call | solution.py:188
  9.2 0.7 copy.20
  10.0 0.1 reduce-window.13
  10.1 0.8 reduce-window.14
  10.9 0.5 slice.76
  11.4 0.7 convert_bitcast_fusion
  12.1 0.1 copy.21
  12.2 0.6 compare_reduce_fusion
  12.8 1.3 %fusion.11 = f32[8,1]{0,1:T(1,128)S(1)} fusion(pred[]{:T(512)} %compare_reduce_fusion, s32[8]{0:T(128)} %param.25), kind=kLoop, calls=%fused_computation.24 | loop fusion | flops 16 | bytes 65 | tf_op jit(solution)/shard_map/reshape.134
  14.1 0.1 copy.22
  14.2 0.6 compare_reduce_fusion.1
  14.8 0.6 iota_compare_fusion.3
  15.5 0.1 add_reduce_fusion
  15.6 0.7 broadcast_compare_fusion
  16.3 0.1 select_reduce_fusion
  16.4 0.1 convert_reduce_fusion
  16.5 0.7 convert_select_fusion
  17.2 0.7 scatter.14.refs_2_
  17.8 0.7 reshape.196
  18.5 0.1 scatter.11.refs_1_
  18.6 1.1 fusion.1
  19.7 0.7 fusion.8.refs_3_
  20.4 1.7 %fusion = f32[64]{0:T(128)} fusion(bf16[2048,1]{0,1:T(2,128)(2,1)S(1)} %reshape.196, bf16[64,2048]{1,0:T(8,128)(2,1)} %hidden_ref.1, f32[2048]{0:T(1024)} %param.19, f32[64]{0:T(128)S(1)} %add_rsqrt_fusion, s32[64]{0:T(128)} %param.23), kind=kOutput, calls=%fused_computation.1 | convolution fusion | flops 786560 | bytes 275200 | tf_op jit(solution)/shard_map/dot_general | solution.py:284
  22.2 47.5 %all-gather.2.cloned.1.call-done.x_ref = bf16[1536,2176]{1,0:T(8,128)(2,1)} async-done(((bf16[48,2176]{1,0:T(8,128)(2,1)}), bf16[1536,2176]{1,0:T(8,128)(2,1)}) %all-gather.2.cloned.1.call-update) | async-done | bytes 6684688 | tf_op jit(solution)/shard_map/all_gather | solution.py:294
  69.7 20.2 %shard_map.117 = f32[8,1536]{1,0:T(8,128)} custom-call(bf16[1536,2176]{1,0:T(8,128)(2,1)} %all-gather.2.cloned.1.call-done.x_ref, bf16[1572,2048]{1,0:T(8,128)(2,1)} %bitcast.31), custom_call_target="tpu_custom_call" | custom-call | flops 9890168832 | bytes 13172736 | tf_op jit(solution)/shard_map/pallas_call | solution.py:253
  89.9 0.8 slice.75
  90.7 0.1 reshape.190
  90.8 0.7 copy.24
  91.5 22.9 %shard_map.118 = f32[8,128]{1,0:T(8,128)} custom-call(f32[32,4,48]{2,1,0:T(4,128)} %bitcast.26, f32[8,128]{1,0:T(8,128)} %copy-done, f32[8,128]{1,0:T(8,128)} %scatter.14.refs_2_, f32[64,48]{1,0:T(8,128)} %fusion.8.refs_3_), custom_call_target="tpu_custom_call" | custom-call | tf_op jit(solution)/shard_map/pallas_call | solution.py:138
  114.5 1.3 %slice_bitcast_fusion.1 = (f32[64]{0:T(128)}, f32[64]{0:T(128)}) fusion(f32[8,128]{1,0:T(8,128)} %shard_map.118), kind=kLoop, calls=%fused_computation.27 | loop fusion | bytes 1024 | tf_op jit(solution)/shard_map/squeeze | solution.py:315
  115.7 1.2 slice_bitcast_fusion
  (6 shorter events, 0.0 us)
Async XLA Ops:
  7.2 62.5 %all-gather.2.cloned.1.call-start = ((), (), s32[]{:S(2)}) async-start(), calls=%async_computation | async-start | bytes 6893568 | tf_op jit(solution)/shard_map/all_gather | solution.py:294
  18.6 71.3 %copy-start = (f32[8,128]{1,0:T(8,128)}, f32[8,128]{1,0:T(8,128)S(1)}, u32[]{:S(2)}) copy-start(f32[8,128]{1,0:T(8,128)S(1)} %scatter.11.refs_1_) | copy-start | bytes 12292
Sparse Core Ops, SparseCore 0:
  10.6 59.0 all-gather.1
